TPU v7x, 128 devices: a whole 4x4x4 slice. The times are simulated.
128 devices in a mesh: img: 2 (over core), band: 64 (over z, y, x).
Axes of the slice: x: 4, y: 4, z: 4, core: 2. Of those that a mesh axis runs over, the one named last changes fastest.
Arguments:
- latent: bfloat16 [8, 256, 32, 1280], P('img', 'band'), parts along dimension 0, may hold values from -80 to 80
- stale_act: bfloat16 [8, 256, 32, 1280], P('img', 'band'), parts along dimension 0, may hold values from -4 to 4
- stale_kv: bfloat16 [2, 8, 256, 32, 640], P(None, 'img', 'band'), parts along dimension 1, may hold values from -600 to 600
- timestep: int32 [8, 8], P('img'), parts along dimension 0, may hold values from 0 to 999
- norm_gain: float32 [1280], replicated, may hold values from 0.1 to 1.9
- norm_shift: float32 [1280], replicated, may hold values from -1 to 1
- conv_weight: bfloat16 [3, 3, 1280, 640], replicated, may hold values from -0.0546875 to 0.0546875
- time_weight: bfloat16 [1280, 640], replicated, may hold values from -0.15625 to 0.15625
- attn_in: bfloat16 [1280, 1920], replicated, may hold values from -0.15625 to 0.15625
- attn_out: bfloat16 [640, 1280], replicated, may hold values from -0.25 to 0.25
Outputs:
- block_out: bfloat16 [8, 256, 32, 1280], P('img', 'band'), parts along dimension 0
- fresh_kv: bfloat16 [2, 8, 256, 32, 640], P(None, 'img', 'band'), parts along dimension 1
There are 2 independent parts, one for each index of `img`. A program takes and returns all parts, laid end to end along the dimension named above; an argument that names none is the same for every part. Nothing has to cross between parts.
All inputs are finite; a program needn't handle non-finite values.
Results may differ from a plain program's by a relative error of at most 0.0055.
Values may be sent and summed in bfloat16 or wider, within the bound.
No kernel may reach another device: no remote copies, remote signals or barrier semaphores. Data moves between devices by JAX's collectives and lax.ppermute only.
A program may use at most 192 MiB of HBM per device.

v0:
```python
import math

import jax
import jax.numpy as jnp
from jax import lax
from jax.sharding import PartitionSpec as P

IMG_ROWS = 32
GROUPS = 32
HEADS = 10
TDIM = 1280


def shifted(value, axis, by):
    count = lax.axis_size(axis)
    pairs = [(i, i + by) for i in range(count) if 0 <= i + by < count]
    return lax.ppermute(value, axis, pairs)


def time_term(timestep, time_weight):
    half_dim = TDIM // 2
    frequency = jnp.exp(-math.log(10000.0) * jnp.arange(half_dim, dtype=jnp.float32) / half_dim)
    angles = timestep.astype(jnp.float32)[:, None] * frequency[None, :]
    embedding = jnp.concatenate([jnp.cos(angles), jnp.sin(angles)], axis=1)
    return jnp.dot(
        jax.nn.silu(embedding), time_weight.astype(jnp.float32), precision=lax.Precision.HIGHEST
    )


def attend_block(queries, keys, values, scale_factor):
    scores = (
        jnp.einsum("bqhd,bkhd->bhqk", queries, keys, preferred_element_type=jnp.float32)
        * scale_factor
    )
    peak = jnp.max(scores, axis=-1)
    exponent = jnp.exp(scores - peak[..., None])
    context = jnp.einsum(
        "bhqk,bkhd->bhqd", exponent.astype(jnp.bfloat16), values, preferred_element_type=jnp.float32
    )
    return (peak, jnp.sum(exponent, axis=-1), context)


def on_device(
    latent,
    stale_act,
    stale_kv,
    timestep,
    norm_gain,
    norm_shift,
    conv_weight,
    time_weight,
    attn_in,
    attn_out,
):
    images, height, columns, channels = latent.shape
    conv_width = conv_weight.shape[3]
    inner_width = attn_out.shape[0]
    head_count = HEADS
    head_size = inner_width // head_count
    per_group = channels // GROUPS
    group_size = IMG_ROWS // height
    band_count = lax.axis_size("band")
    stacked = band_count * height // IMG_ROWS
    band_index = lax.axis_index("band")
    slot = band_index % stacked
    place = band_index // stacked
    slot_mask = (jnp.arange(stacked) == slot).astype(jnp.float32)[:, None, None]
    counted = float(IMG_ROWS * columns * per_group)
    floats = latent.astype(jnp.float32)
    grouped = floats.reshape(images, height * columns, GROUPS, per_group)
    totals = lax.psum(slot_mask * jnp.sum(grouped, axis=(1, 3))[None], "band")
    center = jnp.sum(totals * slot_mask, axis=0) / counted
    deviation = grouped - center[:, None, :, None]
    spreads = lax.psum(slot_mask * jnp.sum(deviation * deviation, axis=(1, 3))[None], "band")
    spread = jnp.sum(spreads * slot_mask, axis=0) / counted
    normed = (
        (grouped - center[:, None, :, None]) / jnp.sqrt(spread + 1e-05)[:, None, :, None]
    ).reshape(latent.shape)
    activated = jax.nn.silu(normed * norm_gain + norm_shift).astype(jnp.bfloat16)
    top_rim = shifted(stale_act[:, height - 1 :], "band", stacked)
    bottom_rim = shifted(stale_act[:, :1], "band", -stacked)
    top_rim = jnp.where(place == 0, jnp.zeros_like(top_rim), top_rim)
    bottom_rim = jnp.where(place == group_size - 1, jnp.zeros_like(bottom_rim), bottom_rim)
    extended = jnp.concatenate([top_rim, activated, bottom_rim], axis=1)
    padded = jnp.pad(extended, ((0, 0), (0, 0), (1, 1), (0, 0)))
    convolved = jnp.zeros((images, height, columns, conv_width), jnp.float32)
    for row_tap in range(3):
        for col_tap in range(3):
            convolved = convolved + jnp.einsum(
                "bhwc,cd->bhwd",
                padded[:, row_tap : row_tap + height, col_tap : col_tap + columns],
                conv_weight[row_tap, col_tap],
                preferred_element_type=jnp.float32,
            )
    own_steps = lax.dynamic_index_in_dim(timestep, slot, 1, keepdims=False)
    time_bias = time_term(own_steps, time_weight)
    window = (floats[..., :conv_width] + convolved + time_bias[:, None, None, :]).astype(
        jnp.bfloat16
    )
    hidden = jnp.concatenate([window, latent[..., conv_width:]], axis=-1)
    widened = hidden.astype(jnp.float32)
    token_mean = jnp.mean(widened, axis=-1, keepdims=True)
    token_var = jnp.mean((widened - token_mean) ** 2, axis=-1, keepdims=True)
    normalized = ((widened - token_mean) / jnp.sqrt(token_var + 1e-05)).astype(jnp.bfloat16)
    projected = jnp.dot(
        normalized.reshape(-1, channels), attn_in, preferred_element_type=jnp.float32
    )
    projected = projected.astype(jnp.bfloat16).reshape(images, height, columns, 3 * inner_width)
    fresh_kv = jnp.stack(
        [projected[..., inner_width : 2 * inner_width], projected[..., 2 * inner_width :]]
    )
    tokens_dev = height * columns
    query_heads = projected[..., :inner_width].reshape(images, tokens_dev, head_count, head_size)
    fresh_keys = fresh_kv[0].reshape(images, tokens_dev, head_count, head_size)
    fresh_values = fresh_kv[1].reshape(images, tokens_dev, head_count, head_size)
    scale_factor = head_size ** (-0.5)
    start_carry = attend_block(query_heads, fresh_keys, fresh_values, scale_factor)

    def absorb(carry, piece):
        running_max, running_sum, context = carry
        piece_rows = piece.shape[2]
        piece_keys = piece[0].reshape(images, piece_rows * columns, head_count, head_size)
        piece_values = piece[1].reshape(images, piece_rows * columns, head_count, head_size)
        peak, total, partial_ctx = attend_block(query_heads, piece_keys, piece_values, scale_factor)
        new_max = jnp.maximum(running_max, peak)
        old_factor = jnp.exp(running_max - new_max)
        new_factor = jnp.exp(peak - new_max)
        return (
            new_max,
            running_sum * old_factor + total * new_factor,
            context * old_factor[..., None] + partial_ctx * new_factor[..., None],
        )

    def chain_step(step, state):
        upward, downward, carry = state
        upward = shifted(upward, "band", stacked)
        downward = shifted(downward, "band", -stacked)
        carry = lax.cond(place >= step, lambda held: absorb(held, upward), lambda held: held, carry)
        carry = lax.cond(
            place + step < group_size, lambda held: absorb(held, downward), lambda held: held, carry
        )
        return (upward, downward, carry)

    final_state = lax.fori_loop(1, group_size, chain_step, (stale_kv, stale_kv, start_carry))
    running_max, running_sum, context = final_state[2]
    attended = jnp.transpose(context / running_sum[..., None], (0, 2, 1, 3)).astype(jnp.bfloat16)
    update = jnp.dot(
        attended.reshape(-1, inner_width), attn_out, preferred_element_type=jnp.float32
    )
    block_out = (widened + update.reshape(images, height, columns, channels)).astype(jnp.bfloat16)
    return (block_out, fresh_kv)


def solution(mesh):
    return jax.shard_map(
        on_device,
        mesh=mesh,
        in_specs=(
            P("img", "band", None, None),
            P("img", "band", None, None),
            P(None, "img", "band", None, None),
            P("img", None),
            P(),
            P(),
            P(),
            P(),
            P(),
            P(),
        ),
        out_specs=(P("img", "band", None, None), P(None, "img", "band", None, None)),
        check_vma=False,
    )
```

profile of v0, /device:TPU:0, one launch (start us, length us, event | category | flops | bytes accessed | tf_op | source)
XLA Modules:
  0.0 1268.4 jit_solution(8291177125210356071)
XLA Ops:
  0.7 2.7 copy.108
  4.1 5.9 collective-permute-start.2
  14.5 351.0 %psum.14 = f32[8,4,32]{2,0,1:T(8,128)S(1)} all-reduce(f32[8,4,32]{2,0,1:T(8,128)S(1)} %broadcast_multiply_fusion.1), channel_id=1, replica_groups=mesh['img'=2,'band'=64] {'band'}, use_global_device_ids=true, to_apply=%region_2.3 | all-reduce | flops 1024 | bytes 8192 | tf_op jit(solution)/shard_map/psum | solution.py:71
  366.5 341.7 %psum.15 = f32[8,4,32]{2,0,1:T(8,128)S(1)} all-reduce(f32[8,4,32]{2,0,1:T(8,128)S(1)} %broadcast_multiply_fusion), channel_id=1, replica_groups=mesh['img'=2,'band'=64] {'band'}, use_global_device_ids=true, to_apply=%region_6.7 | all-reduce | flops 1024 | bytes 8192 | tf_op jit(solution)/shard_map/psum | solution.py:74
  708.5 2.5 copy.90
  713.2 2.8 fusion.47
  718.9 2.6 fusion.49
  731.6 5.4 convolution_convert_fusion
  743.0 3.8 reshape_squeeze_stack.6
  753.3 502.6 %while.21 = (s32[]{:T(128)}, bf16[2,4,4,32,640]{4,3,2,1,0:T(8,128)(2,1)}, bf16[2,4,4,32,640]{4,3,2,1,0:T(8,128)(2,1)}, f32[4,10,128]{2,1,0:T(8,128)S(1)}, f32[4,...) while((s32[]{:T(128)}, ...), condition=%wide.region_21.22_spmd, body=%wide.region_12.21_spmd.sunk | while | flops 348037120 | bytes 72663480 | solution.py:144
  757.0 26.2 %collective-permute-done = bf16[2,4,4,32,640]{4,3,2,1,0:T(8,128)(2,1)} collective-permute-done((bf16[2,4,4,32,640]{4,3,2,1,0:T(8,128)(2,1)}, bf16[2,4,4,32,640]{4,3,2,1,0:T(8,128)(2,1)}, u32[]{:S(2)}, u32[]{:S(2)}) %collective-permute-start) | collective-permute-done | bytes 1310752 | tf_op jit(solution)/shard_map/while/body/eval_jaxpr/ppermute | solution.py:17
  783.2 5.8 collective-permute-done.1
  789.0 17.1 %conditional.5 = ((f32[4,10,128]{2,1,0:T(8,128)S(1)}, f32[4,10,128]{2,1,0:T(8,128)S(1)}, f32[4,10,128,64]{2,3,1,0:T(8,128)S(1)})) conditional(s32[]{:T(128)} %convert_element_type.114, (f32[4,10,128]{2,1,0:T(8,128)S(1)}, f32[4,10,128]{2,1,0:T(8,128)S(1)}, f32[4,10,128,64]{2,3,1,0:T(8,128)S(1)}) %get-tuple-element.368, ...), branch_computations={%region_17.17_spmd, %region_18.20_spmd} | conditional | flops 174018560 | bytes 28467260 | solution.py:139
  791.5 3.5 squeeze.30
  799.4 3.5 squeeze.31
  802.9 3.2 fusion.12
  806.1 2.5 copy.101
  811.1 18.4 %collective-permute-start = (bf16[2,4,4,32,640]{4,3,2,1,0:T(8,128)(2,1)}, bf16[2,4,4,32,640]{4,3,2,1,0:T(8,128)(2,1)}, u32[]{:S(2)}, u32[]{:S(2)}) collective-permute-start(bf16[2,4,4,32,640]{4,3,2,1,0:T(8,128)(2,1)} %get-tuple-element.349), channel_id=1, source_target_pairs={{0,8},{1,9},{2,10},{3,11},{4,12},{5,13},{6,14},{7,15},{8,16},{9,17... | collective-permute-start | bytes 3932168 | tf_op jit(solution)/shard_map/while/body/eval_jaxpr/ppermute | solution.py:17
  830.8 26.5 %collective-permute-done = bf16[2,4,4,32,640]{4,3,2,1,0:T(8,128)(2,1)} collective-permute-done((bf16[2,4,4,32,640]{4,3,2,1,0:T(8,128)(2,1)}, bf16[2,4,4,32,640]{4,3,2,1,0:T(8,128)(2,1)}, u32[]{:S(2)}, u32[]{:S(2)}) %collective-permute-start) | collective-permute-done | bytes 1310752 | tf_op jit(solution)/shard_map/while/body/eval_jaxpr/ppermute | solution.py:17
  857.3 28.8 %collective-permute-done.1 = bf16[2,4,4,32,640]{4,3,2,1,0:T(8,128)(2,1)} collective-permute-done((bf16[2,4,4,32,640]{4,3,2,1,0:T(8,128)(2,1)}, bf16[2,4,4,32,640]{4,3,2,1,0:T(8,128)(2,1)}, u32[]{:S(2)}, u32[]{:S(2)}) %collective-permute-start.1) | collective-permute-done | bytes 1310752 | tf_op jit(solution)/shard_map/while/body/eval_jaxpr/ppermute | solution.py:17
  886.2 17.1 %conditional.5 = ((f32[4,10,128]{2,1,0:T(8,128)S(1)}, f32[4,10,128]{2,1,0:T(8,128)S(1)}, f32[4,10,128,64]{2,3,1,0:T(8,128)S(1)})) conditional(s32[]{:T(128)} %convert_element_type.114, (f32[4,10,128]{2,1,0:T(8,128)S(1)}, f32[4,10,128]{2,1,0:T(8,128)S(1)}, f32[4,10,128,64]{2,3,1,0:T(8,128)S(1)}) %get-tuple-element.368, ...), branch_computations={%region_17.17_spmd, %region_18.20_spmd} | conditional | flops 174018560 | bytes 28467260 | solution.py:139
  888.6 3.5 squeeze.30
  896.5 3.5 squeeze.31
  900.1 3.2 fusion.12
  903.3 2.5 copy.101
  908.3 2.5 collective-permute-start
  912.1 26.1 %collective-permute-done = bf16[2,4,4,32,640]{4,3,2,1,0:T(8,128)(2,1)} collective-permute-done((bf16[2,4,4,32,640]{4,3,2,1,0:T(8,128)(2,1)}, bf16[2,4,4,32,640]{4,3,2,1,0:T(8,128)(2,1)}, u32[]{:S(2)}, u32[]{:S(2)}) %collective-permute-start) | collective-permute-done | bytes 1310752 | tf_op jit(solution)/shard_map/while/body/eval_jaxpr/ppermute | solution.py:17
  938.2 28.7 %collective-permute-done.1 = bf16[2,4,4,32,640]{4,3,2,1,0:T(8,128)(2,1)} collective-permute-done((bf16[2,4,4,32,640]{4,3,2,1,0:T(8,128)(2,1)}, bf16[2,4,4,32,640]{4,3,2,1,0:T(8,128)(2,1)}, u32[]{:S(2)}, u32[]{:S(2)}) %collective-permute-start.1) | collective-permute-done | bytes 1310752 | tf_op jit(solution)/shard_map/while/body/eval_jaxpr/ppermute | solution.py:17
  966.9 17.1 %conditional.5 = ((f32[4,10,128]{2,1,0:T(8,128)S(1)}, f32[4,10,128]{2,1,0:T(8,128)S(1)}, f32[4,10,128,64]{2,3,1,0:T(8,128)S(1)})) conditional(s32[]{:T(128)} %convert_element_type.114, (f32[4,10,128]{2,1,0:T(8,128)S(1)}, f32[4,10,128]{2,1,0:T(8,128)S(1)}, f32[4,10,128,64]{2,3,1,0:T(8,128)S(1)}) %get-tuple-element.368, ...), branch_computations={%region_17.17_spmd, %region_18.20_spmd} | conditional | flops 174018560 | bytes 28467260 | solution.py:139
  969.4 3.5 squeeze.30
  977.3 3.5 squeeze.31
  980.8 3.2 fusion.12
  984.0 2.5 copy.101
  989.0 2.6 collective-permute-start
  992.9 25.5 %collective-permute-done = bf16[2,4,4,32,640]{4,3,2,1,0:T(8,128)(2,1)} collective-permute-done((bf16[2,4,4,32,640]{4,3,2,1,0:T(8,128)(2,1)}, bf16[2,4,4,32,640]{4,3,2,1,0:T(8,128)(2,1)}, u32[]{:S(2)}, u32[]{:S(2)}) %collective-permute-start) | collective-permute-done | bytes 1310752 | tf_op jit(solution)/shard_map/while/body/eval_jaxpr/ppermute | solution.py:17
  1018.4 28.7 %collective-permute-done.1 = bf16[2,4,4,32,640]{4,3,2,1,0:T(8,128)(2,1)} collective-permute-done((bf16[2,4,4,32,640]{4,3,2,1,0:T(8,128)(2,1)}, bf16[2,4,4,32,640]{4,3,2,1,0:T(8,128)(2,1)}, u32[]{:S(2)}, u32[]{:S(2)}) %collective-permute-start.1) | collective-permute-done | bytes 1310752 | tf_op jit(solution)/shard_map/while/body/eval_jaxpr/ppermute | solution.py:17
  1047.1 17.1 %conditional.5 = ((f32[4,10,128]{2,1,0:T(8,128)S(1)}, f32[4,10,128]{2,1,0:T(8,128)S(1)}, f32[4,10,128,64]{2,3,1,0:T(8,128)S(1)})) conditional(s32[]{:T(128)} %convert_element_type.114, (f32[4,10,128]{2,1,0:T(8,128)S(1)}, f32[4,10,128]{2,1,0:T(8,128)S(1)}, f32[4,10,128,64]{2,3,1,0:T(8,128)S(1)}) %get-tuple-element.368, ...), branch_computations={%region_17.17_spmd, %region_18.20_spmd} | conditional | flops 174018560 | bytes 28467260 | solution.py:139
  1049.6 3.5 squeeze.30
  1057.5 3.5 squeeze.31
  1061.0 3.2 fusion.12
  1064.2 2.5 copy.101
  1069.3 2.6 collective-permute-start
  1073.1 24.9 %collective-permute-done = bf16[2,4,4,32,640]{4,3,2,1,0:T(8,128)(2,1)} collective-permute-done((bf16[2,4,4,32,640]{4,3,2,1,0:T(8,128)(2,1)}, bf16[2,4,4,32,640]{4,3,2,1,0:T(8,128)(2,1)}, u32[]{:S(2)}, u32[]{:S(2)}) %collective-permute-start) | collective-permute-done | bytes 1310752 | tf_op jit(solution)/shard_map/while/body/eval_jaxpr/ppermute | solution.py:17
  1098.0 28.7 %collective-permute-done.1 = bf16[2,4,4,32,640]{4,3,2,1,0:T(8,128)(2,1)} collective-permute-done((bf16[2,4,4,32,640]{4,3,2,1,0:T(8,128)(2,1)}, bf16[2,4,4,32,640]{4,3,2,1,0:T(8,128)(2,1)}, u32[]{:S(2)}, u32[]{:S(2)}) %collective-permute-start.1) | collective-permute-done | bytes 1310752 | tf_op jit(solution)/shard_map/while/body/eval_jaxpr/ppermute | solution.py:17
  1126.7 17.1 %conditional.5 = ((f32[4,10,128]{2,1,0:T(8,128)S(1)}, f32[4,10,128]{2,1,0:T(8,128)S(1)}, f32[4,10,128,64]{2,3,1,0:T(8,128)S(1)})) conditional(s32[]{:T(128)} %convert_element_type.114, (f32[4,10,128]{2,1,0:T(8,128)S(1)}, f32[4,10,128]{2,1,0:T(8,128)S(1)}, f32[4,10,128,64]{2,3,1,0:T(8,128)S(1)}) %get-tuple-element.368, ...), branch_computations={%region_17.17_spmd, %region_18.20_spmd} | conditional | flops 174018560 | bytes 28467260 | solution.py:139
  1129.2 3.5 squeeze.30
  1137.1 3.5 squeeze.31
  1140.6 3.2 fusion.12
  1148.9 2.5 collective-permute-start
  1152.7 13.0 %collective-permute-done = bf16[2,4,4,32,640]{4,3,2,1,0:T(8,128)(2,1)} collective-permute-done((bf16[2,4,4,32,640]{4,3,2,1,0:T(8,128)(2,1)}, bf16[2,4,4,32,640]{4,3,2,1,0:T(8,128)(2,1)}, u32[]{:S(2)}, u32[]{:S(2)}) %collective-permute-start) | collective-permute-done | bytes 1310752 | tf_op jit(solution)/shard_map/while/body/eval_jaxpr/ppermute | solution.py:17
  1165.7 14.5 %collective-permute-done.1 = bf16[2,4,4,32,640]{4,3,2,1,0:T(8,128)(2,1)} collective-permute-done((bf16[2,4,4,32,640]{4,3,2,1,0:T(8,128)(2,1)}, bf16[2,4,4,32,640]{4,3,2,1,0:T(8,128)(2,1)}, u32[]{:S(2)}, u32[]{:S(2)}) %collective-permute-start.1) | collective-permute-done | bytes 1310752 | tf_op jit(solution)/shard_map/while/body/eval_jaxpr/ppermute | solution.py:17
  1180.2 17.1 %conditional.5 = ((f32[4,10,128]{2,1,0:T(8,128)S(1)}, f32[4,10,128]{2,1,0:T(8,128)S(1)}, f32[4,10,128,64]{2,3,1,0:T(8,128)S(1)})) conditional(s32[]{:T(128)} %convert_element_type.114, (f32[4,10,128]{2,1,0:T(8,128)S(1)}, f32[4,10,128]{2,1,0:T(8,128)S(1)}, f32[4,10,128,64]{2,3,1,0:T(8,128)S(1)}) %get-tuple-element.368, ...), branch_computations={%region_17.17_spmd, %region_18.20_spmd} | conditional | flops 174018560 | bytes 28467260 | solution.py:139
  1182.7 3.5 squeeze.30
  1190.6 3.5 squeeze.31
  1194.1 3.2 fusion.12
  1202.4 2.6 collective-permute-start
  1206.2 13.0 %collective-permute-done = bf16[2,4,4,32,640]{4,3,2,1,0:T(8,128)(2,1)} collective-permute-done((bf16[2,4,4,32,640]{4,3,2,1,0:T(8,128)(2,1)}, bf16[2,4,4,32,640]{4,3,2,1,0:T(8,128)(2,1)}, u32[]{:S(2)}, u32[]{:S(2)}) %collective-permute-start) | collective-permute-done | bytes 1310752 | tf_op jit(solution)/shard_map/while/body/eval_jaxpr/ppermute | solution.py:17
  1219.2 14.5 %collective-permute-done.1 = bf16[2,4,4,32,640]{4,3,2,1,0:T(8,128)(2,1)} collective-permute-done((bf16[2,4,4,32,640]{4,3,2,1,0:T(8,128)(2,1)}, bf16[2,4,4,32,640]{4,3,2,1,0:T(8,128)(2,1)}, u32[]{:S(2)}, u32[]{:S(2)}) %collective-permute-start.1) | collective-permute-done | bytes 1310752 | tf_op jit(solution)/shard_map/while/body/eval_jaxpr/ppermute | solution.py:17
  1233.7 17.1 %conditional.5 = ((f32[4,10,128]{2,1,0:T(8,128)S(1)}, f32[4,10,128]{2,1,0:T(8,128)S(1)}, f32[4,10,128,64]{2,3,1,0:T(8,128)S(1)})) conditional(s32[]{:T(128)} %convert_element_type.114, (f32[4,10,128]{2,1,0:T(8,128)S(1)}, f32[4,10,128]{2,1,0:T(8,128)S(1)}, f32[4,10,128,64]{2,3,1,0:T(8,128)S(1)}) %get-tuple-element.368, ...), branch_computations={%region_17.17_spmd, %region_18.20_spmd} | conditional | flops 174018560 | bytes 28467260 | solution.py:139
  1236.2 3.5 squeeze.30
  1244.1 3.5 squeeze.31
  1247.6 3.2 fusion.12
  1256.9 3.4 copy.44
  1260.3 3.8 dot_general.69
  (157 shorter events, 123.1 us)
Async XLA Ops:
  0.6 1264.7 %copy-start = (bf16[640,1280]{1,0:T(8,128)(2,1)S(1)}, bf16[640,1280]{1,0:T(8,128)(2,1)}, u32[]{:S(2)}) copy-start(bf16[640,1280]{1,0:T(8,128)(2,1)} %param.25) | copy-start | bytes 4915204
  0.6 10.7 copy-start.4
  0.7 2.7 copy-start.16
  4.1 711.9 %collective-permute-start.2 = (bf16[4,1,32,1280]{3,2,1,0:T(8,128)(2,1)}, bf16[4,1,32,1280]{3,2,1,0:T(8,128)(2,1)}, u32[]{:S(2)}, u32[]{:S(2)}) collective-permute-start(bf16[4,1,32,1280]{3,2,1,0:T(8,128)(2,1)} %get-tuple-element.259), channel_id=1, source_target_pairs={{0,8},{1,9},{2,10},{3,11},{4,12},{5,13},{6,14},{7,15},{8,16},{9,17... | collective-permute-start | bytes 983048 | tf_op jit(solution)/shard_map/ppermute | solution.py:17
  10.0 706.0 %collective-permute-start.3 = (bf16[4,1,32,1280]{3,2,1,0:T(8,128)(2,1)S(1)}, bf16[4,1,32,1280]{3,2,1,0:T(8,128)(2,1)}, u32[]{:S(2)}, u32[]{:S(2)}) collective-permute-start(bf16[4,1,32,1280]{3,2,1,0:T(8,128)(2,1)S(1)} %get-tuple-element.260), channel_id=1, source_target_pairs={{8,0},{9,1},{10,2},{11,3},{12,4},{13,5},{14,6},{15,7},{16,8},{17,9... | collective-permute-start | bytes 983048 | tf_op jit(solution)/shard_map/ppermute | solution.py:17
  365.8 345.2 %copy-start.19 = (s32[4,8]{1,0:T(4,128)S(1)}, s32[4,8]{1,0:T(4,128)}, u32[]{:S(2)}) copy-start(s32[4,8]{1,0:T(4,128)} %param.19) | copy-start | bytes 388
  365.8 345.5 %copy-start.17 = (f32[1280]{0:T(1024)S(1)}, f32[1280]{0:T(1024)}, u32[]{:S(2)}) copy-start(f32[1280]{0:T(1024)} %param.21) | copy-start | bytes 15364
  365.9 345.5 %copy-start.18 = (f32[1280]{0:T(1024)S(1)}, f32[1280]{0:T(1024)}, u32[]{:S(2)}) copy-start(f32[1280]{0:T(1024)} %param.20) | copy-start | bytes 15364
  711.0 1.4 copy-start.13
  713.2 8.4 copy-start.14
  727.6 1.7 copy-start.9
  729.3 1.3 copy-start.7
  730.6 6.4 copy-start.5
  743.0 5.9 copy-start.3
  751.0 1.6 copy-start.10
  753.3 29.9 %collective-permute-start = (bf16[2,4,4,32,640]{4,3,2,1,0:T(8,128)(2,1)}, bf16[2,4,4,32,640]{4,3,2,1,0:T(8,128)(2,1)}, u32[]{:S(2)}, u32[]{:S(2)}) collective-permute-start(bf16[2,4,4,32,640]{4,3,2,1,0:T(8,128)(2,1)} %get-tuple-element.349), channel_id=1, source_target_pairs={{0,8},{1,9},{2,10},{3,11},{4,12},{5,13},{6,14},{7,15},{8,16},{9,17... | collective-permute-start | bytes 3932168 | tf_op jit(solution)/shard_map/while/body/eval_jaxpr/ppermute | solution.py:17
  755.7 33.3 %collective-permute-start.1 = (bf16[2,4,4,32,640]{4,3,2,1,0:T(8,128)(2,1)}, bf16[2,4,4,32,640]{4,3,2,1,0:T(8,128)(2,1)}, u32[]{:S(2)}, u32[]{:S(2)}) collective-permute-start(bf16[2,4,4,32,640]{4,3,2,1,0:T(8,128)(2,1)} %get-tuple-element.350), channel_id=1, source_target_pairs={{8,0},{9,1},{10,2},{11,3},{12,4},{13,5},{14,6},{15,7},{16,8},{17,9... | collective-permute-start | bytes 3932168 | tf_op jit(solution)/shard_map/while/body/eval_jaxpr/ppermute | solution.py:17
  797.3 1.5 copy-start.2
  811.1 46.2 %collective-permute-start = (bf16[2,4,4,32,640]{4,3,2,1,0:T(8,128)(2,1)}, bf16[2,4,4,32,640]{4,3,2,1,0:T(8,128)(2,1)}, u32[]{:S(2)}, u32[]{:S(2)}) collective-permute-start(bf16[2,4,4,32,640]{4,3,2,1,0:T(8,128)(2,1)} %get-tuple-element.349), channel_id=1, source_target_pairs={{0,8},{1,9},{2,10},{3,11},{4,12},{5,13},{6,14},{7,15},{8,16},{9,17... | collective-permute-start | bytes 3932168 | tf_op jit(solution)/shard_map/while/body/eval_jaxpr/ppermute | solution.py:17
  829.5 56.7 %collective-permute-start.1 = (bf16[2,4,4,32,640]{4,3,2,1,0:T(8,128)(2,1)}, bf16[2,4,4,32,640]{4,3,2,1,0:T(8,128)(2,1)}, u32[]{:S(2)}, u32[]{:S(2)}) collective-permute-start(bf16[2,4,4,32,640]{4,3,2,1,0:T(8,128)(2,1)} %get-tuple-element.350), channel_id=1, source_target_pairs={{8,0},{9,1},{10,2},{11,3},{12,4},{13,5},{14,6},{15,7},{16,8},{17,9... | collective-permute-start | bytes 3932168 | tf_op jit(solution)/shard_map/while/body/eval_jaxpr/ppermute | solution.py:17
  894.4 1.5 copy-start.2
  908.3 29.9 %collective-permute-start = (bf16[2,4,4,32,640]{4,3,2,1,0:T(8,128)(2,1)}, bf16[2,4,4,32,640]{4,3,2,1,0:T(8,128)(2,1)}, u32[]{:S(2)}, u32[]{:S(2)}) collective-permute-start(bf16[2,4,4,32,640]{4,3,2,1,0:T(8,128)(2,1)} %get-tuple-element.349), channel_id=1, source_target_pairs={{0,8},{1,9},{2,10},{3,11},{4,12},{5,13},{6,14},{7,15},{8,16},{9,17... | collective-permute-start | bytes 3932168 | tf_op jit(solution)/shard_map/while/body/eval_jaxpr/ppermute | solution.py:17
  910.8 56.1 %collective-permute-start.1 = (bf16[2,4,4,32,640]{4,3,2,1,0:T(8,128)(2,1)}, bf16[2,4,4,32,640]{4,3,2,1,0:T(8,128)(2,1)}, u32[]{:S(2)}, u32[]{:S(2)}) collective-permute-start(bf16[2,4,4,32,640]{4,3,2,1,0:T(8,128)(2,1)} %get-tuple-element.350), channel_id=1, source_target_pairs={{8,0},{9,1},{10,2},{11,3},{12,4},{13,5},{14,6},{15,7},{16,8},{17,9... | collective-permute-start | bytes 3932168 | tf_op jit(solution)/shard_map/while/body/eval_jaxpr/ppermute | solution.py:17
  975.2 1.5 copy-start.2
  989.0 29.4 %collective-permute-start = (bf16[2,4,4,32,640]{4,3,2,1,0:T(8,128)(2,1)}, bf16[2,4,4,32,640]{4,3,2,1,0:T(8,128)(2,1)}, u32[]{:S(2)}, u32[]{:S(2)}) collective-permute-start(bf16[2,4,4,32,640]{4,3,2,1,0:T(8,128)(2,1)} %get-tuple-element.349), channel_id=1, source_target_pairs={{0,8},{1,9},{2,10},{3,11},{4,12},{5,13},{6,14},{7,15},{8,16},{9,17... | collective-permute-start | bytes 3932168 | tf_op jit(solution)/shard_map/while/body/eval_jaxpr/ppermute | solution.py:17
  991.6 55.5 %collective-permute-start.1 = (bf16[2,4,4,32,640]{4,3,2,1,0:T(8,128)(2,1)}, bf16[2,4,4,32,640]{4,3,2,1,0:T(8,128)(2,1)}, u32[]{:S(2)}, u32[]{:S(2)}) collective-permute-start(bf16[2,4,4,32,640]{4,3,2,1,0:T(8,128)(2,1)} %get-tuple-element.350), channel_id=1, source_target_pairs={{8,0},{9,1},{10,2},{11,3},{12,4},{13,5},{14,6},{15,7},{16,8},{17,9... | collective-permute-start | bytes 3932168 | tf_op jit(solution)/shard_map/while/body/eval_jaxpr/ppermute | solution.py:17
  1055.4 1.5 copy-start.2
  1069.3 28.7 %collective-permute-start = (bf16[2,4,4,32,640]{4,3,2,1,0:T(8,128)(2,1)}, bf16[2,4,4,32,640]{4,3,2,1,0:T(8,128)(2,1)}, u32[]{:S(2)}, u32[]{:S(2)}) collective-permute-start(bf16[2,4,4,32,640]{4,3,2,1,0:T(8,128)(2,1)} %get-tuple-element.349), channel_id=1, source_target_pairs={{0,8},{1,9},{2,10},{3,11},{4,12},{5,13},{6,14},{7,15},{8,16},{9,17... | collective-permute-start | bytes 3932168 | tf_op jit(solution)/shard_map/while/body/eval_jaxpr/ppermute | solution.py:17
  1071.8 54.9 %collective-permute-start.1 = (bf16[2,4,4,32,640]{4,3,2,1,0:T(8,128)(2,1)}, bf16[2,4,4,32,640]{4,3,2,1,0:T(8,128)(2,1)}, u32[]{:S(2)}, u32[]{:S(2)}) collective-permute-start(bf16[2,4,4,32,640]{4,3,2,1,0:T(8,128)(2,1)} %get-tuple-element.350), channel_id=1, source_target_pairs={{8,0},{9,1},{10,2},{11,3},{12,4},{13,5},{14,6},{15,7},{16,8},{17,9... | collective-permute-start | bytes 3932168 | tf_op jit(solution)/shard_map/while/body/eval_jaxpr/ppermute | solution.py:17
  1135.0 1.5 copy-start.2
  1148.9 16.9 %collective-permute-start = (bf16[2,4,4,32,640]{4,3,2,1,0:T(8,128)(2,1)}, bf16[2,4,4,32,640]{4,3,2,1,0:T(8,128)(2,1)}, u32[]{:S(2)}, u32[]{:S(2)}) collective-permute-start(bf16[2,4,4,32,640]{4,3,2,1,0:T(8,128)(2,1)} %get-tuple-element.349), channel_id=1, source_target_pairs={{0,8},{1,9},{2,10},{3,11},{4,12},{5,13},{6,14},{7,15},{8,16},{9,17... | collective-permute-start | bytes 3932168 | tf_op jit(solution)/shard_map/while/body/eval_jaxpr/ppermute | solution.py:17
  1151.4 28.8 %collective-permute-start.1 = (bf16[2,4,4,32,640]{4,3,2,1,0:T(8,128)(2,1)}, bf16[2,4,4,32,640]{4,3,2,1,0:T(8,128)(2,1)}, u32[]{:S(2)}, u32[]{:S(2)}) collective-permute-start(bf16[2,4,4,32,640]{4,3,2,1,0:T(8,128)(2,1)} %get-tuple-element.350), channel_id=1, source_target_pairs={{8,0},{9,1},{10,2},{11,3},{12,4},{13,5},{14,6},{15,7},{16,8},{17,9... | collective-permute-start | bytes 3932168 | tf_op jit(solution)/shard_map/while/body/eval_jaxpr/ppermute | solution.py:17
  1188.5 1.5 copy-start.2
  1202.4 16.9 %collective-permute-start = (bf16[2,4,4,32,640]{4,3,2,1,0:T(8,128)(2,1)}, bf16[2,4,4,32,640]{4,3,2,1,0:T(8,128)(2,1)}, u32[]{:S(2)}, u32[]{:S(2)}) collective-permute-start(bf16[2,4,4,32,640]{4,3,2,1,0:T(8,128)(2,1)} %get-tuple-element.349), channel_id=1, source_target_pairs={{0,8},{1,9},{2,10},{3,11},{4,12},{5,13},{6,14},{7,15},{8,16},{9,17... | collective-permute-start | bytes 3932168 | tf_op jit(solution)/shard_map/while/body/eval_jaxpr/ppermute | solution.py:17
  1204.9 28.8 %collective-permute-start.1 = (bf16[2,4,4,32,640]{4,3,2,1,0:T(8,128)(2,1)}, bf16[2,4,4,32,640]{4,3,2,1,0:T(8,128)(2,1)}, u32[]{:S(2)}, u32[]{:S(2)}) collective-permute-start(bf16[2,4,4,32,640]{4,3,2,1,0:T(8,128)(2,1)} %get-tuple-element.350), channel_id=1, source_target_pairs={{8,0},{9,1},{10,2},{11,3},{12,4},{13,5},{14,6},{15,7},{16,8},{17,9... | collective-permute-start | bytes 3932168 | tf_op jit(solution)/shard_map/while/body/eval_jaxpr/ppermute | solution.py:17
  1242.0 1.5 copy-start.2
  1260.3 3.8 copy-start.11
  1260.3 3.8 copy-start.12
  1264.1 1.2 copy-start.6
  1264.1 1.8 copy-start.8
  1264.1 2.0 copy-start.15
where the time goes:
time: 1270 us
  blocking collectives  693 us (55%)
  waiting for transfers between devices  305 us (24%)
  local copies, waits for them, and re-layouts  141 us (11%)
  matrix products  63.4 us (5%)
  starting transfers between devices  49.7 us (4%)
  other arithmetic  14.6 us (1%)
    psum x1, blocking collectives, on_device(): totals = lax.psum(slot_mask * jnp.sum(grouped, axis=(1, 3))[None], 'band')  351 us
    psum x1, blocking collectives, on_device(): lax.psum(slot_mask * jnp.sum(deviation * deviation, axis=(1, 3))[None], '...  342 us
    ppermute x16, waiting for transfers between devices, shifted(): return lax.ppermute(value, axis, pairs)  305 us
    ppermute x16, starting transfers between devices, shifted(): return lax.ppermute(value, axis, pairs)  49.7 us
    while x14, local copies, waits for them, and re-layouts  35.1 us
  transfers between devices with their start and end apart: 16, of which 14 were waited for; matrix products, arithmetic and copies ran while one was open for 1% of the time, Pallas kernels for 0%

commit v1 on v0

v1 whole, which is shorter than its diff:
```python
import math

import jax
import jax.numpy as jnp
from jax import lax
from jax.experimental import pallas as pl
from jax.experimental.pallas import tpu as pltpu
from jax.sharding import PartitionSpec as P

IMG_ROWS = 32
GROUPS = 32
HEADS = 10
TDIM = 1280
LANES = 128
MIB = 1 << 20
STACK = 8


def rotated(value, by):
    count = lax.axis_size("band")
    return lax.ppermute(value, "band", [(i, (i + by) % count) for i in range(count)])


def shifted(value, by):
    count = lax.axis_size("band")
    pairs = [(i, i + by) for i in range(count) if 0 <= i + by < count]
    return lax.ppermute(value, "band", pairs)


def flipped(value, bit):
    count = lax.axis_size("band")
    return lax.ppermute(value, "band", [(i, i ^ (bit * STACK)) for i in range(count)])


def time_term(timestep, time_weight):
    half_dim = TDIM // 2
    frequency = jnp.exp(-math.log(10000.0) * jnp.arange(half_dim, dtype=jnp.float32) / half_dim)
    angles = timestep.astype(jnp.float32)[:, None] * frequency[None, :]
    embedding = jnp.concatenate([jnp.cos(angles), jnp.sin(angles)], axis=1)
    return jnp.dot(
        jax.nn.silu(embedding), time_weight.astype(jnp.float32), precision=lax.Precision.HIGHEST
    )


def group_matrix(channels, per_group, transposed):
    shape = (LANES, channels) if transposed else (channels, LANES)
    channel = lax.broadcasted_iota(jnp.int32, shape, 1 if transposed else 0)
    first = lax.broadcasted_iota(jnp.int32, shape, 0 if transposed else 1) * per_group
    return jnp.where((channel >= first) & (channel < first + per_group), 1.0, 0.0)


def exact_dot(left, right):
    return jnp.dot(
        left, right, precision=lax.Precision.HIGHEST, preferred_element_type=jnp.float32
    )


def stats_kernel(latent, out, sums):
    images, tokens, channels = latent.shape
    per_group = channels // GROUPS
    gather = group_matrix(channels, per_group, False)
    spread = group_matrix(channels, per_group, True)
    sums[...] = jnp.zeros_like(sums)
    for i in range(images):
        sums[i : i + 1, :] = jnp.sum(latent[i].astype(jnp.float32), axis=0, keepdims=True)
    mean = exact_dot(sums[...], gather) * (1.0 / (tokens * per_group))
    center = exact_dot(mean, spread)
    for i in range(images):
        deviation = latent[i].astype(jnp.float32) - center[i : i + 1, :]
        sums[i : i + 1, :] = jnp.sum(deviation * deviation, axis=0, keepdims=True)
    out[0] = mean
    out[1] = exact_dot(sums[...], gather)


def local_stats(latent):
    images, tokens, channels = latent.shape
    return pl.pallas_call(
        stats_kernel,
        out_shape=jax.ShapeDtypeStruct((2, 8, LANES), jnp.float32),
        scratch_shapes=[pltpu.VMEM((8, channels), jnp.float32)],
        compiler_params=pltpu.CompilerParams(vmem_limit_bytes=24 * MIB),
        cost_estimate=pl.CostEstimate(
            flops=8 * latent.size, bytes_accessed=2 * latent.size, transcendentals=0
        ),
        name="group_stats",
    )(latent)


def merged(own, other, count):
    gap = own[0] - other[0]
    return jnp.stack([(own[0] + other[0]) * 0.5, own[1] + other[1] + gap * gap * (count * 0.5)])


def conv_kernel(
    counted,
    stats,
    gain,
    shift,
    bias,
    latent,
    top,
    bottom,
    conv_hbm,
    attn_hbm,
    hidden,
    normal,
    queries,
    ext,
    weights,
    query_weight,
    acc,
    scales,
    sems,
):
    images, tokens, channels = latent.shape
    columns = top.shape[1]
    height = tokens // columns
    width = acc.shape[1]
    slab = images * columns
    inner = query_weight.shape[1]
    copies = [
        pltpu.make_async_copy(conv_hbm.at[dy], weights.at[dy], sems.at[dy]) for dy in range(3)
    ]
    copies.append(pltpu.make_async_copy(attn_hbm.at[:, :inner], query_weight, sems.at[3]))
    for copy in copies:
        copy.start()
    spread = group_matrix(channels, channels // GROUPS, True)
    scales[0] = exact_dot(stats[0], spread)
    inverse = 1.0 / jnp.sqrt(stats[1] * (1.0 / counted) + 1e-05)
    scales[1] = exact_dot(inverse, spread) * gain[...]
    place = lax.broadcasted_iota(jnp.int32, (columns, channels), 0)

    def put(value, row, i):
        rows = pl.ds(pl.multiple_of(row * slab + i * columns, columns), columns)
        before = jnp.where(place == 0, 0.0, pltpu.roll(value, 1, 0))
        after = jnp.where(place == columns - 1, 0.0, pltpu.roll(value, columns - 1, 0))
        ext[rows, 0:channels] = before.astype(jnp.bfloat16)
        ext[rows, channels : 2 * channels] = value.astype(jnp.bfloat16)
        ext[rows, 2 * channels : 3 * channels] = after.astype(jnp.bfloat16)

    def fill(i, carry):
        center = scales[0, pl.ds(i, 1), :]
        factor = scales[1, pl.ds(i, 1), :]
        put(top[i].astype(jnp.float32), 0, i)
        put(bottom[i].astype(jnp.float32), height + 1, i)
        for y in range(height):
            value = latent[i, y * columns : (y + 1) * columns, :].astype(jnp.float32)
            value = (value - center) * factor + shift[...]
            put(value / (1.0 + jnp.exp(-value)), y + 1, i)
        return carry

    lax.fori_loop(0, images, fill, 0)
    for dy in range(3):
        copies[dy].wait()
        part = jnp.dot(
            ext[dy * slab : (dy + height) * slab, :],
            weights[dy],
            preferred_element_type=jnp.float32,
        )
        if dy == 0:
            acc[...] = part
        else:
            acc[...] += part

    def finish(i, carry):
        for y in range(height):
            tokens_of = slice(y * columns, (y + 1) * columns)
            rows = pl.ds(pl.multiple_of(y * slab + i * columns, columns), columns)
            window = latent[i, tokens_of, :width].astype(jnp.float32) + acc[rows, :]
            window = (window + bias[pl.ds(i, 1), :]).astype(jnp.bfloat16)
            whole = jnp.concatenate([window, latent[i, tokens_of, width:]], axis=-1)
            hidden[i, tokens_of, :] = whole
            wide = whole.astype(jnp.float32)
            wide = wide - jnp.mean(wide, axis=-1, keepdims=True)
            variance = jnp.mean(wide * wide, axis=-1, keepdims=True)
            normal[i, tokens_of, :] = (wide * (1.0 / jnp.sqrt(variance + 1e-05))).astype(
                jnp.bfloat16
            )
        return carry

    lax.fori_loop(0, images, finish, 0)
    copies[3].wait()
    found = jnp.dot(
        normal[...].reshape(images * tokens, channels),
        query_weight[...],
        preferred_element_type=jnp.float32,
    )
    found = found.astype(jnp.bfloat16) * jnp.bfloat16((inner // HEADS) ** -0.5)
    queries[...] = found.reshape(images, tokens, inner)


def convolve(stats, gain, shift, bias, latent, top, bottom, conv_weight, attn_in, counted):
    images, tokens, channels = latent.shape
    columns = top.shape[1]
    width = conv_weight.shape[-1]
    inner = attn_in.shape[1] // 3
    slab = images * columns
    vmem = pl.BlockSpec(memory_space=pltpu.VMEM)
    anywhere = pl.BlockSpec(memory_space=pl.ANY)

    def body(*refs):
        conv_kernel(counted, *refs)

    return pl.pallas_call(
        body,
        out_shape=(
            jax.ShapeDtypeStruct(latent.shape, jnp.bfloat16),
            jax.ShapeDtypeStruct(latent.shape, jnp.bfloat16),
            jax.ShapeDtypeStruct((images, tokens, inner), jnp.bfloat16),
        ),
        in_specs=[vmem] * 7 + [anywhere] * 2,
        out_specs=(vmem,) * 3,
        scratch_shapes=[
            pltpu.VMEM(((tokens // columns + 2) * slab, 3 * channels), jnp.bfloat16),
            pltpu.VMEM((3, 3 * channels, width), jnp.bfloat16),
            pltpu.VMEM((channels, inner), jnp.bfloat16),
            pltpu.VMEM((images * tokens, width), jnp.float32),
            pltpu.VMEM((2, 8, channels), jnp.float32),
            pltpu.SemaphoreType.DMA((4,)),
        ],
        compiler_params=pltpu.CompilerParams(vmem_limit_bytes=48 * MIB),
        cost_estimate=pl.CostEstimate(
            flops=2 * images * tokens * channels * (9 * width + inner),
            bytes_accessed=2 * (conv_weight.size + channels * inner + 5 * latent.size),
            transcendentals=latent.size,
        ),
        name="conv_queries",
    )(stats, gain, shift, bias, latent, top, bottom, conv_weight, attn_in)


def project_kernel(normal, weight, out):
    images, tokens, channels = normal.shape
    found = jnp.dot(
        normal[...].reshape(images * tokens, channels),
        weight[...],
        preferred_element_type=jnp.float32,
    )
    out[0] = found.astype(jnp.bfloat16).reshape(out.shape[1:])


def project(normal, attn_in):
    images, tokens, channels = normal.shape
    inner = attn_in.shape[1] // 3
    return pl.pallas_call(
        project_kernel,
        grid=(2,),
        out_shape=jax.ShapeDtypeStruct((2, images, tokens, inner), jnp.bfloat16),
        in_specs=[
            pl.BlockSpec(normal.shape, lambda j: (0, 0, 0)),
            pl.BlockSpec((channels, inner), lambda j: (0, j + 1)),
        ],
        out_specs=pl.BlockSpec((1, images, tokens, inner), lambda j: (j, 0, 0, 0)),
        compiler_params=pltpu.CompilerParams(vmem_limit_bytes=24 * MIB),
        cost_estimate=pl.CostEstimate(
            flops=4 * images * tokens * channels * inner,
            bytes_accessed=4 * (channels * inner + normal.size),
            transcendentals=0,
        ),
        name="keys_values",
    )(normal, attn_in)


def attend_kernel(queries, first, second, third, fourth, out, logs):
    tokens, inner = queries.shape[1:]
    size = inner // HEADS
    pair = 2 * size
    lane = lax.broadcasted_iota(jnp.int32, (tokens, pair), 1)
    low = lane < size
    sources = (first, second, third, fourth)
    found = jnp.zeros((tokens, LANES), jnp.float32)
    spot = lax.broadcasted_iota(jnp.int32, (tokens, LANES), 1)
    for p in range(HEADS // 2):
        lanes = slice(p * pair, (p + 1) * pair)
        query = queries[0, :, lanes]
        blank = jnp.zeros_like(query)
        both = jnp.concatenate(
            [jnp.where(low, query, blank), jnp.where(low, blank, query)], axis=0
        )
        keys = jnp.concatenate([s[0, 0, :, lanes] for s in sources], axis=0)
        values = jnp.concatenate([s[1, 0, :, lanes] for s in sources], axis=0)
        scores = lax.dot_general(
            both, keys, (((1,), (1,)), ((), ())), preferred_element_type=jnp.float32
        )
        peak = jnp.max(scores, axis=-1, keepdims=True)
        exponent = jnp.exp(scores - peak)
        total = jnp.sum(exponent, axis=-1, keepdims=True)
        context = jnp.dot(
            exponent.astype(jnp.bfloat16), values, preferred_element_type=jnp.float32
        )
        context = context * (1.0 / total)
        out[0, :, lanes] = jnp.where(low, context[:tokens], context[tokens:]).astype(out.dtype)
        level = peak + jnp.log(total)
        found = jnp.where(spot == 2 * p, level[:tokens], found)
        found = jnp.where(spot == 2 * p + 1, level[tokens:], found)
    logs[0] = jnp.transpose(found)[: logs.shape[1], :]


def attend(queries, first, second, third, fourth, start, images, dtype):
    tokens, inner = queries.shape[1:]
    kv_spec = pl.BlockSpec((2, 1, tokens, inner), lambda i: (0, i + start, 0, 0))
    elements = images * HEADS * tokens * 4 * tokens
    return pl.pallas_call(
        attend_kernel,
        grid=(images,),
        out_shape=(
            jax.ShapeDtypeStruct((images, tokens, inner), dtype),
            jax.ShapeDtypeStruct((images, 16, tokens), jnp.float32),
        ),
        in_specs=[pl.BlockSpec((1, tokens, inner), lambda i: (i, 0, 0))] + [kv_spec] * 4,
        out_specs=(
            pl.BlockSpec((1, tokens, inner), lambda i: (i, 0, 0)),
            pl.BlockSpec((1, 16, tokens), lambda i: (i, 0, 0)),
        ),
        compiler_params=pltpu.CompilerParams(vmem_limit_bytes=24 * MIB),
        cost_estimate=pl.CostEstimate(
            flops=4 * elements * 256,
            bytes_accessed=images * tokens * inner * 24,
            transcendentals=elements,
        ),
        name="attend",
    )(queries, first, second, third, fourth)


def join_kernel(own, own_logs, far, far_logs, hidden, weight, out, attended):
    images, tokens, inner = own.shape
    size = inner // HEADS
    pair = 2 * size
    low = lax.broadcasted_iota(jnp.int32, (tokens, pair), 1) < size
    for i in range(images):
        here, there = own_logs[i], far_logs[i]
        top = jnp.maximum(here, there)
        here, there = jnp.exp(here - top), jnp.exp(there - top)
        share = there * (1.0 / (here + there))
        share = jnp.concatenate(
            [share, jnp.zeros((LANES - share.shape[0], tokens), jnp.float32)], axis=0
        )
        share = jnp.transpose(share)
        for p in range(HEADS // 2):
            lanes = slice(p * pair, (p + 1) * pair)
            part = jnp.where(
                low,
                jnp.broadcast_to(share[:, 2 * p : 2 * p + 1], (tokens, pair)),
                jnp.broadcast_to(share[:, 2 * p + 1 : 2 * p + 2], (tokens, pair)),
            )
            mine = own[i, :, lanes].astype(jnp.float32)
            theirs = far[i, :, lanes].astype(jnp.float32)
            attended[i * tokens : (i + 1) * tokens, lanes] = (
                mine * (1.0 - part) + theirs * part
            ).astype(jnp.bfloat16)
    update = jnp.dot(attended[...], weight[...], preferred_element_type=jnp.float32)
    update = update.reshape(out.shape)
    out[...] = (hidden[...].astype(jnp.float32) + update).astype(jnp.bfloat16)


def join(own, own_logs, far, far_logs, hidden, attn_out):
    images, tokens, inner = own.shape
    channels = hidden.shape[-1]
    step = 2

    def spec(rows, lanes):
        return pl.BlockSpec((step, rows, lanes), lambda i: (i, 0, 0))

    return pl.pallas_call(
        join_kernel,
        grid=(images // step,),
        out_shape=jax.ShapeDtypeStruct(hidden.shape, jnp.bfloat16),
        in_specs=[
            spec(tokens, inner),
            spec(16, tokens),
            spec(tokens, inner),
            spec(16, tokens),
            spec(tokens, channels),
            pl.BlockSpec(attn_out.shape, lambda i: (0, 0)),
        ],
        out_specs=spec(tokens, channels),
        scratch_shapes=[pltpu.VMEM((step * tokens, inner), jnp.bfloat16)],
        compiler_params=pltpu.CompilerParams(vmem_limit_bytes=24 * MIB),
        cost_estimate=pl.CostEstimate(
            flops=2 * images * tokens * inner * channels,
            bytes_accessed=2 * attn_out.size + 4 * hidden.size + 6 * own.size,
            transcendentals=0,
        ),
        name="join_project",
    )(own, own_logs, far, far_logs, hidden, attn_out)


def on_device(
    latent,
    stale_act,
    stale_kv,
    timestep,
    norm_gain,
    norm_shift,
    conv_weight,
    time_weight,
    attn_in,
    attn_out,
):
    images, height, columns, channels = latent.shape
    width = conv_weight.shape[3]
    inner = attn_out.shape[0]
    tokens = height * columns
    per_group = channels // GROUPS
    out_shape = latent.shape
    kv_shape = stale_kv.shape
    slot = lax.axis_index("band") % STACK
    latent = latent.reshape(images, tokens, channels)
    stale_kv = stale_kv.reshape(2, images, tokens, inner)

    top = shifted(stale_act[:, height - 1], STACK)
    bottom = shifted(stale_act[:, 0], -STACK)
    kv_up = rotated(stale_kv, 2 * STACK)
    kv_down = rotated(stale_kv, -2 * STACK)
    kv_far = rotated(stale_kv, 4 * STACK)

    stats = local_stats(latent)
    count = tokens * per_group
    for bit in (1, 2, 4):
        stats = merged(stats, flipped(stats, bit), count)
        count *= 2

    own_steps = lax.dynamic_index_in_dim(timestep, slot, 1, keepdims=False)
    bias = time_term(own_steps, time_weight)
    hidden, normal, queries = convolve(
        stats,
        norm_gain.reshape(1, channels),
        norm_shift.reshape(1, channels),
        bias,
        latent,
        top,
        bottom,
        conv_weight.reshape(3, 3 * channels, width),
        attn_in,
        float(count),
    )
    half = images // 2
    far_queries = [flipped(queries[k * half : (k + 1) * half], 1) for k in range(2)]
    fresh_kv = project(normal, attn_in)
    own, own_logs = attend(
        queries, fresh_kv, kv_up, kv_down, kv_far, 0, images, jnp.float32
    )
    far, far_logs = [], []
    for k in range(2):
        context, logs = attend(
            far_queries[k], stale_kv, kv_up, kv_down, kv_far, k * half, half, jnp.bfloat16
        )
        far.append(flipped(context, 1))
        far_logs.append(flipped(logs, 1))
    block_out = join(
        own,
        own_logs,
        jnp.concatenate(far, axis=0),
        jnp.concatenate(far_logs, axis=0),
        hidden,
        attn_out,
    )
    return (block_out.reshape(out_shape), fresh_kv.reshape(kv_shape))


def solution(mesh):
    return jax.shard_map(
        on_device,
        mesh=mesh,
        in_specs=(
            P("img", "band", None, None),
            P("img", "band", None, None),
            P(None, "img", "band", None, None),
            P("img", None),
            P(),
            P(),
            P(),
            P(),
            P(),
            P(),
        ),
        out_specs=(P("img", "band", None, None), P(None, "img", "band", None, None)),
        check_vma=False,
    )
```

time: 1270 us -> 143 us (0.11)
  blocking collectives: 693 us -> 0 us
  waiting for transfers between devices: 305 us -> 64.5 us
  local copies, waits for them, and re-layouts: 141 us -> 2.32 us
  matrix products: 63.4 us -> 0.74 us
  Pallas kernels: 0 us -> 45.2 us
  starting transfers between devices: 49.7 us -> 28.6 us
  other arithmetic: 14.6 us -> 0.47 us
    psum x2 -> x0, blocking collectives: 693 us -> none  [the longest x1 351 us: on_device(): totals = lax.psum(slot_mask * jnp.sum(grouped, axis=(1, 3))[None], 'band')]
    ppermute x16 -> x14, waiting for transfers between devices: 305 us -> 64.5 us  [the longest x9 54.4 us: flipped(): lax.ppermute(value, 'band', [(i, i ^ bit * STACK) for i in range(count)])]
    dot_general x27 -> x0, matrix products: 62.6 us -> none  [the longest x8 23.1 us: attend_block(): jnp.einsum('bhqk,bkhd->bhqd', exponent.astype(jnp.bfloat16), values, pref...]
    squeeze x14 -> x1, local copies, waits for them, and re-layouts: 49.6 us -> 0.87 us  [on_device(): bottom = shifted(stale_act[:, 0], -STACK)]
    pallas_call x0 -> x7, Pallas kernels: none -> 45.2 us  [the longest x1 18.8 us: convolve(): pl.pallas_call(body, out_shape=(jax.ShapeDtypeStruct(latent.shape, jnp.bf...]
    while x14 -> x0, local copies, waits for them, and re-layouts: 35.1 us -> none
    ppermute x16 -> x14, starting transfers between devices: 49.7 us -> 28.6 us  [the longest x9 18.8 us: flipped(): lax.ppermute(value, 'band', [(i, i ^ bit * STACK) for i in range(count)])]
    slice x9 -> x1, local copies, waits for them, and re-layouts: 18.9 us -> 0.06 us  [on_device(): queries[k * half:(k + 1) * half]]
  transfers between devices with their start and end apart: 16 -> 14, of which waited for: 14 -> 4; matrix products, arithmetic and copies ran while one was open for 1% -> 1% of each run, Pallas kernels for 0% -> 29%
where the time goes in v1:
time: 143 us
  waiting for transfers between devices  64.5 us (45%)
  Pallas kernels  45.2 us (32%)
  starting transfers between devices  28.6 us (20%)
  local copies, waits for them, and re-layouts  2.32 us (2%)
    ppermute x9, waiting for transfers between devices, flipped(): lax.ppermute(value, 'band', [(i, i ^ bit * STACK) for i in range(count)])  54.4 us
    pallas_call x1, Pallas kernels, convolve(): pl.pallas_call(body, out_shape=(jax.ShapeDtypeStruct(latent.shape, jnp.bf...  18.8 us
    ppermute x9, starting transfers between devices, flipped(): lax.ppermute(value, 'band', [(i, i ^ bit * STACK) for i in range(count)])  18.8 us
    pallas_call x3, Pallas kernels, attend(): pl.pallas_call(attend_kernel, grid=(images,), out_shape=(jax.ShapeDtypeSt...  17.4 us
    ppermute x2, waiting for transfers between devices, shifted(): return lax.ppermute(value, 'band', pairs)  10 us
    ppermute x3, starting transfers between devices, rotated(): lax.ppermute(value, 'band', [(i, (i + by) % count) for i in range(count)])  6.05 us
    ppermute x2, starting transfers between devices, shifted(): return lax.ppermute(value, 'band', pairs)  3.71 us
    pallas_call x1, Pallas kernels, project(): pl.pallas_call(project_kernel, grid=(2,), out_shape=jax.ShapeDtypeStruct(...  3.56 us
  transfers between devices with their start and end apart: 14, of which 4 were waited for; matrix products, arithmetic and copies ran while one was open for 1% of the time, Pallas kernels for 29%

profile of v1, /device:TPU:0, one launch (start us, length us, event | category | flops | bytes accessed | tf_op | source)
XLA Modules:
  0.0 142.6 jit_solution(6048837551676054666)
XLA Ops:
  0.6 0.0 copy-start
  0.6 2.1 %collective-permute-start.5 = (bf16[2,4,128,640]{3,2,1,0:T(8,128)(2,1)}, bf16[2,4,128,640]{3,2,1,0:T(8,128)(2,1)S(1)}, u32[]{:S(2)}, u32[]{:S(2)}) collective-permute-start(bf16[2,4,128,640]{3,2,1,0:T(8,128)(2,1)} %bitcast.14), channel_id=1, source_target_pairs={{0,16},{1,17},{2,18},{3,19},{4,20},{5,21},{6,22},{7,23},{8,24},{9,... | collective-permute-start | bytes 3932168 | tf_op jit(solution)/shard_map/ppermute | solution.py:21
  2.7 2.2 %collective-permute-start.6 = (bf16[2,4,128,640]{3,2,1,0:T(8,128)(2,1)}, bf16[2,4,128,640]{3,2,1,0:T(8,128)(2,1)}, u32[]{:S(2)}, u32[]{:S(2)}) collective-permute-start(bf16[2,4,128,640]{3,2,1,0:T(8,128)(2,1)} %bitcast.15), channel_id=1, source_target_pairs={{0,48},{1,49},{2,50},{3,51},{4,52},{5,53},{6,54},{7,55},{8,56},{9,... | collective-permute-start | bytes 3932168 | tf_op jit(solution)/shard_map/ppermute | solution.py:21
  4.9 1.8 %collective-permute-start.7 = (bf16[2,4,128,640]{3,2,1,0:T(8,128)(2,1)}, bf16[2,4,128,640]{3,2,1,0:T(8,128)(2,1)}, u32[]{:S(2)}, u32[]{:S(2)}) collective-permute-start(bf16[2,4,128,640]{3,2,1,0:T(8,128)(2,1)} %bitcast.16), channel_id=1, source_target_pairs={{0,32},{1,33},{2,34},{3,35},{4,36},{5,37},{6,38},{7,39},{8,40},{9,... | collective-permute-start | bytes 3932168 | tf_op jit(solution)/shard_map/ppermute | solution.py:21
  6.7 0.0 copy-start.4
  6.7 1.3 copy-done.4
  8.0 0.0 copy-start.7
  8.0 0.0 copy-start.10
  8.0 1.8 %group_stats.1 = f32[2,8,128]{2,1,0:T(8,128)S(1)} custom-call(bf16[4,128,1280]{2,1,0:T(8,128)(2,1)S(1)} %bitcast.22), custom_call_target="tpu_custom_call" | custom-call | flops 5242880 | bytes 1310720 | tf_op jit(solution)/shard_map/group_stats/pallas_call | solution.py:77
  9.8 0.0 copy-start.8
  9.8 0.0 copy-start.9
  9.9 3.3 %collective-permute-start = (f32[2,8,128]{2,1,0:T(8,128)S(1)}, f32[2,8,128]{2,1,0:T(8,128)S(1)}, u32[]{:S(2)}, u32[]{:S(2)}) collective-permute-start(f32[2,8,128]{2,1,0:T(8,128)S(1)} %group_stats.1), channel_id=1, source_target_pairs={{0,8},{1,9},{2,10},{3,11},{4,12},{5,13},{6,14},{7,15},{8,0},{9,1},... | collective-permute-start | bytes 24584 | tf_op jit(solution)/shard_map/ppermute | solution.py:32
  13.1 0.0 copy-done.7
  13.1 0.9 slice_bitcast_fusion
  14.0 2.2 %collective-permute-start.3 = (bf16[4,32,1280]{2,1,0:T(8,128)(2,1)}, bf16[4,32,1280]{2,1,0:T(8,128)(2,1)S(1)}, u32[]{:S(2)}, u32[]{:S(2)}) collective-permute-start(bf16[4,32,1280]{2,1,0:T(8,128)(2,1)} %get-tuple-element.21), channel_id=1, source_target_pairs={{0,8},{1,9},{2,10},{3,11},{4,12},{5,13},{6,14},{7,15},{8,16},{9,17... | collective-permute-start | bytes 983048 | tf_op jit(solution)/shard_map/ppermute | solution.py:27
  16.3 0.0 copy-done.10
  16.3 0.0 copy-start.6
  16.3 0.0 copy-start.5
  16.3 0.2 convert_reduce_fusion
  16.5 0.0 collective-permute-done
  16.5 1.1 collective-permute-start.1
  17.6 0.2 multiply_cosine_fusion
  17.8 48.5 %collective-permute-done.1 = f32[2,8,128]{2,1,0:T(8,128)S(1)} collective-permute-done((f32[2,8,128]{2,1,0:T(8,128)S(1)}, f32[2,8,128]{2,1,0:T(8,128)S(1)}, u32[]{:S(2)}, u32[]{:S(2)}) %collective-permute-start.1) | collective-permute-done | bytes 8224 | tf_op jit(solution)/shard_map/ppermute | solution.py:32
  66.3 3.6 %collective-permute-start.2 = (f32[2,8,128]{2,1,0:T(8,128)S(1)}, f32[2,8,128]{2,1,0:T(8,128)S(1)}, u32[]{:S(2)}, u32[]{:S(2)}) collective-permute-start(f32[2,8,128]{2,1,0:T(8,128)S(1)} %pad_maximum_fusion.5), channel_id=1, source_target_pairs={{0,32},{1,33},{2,34},{3,35},{4,36},{5,37},{6,38},{7,39},{8,40},{9,... | collective-permute-start | bytes 24584 | tf_op jit(solution)/shard_map/ppermute | solution.py:32
  69.9 0.0 copy-done
  70.0 0.7 fusion.refs_3_
  70.7 0.0 copy-done.8
  70.7 0.0 copy-done.9
  70.7 0.8 collective-permute-done.2
  71.6 0.0 copy-done.6
  71.6 1.5 %collective-permute-start.4 = (bf16[4,32,1280]{2,1,0:T(8,128)(2,1)S(1)}, bf16[4,32,1280]{2,1,0:T(8,128)(2,1)S(1)}, u32[]{:S(2)}, u32[]{:S(2)}) collective-permute-start(bf16[4,32,1280]{2,1,0:T(8,128)(2,1)S(1)} %copy-done.6), channel_id=1, source_target_pairs={{8,0},{9,1},{10,2},{11,3},{12,4},{13,5},{14,6},{15,7},{16,8},{17,9... | collective-permute-start | bytes 983048 | tf_op jit(solution)/shard_map/ppermute | solution.py:27
  73.1 0.0 collective-permute-done.3.refs_5_
  73.1 10.0 %collective-permute-done.4.refs_6_ = bf16[4,32,1280]{2,1,0:T(8,128)(2,1)S(1)} collective-permute-done((bf16[4,32,1280]{2,1,0:T(8,128)(2,1)S(1)}, bf16[4,32,1280]{2,1,0:T(8,128)(2,1)S(1)}, u32[]{:S(2)}, u32[]{:S(2)}) %collective-permute-start.4) | collective-permute-done | bytes 327712 | tf_op jit(solution)/shard_map/ppermute | solution.py:27
  83.1 0.0 slice-start
  83.1 0.0 copy-done.5
  83.1 0.0 slice-start.1
  83.1 18.8 %conv_queries.1 = (bf16[4,128,1280]{2,1,0:T(8,128)(2,1)S(1)}, bf16[4,128,1280]{2,1,0:T(8,128)(2,1)S(1)}, bf16[4,128,640]{2,1,0:T(8,128)(2,1)S(1)}) custom-call(f32[2,8,128]{2,1,0:T(8,128)S(1)} %pad_maximum_fusion.6.refs_0_, f32[1,1280]{1,0:T(1,128)S(1)} %reshape.31.refs_1_, f32[1,1280]{1,0:T(1,128)S(1)} %reshape.32.refs_2_, f32[4,640]{1,0:T(4,128)S(1)} %fusion.refs_3_, ...), custom_call_target="tpu_custom_call" | custom-call | flops 8388608000 | bytes 22937600 | tf_op jit(solution)/shard_map/conv_queries/pallas_call | solution.py:204
  102.0 0.1 fusion.10
  102.0 1.2 collective-permute-start.10
  103.3 2.4 %collective-permute-start.8 = (bf16[2,128,640]{2,1,0:T(8,128)(2,1)S(1)}, bf16[2,128,640]{2,1,0:T(8,128)(2,1)S(1)}, u32[]{:S(2)}, u32[]{:S(2)}) collective-permute-start(bf16[2,128,640]{2,1,0:T(8,128)(2,1)S(1)} %get-tuple-element.22), channel_id=1, source_target_pairs={{0,8},{1,9},{2,10},{3,11},{4,12},{5,13},{6,14},{7,15},{8,0},{9,1},... | collective-permute-start | bytes 983048 | tf_op jit(solution)/shard_map/ppermute | solution.py:32
  105.7 0.0 slice-done
  105.7 0.0 slice-done.1
  105.7 3.6 %keys_values.1.first = bf16[2,4,128,640]{3,2,1,0:T(8,128)(2,1)} custom-call(bf16[4,128,1280]{2,1,0:T(8,128)(2,1)S(1)} %get-tuple-element.12.normal, bf16[1280,1920]{1,0:T(8,128)(2,1)S(1)} %bitcast.20), custom_call_target="tpu_custom_call" | custom-call | flops 1677721600 | bytes 5898240 | tf_op jit(solution)/shard_map/keys_values/pallas_call | solution.py:244
  109.2 5.1 %collective-permute-done.10.queries = bf16[2,128,640]{2,1,0:T(8,128)(2,1)S(1)} collective-permute-done((bf16[2,128,640]{2,1,0:T(8,128)(2,1)S(1)}, bf16[2,128,640]{2,1,0:T(8,128)(2,1)S(1)}, u32[]{:S(2)}, u32[]{:S(2)}) %collective-permute-start.10) | collective-permute-done | bytes 327712 | tf_op jit(solution)/shard_map/ppermute | solution.py:32
  114.3 0.0 collective-permute-done.5.second
  114.3 0.0 collective-permute-done.6.third
  114.3 0.0 collective-permute-done.7.fourth
  114.3 0.0 copy-done.1
  114.3 4.6 %attend.5 = (bf16[2,128,640]{2,1,0:T(8,128)(2,1)S(1)}, f32[2,16,128]{2,1,0:T(8,128)S(1)}) custom-call(bf16[2,128,640]{2,1,0:T(8,128)(2,1)S(1)} %collective-permute-done.10.queries, bf16[2,4,128,640]{3,2,1,0:T(8,128)(2,1)S(1)} %bitcast.17, bf16[2,4,128,640]{3,2,1,0:T(8,128)(2,1)S(1)} %collective-permute-done.5.second, ...), custom_call_target="tpu_custom_call" | custom-call | flops 1342177280 | bytes 3932160 | tf_op jit(solution)/shard_map/attend/pallas_call | solution.py:302
  118.9 0.6 collective-permute-start.11
  119.5 0.0 collective-permute-done.8.queries
  119.5 4.6 %attend.4 = (bf16[2,128,640]{2,1,0:T(8,128)(2,1)S(1)}, f32[2,16,128]{2,1,0:T(8,128)S(1)}) custom-call(bf16[2,128,640]{2,1,0:T(8,128)(2,1)S(1)} %collective-permute-done.8.queries, bf16[2,4,128,640]{3,2,1,0:T(8,128)(2,1)S(1)} %bitcast.18, bf16[2,4,128,640]{3,2,1,0:T(8,128)(2,1)S(1)} %collective-permute-done.5.second, ...), custom_call_target="tpu_custom_call" | custom-call | flops 1342177280 | bytes 3932160 | tf_op jit(solution)/shard_map/attend/pallas_call | solution.py:302
  124.0 3.1 %collective-permute-start.9 = (bf16[2,128,640]{2,1,0:T(8,128)(2,1)S(1)}, bf16[2,128,640]{2,1,0:T(8,128)(2,1)S(1)}, u32[]{:S(2)}, u32[]{:S(2)}) collective-permute-start(bf16[2,128,640]{2,1,0:T(8,128)(2,1)S(1)} %get-tuple-element.15), channel_id=1, source_target_pairs={{0,8},{1,9},{2,10},{3,11},{4,12},{5,13},{6,14},{7,15},{8,0},{9,1},... | collective-permute-start | bytes 983048 | tf_op jit(solution)/shard_map/ppermute | solution.py:32
  127.2 0.5 collective-permute-start.13
  127.6 3.0 %collective-permute-start.12 = (f32[2,16,128]{2,1,0:T(8,128)S(1)}, f32[2,16,128]{2,1,0:T(8,128)S(1)}, u32[]{:S(2)}, u32[]{:S(2)}) collective-permute-start(f32[2,16,128]{2,1,0:T(8,128)S(1)} %get-tuple-element.17), channel_id=1, source_target_pairs={{0,8},{1,9},{2,10},{3,11},{4,12},{5,13},{6,14},{7,15},{8,0},{9,1},... | collective-permute-start | bytes 49160 | tf_op jit(solution)/shard_map/ppermute | solution.py:32
  130.7 0.0 copy-done.3
  130.7 8.3 %attend.3 = (f32[4,128,640]{2,1,0:T(8,128)S(1)}, f32[4,16,128]{2,1,0:T(8,128)S(1)}) custom-call(bf16[4,128,640]{2,1,0:T(8,128)(2,1)S(1)} %get-tuple-element.11.queries, bf16[2,4,128,640]{3,2,1,0:T(8,128)(2,1)S(1)} %copy-done.3, bf16[2,4,128,640]{3,2,1,0:T(8,128)(2,1)S(1)} %collective-permute-done.5.second, ...), custom_call_target="tpu_custom_call" | custom-call | flops 2684354560 | bytes 7864320 | tf_op jit(solution)/shard_map/attend/pallas_call | solution.py:302
  139.0 0.0 collective-permute-done.13
  139.0 0.0 collective-permute-done.12
  139.0 0.0 collective-permute-done.11
  139.0 0.0 collective-permute-done.9
  139.0 0.1 pad_maximum_fusion.far
  139.1 0.0 copy-done.2
  139.1 3.5 %join_project.1 = bf16[4,128,1280]{2,1,0:T(8,128)(2,1)} custom-call(f32[4,128,640]{2,1,0:T(8,128)S(1)} %get-tuple-element.13.own, f32[4,16,128]{2,1,0:T(8,128)S(1)} %get-tuple-element.14.own_logs, bf16[4,128,640]{2,1,0:T(8,128)(2,1)S(1)} %pad_maximum_fusion.far, f32[4,16,128]{2,1,0:T(8,128)S(1)} %pad_maximum_fusion.1.far_logs, ...), custom_call_target="tpu_custom_call" | custom-call | flops 838860800 | bytes 6225920 | tf_op jit(solution)/shard_map/join_project/pallas_call | solution.py:363
  (14 shorter events, 0.1 us)
Async XLA Ops:
  0.6 69.3 %copy-start = (bf16[1280,640]{1,0:T(8,128)(2,1)S(1)}, bf16[1280,640]{1,0:T(8,128)(2,1)}, u32[]{:S(2)}) copy-start(bf16[1280,640]{1,0:T(8,128)(2,1)} %param.17) | copy-start | bytes 4915204
  0.6 113.6 %collective-permute-start.5 = (bf16[2,4,128,640]{3,2,1,0:T(8,128)(2,1)}, bf16[2,4,128,640]{3,2,1,0:T(8,128)(2,1)S(1)}, u32[]{:S(2)}, u32[]{:S(2)}) collective-permute-start(bf16[2,4,128,640]{3,2,1,0:T(8,128)(2,1)} %bitcast.14), channel_id=1, source_target_pairs={{0,16},{1,17},{2,18},{3,19},{4,20},{5,21},{6,22},{7,23},{8,24},{9,... | collective-permute-start | bytes 3932168 | tf_op jit(solution)/shard_map/ppermute | solution.py:21
  2.7 111.6 %collective-permute-start.6 = (bf16[2,4,128,640]{3,2,1,0:T(8,128)(2,1)}, bf16[2,4,128,640]{3,2,1,0:T(8,128)(2,1)}, u32[]{:S(2)}, u32[]{:S(2)}) collective-permute-start(bf16[2,4,128,640]{3,2,1,0:T(8,128)(2,1)} %bitcast.15), channel_id=1, source_target_pairs={{0,48},{1,49},{2,50},{3,51},{4,52},{5,53},{6,54},{7,55},{8,56},{9,... | collective-permute-start | bytes 3932168 | tf_op jit(solution)/shard_map/ppermute | solution.py:21
  4.9 109.4 %collective-permute-start.7 = (bf16[2,4,128,640]{3,2,1,0:T(8,128)(2,1)}, bf16[2,4,128,640]{3,2,1,0:T(8,128)(2,1)}, u32[]{:S(2)}, u32[]{:S(2)}) collective-permute-start(bf16[2,4,128,640]{3,2,1,0:T(8,128)(2,1)} %bitcast.16), channel_id=1, source_target_pairs={{0,32},{1,33},{2,34},{3,35},{4,36},{5,37},{6,38},{7,39},{8,40},{9,... | collective-permute-start | bytes 3932168 | tf_op jit(solution)/shard_map/ppermute | solution.py:21
  6.7 1.3 copy-start.4
  8.0 5.1 %copy-start.7 = (bf16[4,4,32,1280]{3,2,1,0:T(8,128)(2,1)S(1)}, bf16[4,4,32,1280]{3,2,1,0:T(8,128)(2,1)}, u32[]{:S(2)}) copy-start(bf16[4,4,32,1280]{3,2,1,0:T(8,128)(2,1)} %param.11) | copy-start | bytes 3932164
  8.0 8.3 %copy-start.10 = (s32[4,8]{1,0:T(4,128)S(1)}, s32[4,8]{1,0:T(4,128)}, u32[]{:S(2)}) copy-start(s32[4,8]{1,0:T(4,128)} %param.13) | copy-start | bytes 388
  9.8 60.8 %copy-start.8 = (f32[1280]{0:T(1024)S(1)}, f32[1280]{0:T(1024)}, u32[]{:S(2)}) copy-start(f32[1280]{0:T(1024)} %param.14) | copy-start | bytes 15364
  9.8 60.9 %copy-start.9 = (f32[1280]{0:T(1024)S(1)}, f32[1280]{0:T(1024)}, u32[]{:S(2)}) copy-start(f32[1280]{0:T(1024)} %param.15) | copy-start | bytes 15364
  9.9 6.7 %collective-permute-start = (f32[2,8,128]{2,1,0:T(8,128)S(1)}, f32[2,8,128]{2,1,0:T(8,128)S(1)}, u32[]{:S(2)}, u32[]{:S(2)}) collective-permute-start(f32[2,8,128]{2,1,0:T(8,128)S(1)} %group_stats.1), channel_id=1, source_target_pairs={{0,8},{1,9},{2,10},{3,11},{4,12},{5,13},{6,14},{7,15},{8,0},{9,1},... | collective-permute-start | bytes 24584 | tf_op jit(solution)/shard_map/ppermute | solution.py:32
  14.0 59.1 %collective-permute-start.3 = (bf16[4,32,1280]{2,1,0:T(8,128)(2,1)}, bf16[4,32,1280]{2,1,0:T(8,128)(2,1)S(1)}, u32[]{:S(2)}, u32[]{:S(2)}) collective-permute-start(bf16[4,32,1280]{2,1,0:T(8,128)(2,1)} %get-tuple-element.21), channel_id=1, source_target_pairs={{0,8},{1,9},{2,10},{3,11},{4,12},{5,13},{6,14},{7,15},{8,16},{9,17... | collective-permute-start | bytes 983048 | tf_op jit(solution)/shard_map/ppermute | solution.py:27
  16.3 55.3 %copy-start.6 = (bf16[4,32,1280]{2,1,0:T(8,128)(2,1)S(1)}, bf16[4,32,1280]{2,1,0:T(8,128)(2,1)}, u32[]{:S(2)}) copy-start(bf16[4,32,1280]{2,1,0:T(8,128)(2,1)} %get-tuple-element.20) | copy-start | bytes 983044
  16.3 66.8 %copy-start.5 = (bf16[4,4,32,1280]{3,2,1,0:T(8,128)(2,1)S(1)}, bf16[4,4,32,1280]{3,2,1,0:T(8,128)(2,1)}, u32[]{:S(2)}) copy-start(bf16[4,4,32,1280]{3,2,1,0:T(8,128)(2,1)} %param.10) | copy-start | bytes 3932164
  16.5 49.8 %collective-permute-start.1 = (f32[2,8,128]{2,1,0:T(8,128)S(1)}, f32[2,8,128]{2,1,0:T(8,128)S(1)}, u32[]{:S(2)}, u32[]{:S(2)}) collective-permute-start(f32[2,8,128]{2,1,0:T(8,128)S(1)} %pad_maximum_fusion.4), channel_id=1, source_target_pairs={{0,16},{1,17},{2,18},{3,19},{4,20},{5,21},{6,22},{7,23},{8,24},{9,... | collective-permute-start | bytes 24584 | tf_op jit(solution)/shard_map/ppermute | solution.py:32
  66.3 5.3 %collective-permute-start.2 = (f32[2,8,128]{2,1,0:T(8,128)S(1)}, f32[2,8,128]{2,1,0:T(8,128)S(1)}, u32[]{:S(2)}, u32[]{:S(2)}) collective-permute-start(f32[2,8,128]{2,1,0:T(8,128)S(1)} %pad_maximum_fusion.5), channel_id=1, source_target_pairs={{0,32},{1,33},{2,34},{3,35},{4,36},{5,37},{6,38},{7,39},{8,40},{9,... | collective-permute-start | bytes 24584 | tf_op jit(solution)/shard_map/ppermute | solution.py:32
  71.6 11.5 %collective-permute-start.4 = (bf16[4,32,1280]{2,1,0:T(8,128)(2,1)S(1)}, bf16[4,32,1280]{2,1,0:T(8,128)(2,1)S(1)}, u32[]{:S(2)}, u32[]{:S(2)}) collective-permute-start(bf16[4,32,1280]{2,1,0:T(8,128)(2,1)S(1)} %copy-done.6), channel_id=1, source_target_pairs={{8,0},{9,1},{10,2},{11,3},{12,4},{13,5},{14,6},{15,7},{16,8},{17,9... | collective-permute-start | bytes 983048 | tf_op jit(solution)/shard_map/ppermute | solution.py:27
  83.1 22.5 %slice-start = ((s8[4915200]{0:T(1024)(128)(4,1)}), s8[4194304]{0:T(1024)(128)(4,1)S(1)}, s32[]{:S(2)}) async-start(s8[4915200]{0:T(1024)(128)(4,1)} %bitcast.19), calls=%async_computation | async-start | bytes 8388608
  83.1 22.5 %slice-start.1 = ((s8[4915200]{0:T(1024)(128)(4,1)}), s8[720896]{0:T(1024)(128)(4,1)S(1)}, s32[]{:S(2)}) async-start(s8[4915200]{0:T(1024)(128)(4,1)} %bitcast.19), calls=%async_computation.1 | async-start | bytes 1441792
  102.0 12.2 %collective-permute-start.10 = (bf16[2,128,640]{2,1,0:T(8,128)(2,1)S(1)}, bf16[2,128,640]{2,1,0:T(8,128)(2,1)S(1)}, u32[]{:S(2)}, u32[]{:S(2)}) collective-permute-start(bf16[2,128,640]{2,1,0:T(8,128)(2,1)S(1)} %get-tuple-element.23), channel_id=1, source_target_pairs={{0,8},{1,9},{2,10},{3,11},{4,12},{5,13},{6,14},{7,15},{8,0},{9,1},... | collective-permute-start | bytes 983048 | tf_op jit(solution)/shard_map/ppermute | solution.py:32
  103.3 16.2 %collective-permute-start.8 = (bf16[2,128,640]{2,1,0:T(8,128)(2,1)S(1)}, bf16[2,128,640]{2,1,0:T(8,128)(2,1)S(1)}, u32[]{:S(2)}, u32[]{:S(2)}) collective-permute-start(bf16[2,128,640]{2,1,0:T(8,128)(2,1)S(1)} %get-tuple-element.22), channel_id=1, source_target_pairs={{0,8},{1,9},{2,10},{3,11},{4,12},{5,13},{6,14},{7,15},{8,0},{9,1},... | collective-permute-start | bytes 983048 | tf_op jit(solution)/shard_map/ppermute | solution.py:32
  105.7 8.6 %copy-start.1 = (bf16[2,4,4,32,640]{4,3,2,1,0:T(8,128)(2,1)S(1)}, bf16[2,4,4,32,640]{4,3,2,1,0:T(8,128)(2,1)}, u32[]{:S(2)}) copy-start(bf16[2,4,4,32,640]{4,3,2,1,0:T(8,128)(2,1)} %param.12) | copy-start | bytes 3932164
  118.9 11.8 %copy-start.3 = (bf16[2,4,128,640]{3,2,1,0:T(8,128)(2,1)S(1)}, bf16[2,4,128,640]{3,2,1,0:T(8,128)(2,1)}, u32[]{:S(2)}) copy-start(bf16[2,4,128,640]{3,2,1,0:T(8,128)(2,1)} %keys_values.1.first) | copy-start | bytes 3932164
  118.9 20.1 %collective-permute-start.11 = (bf16[2,128,640]{2,1,0:T(8,128)(2,1)S(1)}, bf16[2,128,640]{2,1,0:T(8,128)(2,1)S(1)}, u32[]{:S(2)}, u32[]{:S(2)}) collective-permute-start(bf16[2,128,640]{2,1,0:T(8,128)(2,1)S(1)} %get-tuple-element.16), channel_id=1, source_target_pairs={{0,8},{1,9},{2,10},{3,11},{4,12},{5,13},{6,14},{7,15},{8,0},{9,1},... | collective-permute-start | bytes 983048 | tf_op jit(solution)/shard_map/ppermute | solution.py:32
  124.0 15.0 %collective-permute-start.9 = (bf16[2,128,640]{2,1,0:T(8,128)(2,1)S(1)}, bf16[2,128,640]{2,1,0:T(8,128)(2,1)S(1)}, u32[]{:S(2)}, u32[]{:S(2)}) collective-permute-start(bf16[2,128,640]{2,1,0:T(8,128)(2,1)S(1)} %get-tuple-element.15), channel_id=1, source_target_pairs={{0,8},{1,9},{2,10},{3,11},{4,12},{5,13},{6,14},{7,15},{8,0},{9,1},... | collective-permute-start | bytes 983048 | tf_op jit(solution)/shard_map/ppermute | solution.py:32
  127.2 11.8 %collective-permute-start.13 = (f32[2,16,128]{2,1,0:T(8,128)S(1)}, f32[2,16,128]{2,1,0:T(8,128)S(1)}, u32[]{:S(2)}, u32[]{:S(2)}) collective-permute-start(f32[2,16,128]{2,1,0:T(8,128)S(1)} %get-tuple-element.18), channel_id=1, source_target_pairs={{0,8},{1,9},{2,10},{3,11},{4,12},{5,13},{6,14},{7,15},{8,0},{9,1},... | collective-permute-start | bytes 49160 | tf_op jit(solution)/shard_map/ppermute | solution.py:32
  127.6 11.4 %collective-permute-start.12 = (f32[2,16,128]{2,1,0:T(8,128)S(1)}, f32[2,16,128]{2,1,0:T(8,128)S(1)}, u32[]{:S(2)}, u32[]{:S(2)}) collective-permute-start(f32[2,16,128]{2,1,0:T(8,128)S(1)} %get-tuple-element.17), channel_id=1, source_target_pairs={{0,8},{1,9},{2,10},{3,11},{4,12},{5,13},{6,14},{7,15},{8,0},{9,1},... | collective-permute-start | bytes 49160 | tf_op jit(solution)/shard_map/ppermute | solution.py:32
  130.7 8.4 %copy-start.2 = (bf16[640,1280]{1,0:T(8,128)(2,1)S(1)}, bf16[640,1280]{1,0:T(8,128)(2,1)}, u32[]{:S(2)}) copy-start(bf16[640,1280]{1,0:T(8,128)(2,1)} %weight.3) | copy-start | bytes 4915204

commit v2 on v1

v2 whole, which is shorter than its diff:
```python
import math

import jax
import jax.numpy as jnp
from jax import lax
from jax.experimental import pallas as pl
from jax.experimental.pallas import tpu as pltpu
from jax.sharding import PartitionSpec as P

IMG_ROWS = 32
GROUPS = 32
HEADS = 10
TDIM = 1280
LANES = 128
SLOTS = 16
MIB = 1 << 20
STACK = 8


def rotated(value, by):
    count = lax.axis_size("band")
    return lax.ppermute(value, "band", [(i, (i + by) % count) for i in range(count)])


def flipped(value, bit):
    count = lax.axis_size("band")
    return lax.ppermute(value, "band", [(i, i ^ (bit * STACK)) for i in range(count)])


def time_term(timestep, time_weight):
    half_dim = TDIM // 2
    frequency = jnp.exp(-math.log(10000.0) * jnp.arange(half_dim, dtype=jnp.float32) / half_dim)
    angles = timestep.astype(jnp.float32)[:, None] * frequency[None, :]
    embedding = jnp.concatenate([jnp.cos(angles), jnp.sin(angles)], axis=1)
    return jnp.dot(
        jax.nn.silu(embedding), time_weight.astype(jnp.float32), precision=lax.Precision.HIGHEST
    )


def group_matrix(channels, per_group, transposed):
    shape = (LANES, channels) if transposed else (channels, LANES)
    channel = lax.broadcasted_iota(jnp.int32, shape, 1 if transposed else 0)
    first = lax.broadcasted_iota(jnp.int32, shape, 0 if transposed else 1) * per_group
    return jnp.where((channel >= first) & (channel < first + per_group), 1.0, 0.0)


def exact_dot(left, right):
    return jnp.dot(
        left, right, precision=lax.Precision.HIGHEST, preferred_element_type=jnp.float32
    )


def stats_kernel(latent_hbm, act_hbm, out, last_rows, first_rows, latent, rims, sums, sems):
    images, tokens, channels = latent.shape
    columns = last_rows.shape[1]
    per_group = channels // GROUPS
    copies = [
        pltpu.make_async_copy(latent_hbm.at[i], latent.at[i], sems.at[i]) for i in range(images)
    ]
    for copy in copies:
        copy.start()
    sides = (slice(tokens - columns, tokens), slice(0, columns))
    cuts = [
        pltpu.make_async_copy(act_hbm.at[:, side, :], rims.at[k], sems.at[images + k])
        for k, side in enumerate(sides)
    ]
    for cut in cuts:
        cut.start()
    passed = [
        pltpu.make_async_copy(rims.at[k], rows, sems.at[images + 2 + k])
        for k, rows in enumerate((last_rows, first_rows))
    ]
    gather = group_matrix(channels, per_group, False)
    spread = group_matrix(channels, per_group, True)
    sums[...] = jnp.zeros_like(sums)
    for i in range(images):
        copies[i].wait()
        sums[i : i + 1, :] = jnp.sum(latent[i].astype(jnp.float32), axis=0, keepdims=True)
    for cut, onward in zip(cuts, passed):
        cut.wait()
        onward.start()
    mean = exact_dot(sums[...], gather) * (1.0 / (tokens * per_group))
    center = exact_dot(mean, spread)
    for i in range(images):
        deviation = latent[i].astype(jnp.float32) - center[i : i + 1, :]
        sums[i : i + 1, :] = jnp.sum(deviation * deviation, axis=0, keepdims=True)
    out[0] = mean
    out[1] = exact_dot(sums[...], gather)
    for onward in passed:
        onward.wait()


def local_stats(latent, stale_act, columns):
    images, tokens, channels = latent.shape
    anywhere = pl.BlockSpec(memory_space=pltpu.HBM)
    vmem = pl.BlockSpec(memory_space=pltpu.VMEM)
    rim = jax.ShapeDtypeStruct((images, columns, channels), jnp.bfloat16)
    return pl.pallas_call(
        stats_kernel,
        out_shape=(jax.ShapeDtypeStruct((2, 8, LANES), jnp.float32), rim, rim),
        in_specs=[anywhere] * 2,
        out_specs=(vmem, anywhere, anywhere),
        scratch_shapes=[
            pltpu.VMEM(latent.shape, jnp.bfloat16),
            pltpu.VMEM((2,) + rim.shape, jnp.bfloat16),
            pltpu.VMEM((8, channels), jnp.float32),
            pltpu.SemaphoreType.DMA((images + 4,)),
        ],
        compiler_params=pltpu.CompilerParams(vmem_limit_bytes=60 * MIB),
        cost_estimate=pl.CostEstimate(
            flops=8 * latent.size, bytes_accessed=3 * latent.size, transcendentals=0
        ),
        name="group_stats",
    )(latent, stale_act)


def merged(own, other, count):
    gap = own[0] - other[0]
    return jnp.stack([(own[0] + other[0]) * 0.5, own[1] + other[1] + gap * gap * (count * 0.5)])


def conv_kernel(
    counted,
    inside,
    stats,
    gain,
    shift,
    bias,
    top,
    bottom,
    latent_hbm,
    conv_hbm,
    attn_hbm,
    hidden,
    normal,
    queries,
    latent,
    ext,
    weights,
    query_weight,
    acc,
    scales,
    sems,
):
    images, tokens, channels = latent.shape
    columns = top.shape[1]
    height = tokens // columns
    width = acc.shape[1]
    slab = images * columns
    inner = query_weight.shape[1]
    copies = [
        pltpu.make_async_copy(conv_hbm.at[dy], weights.at[dy], sems.at[dy]) for dy in range(3)
    ]
    copies.append(pltpu.make_async_copy(attn_hbm.at[:, :inner], query_weight, sems.at[3]))
    copies.append(pltpu.make_async_copy(latent_hbm, latent, sems.at[4]))
    for copy in copies[-1:] + copies[:-1]:
        copy.start()
    spread = group_matrix(channels, channels // GROUPS, True)
    scales[0] = exact_dot(stats[0], spread)
    inverse = 1.0 / jnp.sqrt(stats[1] * (1.0 / counted) + 1e-05)
    scales[1] = exact_dot(inverse, spread) * gain[...]
    place = lax.broadcasted_iota(jnp.int32, (columns, channels), 0)

    def put(value, row, i):
        rows = pl.ds(pl.multiple_of(row * slab + i * columns, columns), columns)
        before = jnp.where(place == 0, 0.0, pltpu.roll(value, 1, 0))
        after = jnp.where(place == columns - 1, 0.0, pltpu.roll(value, columns - 1, 0))
        ext[rows, 0:channels] = before.astype(jnp.bfloat16)
        ext[rows, channels : 2 * channels] = value.astype(jnp.bfloat16)
        ext[rows, 2 * channels : 3 * channels] = after.astype(jnp.bfloat16)

    def fill(i, carry):
        center = scales[0, pl.ds(i, 1), :]
        factor = scales[1, pl.ds(i, 1), :]
        put(top[i].astype(jnp.float32) * inside[0], 0, i)
        put(bottom[i].astype(jnp.float32) * inside[1], height + 1, i)
        for y in range(height):
            value = latent[i, y * columns : (y + 1) * columns, :].astype(jnp.float32)
            value = (value - center) * factor + shift[...]
            put(value / (1.0 + jnp.exp(-value)), y + 1, i)
        return carry

    copies[4].wait()
    lax.fori_loop(0, images, fill, 0)
    halves = 2
    part_rows = height // halves * slab

    def multiply(dy, m):
        first = dy * slab + m * part_rows
        return jnp.dot(
            ext[first : first + part_rows, :], weights[dy], preferred_element_type=jnp.float32
        )

    def finish(m):
        for y in range(m * height // halves, (m + 1) * height // halves):
            for i in range(images):
                tokens_of = slice(y * columns, (y + 1) * columns)
                rows = slice(y * slab + i * columns, y * slab + (i + 1) * columns)
                window = latent[i, tokens_of, :width].astype(jnp.float32) + acc[rows, :]
                window = (window + bias[i : i + 1, :]).astype(jnp.bfloat16)
                whole = jnp.concatenate([window, latent[i, tokens_of, width:]], axis=-1)
                hidden[i, tokens_of, :] = whole
                wide = whole.astype(jnp.float32)
                wide = wide - jnp.sum(wide, axis=-1, keepdims=True) * (1.0 / channels)
                variance = jnp.sum(wide * wide, axis=-1, keepdims=True) * (1.0 / channels)
                normal[i, tokens_of, :] = (wide * (1.0 / jnp.sqrt(variance + 1e-05))).astype(
                    jnp.bfloat16
                )

    for dy in range(3):
        copies[dy].wait()
        for m in range(halves):
            rows = slice(m * part_rows, (m + 1) * part_rows)
            if dy == 0:
                acc[rows, :] = multiply(dy, m)
            else:
                acc[rows, :] += multiply(dy, m)
            if dy == 2:
                finish(m)
    copies[3].wait()
    found = jnp.dot(
        normal[...].reshape(images * tokens, channels),
        query_weight[...],
        preferred_element_type=jnp.float32,
    )
    found = found.astype(jnp.bfloat16) * jnp.bfloat16((inner // HEADS) ** -0.5)
    queries[...] = found.reshape(images, tokens, inner)


def convolve(inside, stats, gain, shift, bias, latent, top, bottom, conv_weight, attn_in, counted):
    images, tokens, channels = latent.shape
    columns = top.shape[1]
    width = conv_weight.shape[-1]
    inner = attn_in.shape[1] // 3
    slab = images * columns
    vmem = pl.BlockSpec(memory_space=pltpu.VMEM)
    anywhere = pl.BlockSpec(memory_space=pl.ANY)

    def body(*refs):
        conv_kernel(counted, *refs)

    return pl.pallas_call(
        body,
        out_shape=(
            jax.ShapeDtypeStruct(latent.shape, jnp.bfloat16),
            jax.ShapeDtypeStruct(latent.shape, jnp.bfloat16),
            jax.ShapeDtypeStruct((images, tokens, inner), jnp.bfloat16),
        ),
        in_specs=[pl.BlockSpec(memory_space=pltpu.SMEM)] + [vmem] * 6 + [anywhere] * 3,
        out_specs=(vmem,) * 3,
        scratch_shapes=[
            pltpu.VMEM(latent.shape, jnp.bfloat16),
            pltpu.VMEM(((tokens // columns + 2) * slab, 3 * channels), jnp.bfloat16),
            pltpu.VMEM((3, 3 * channels, width), jnp.bfloat16),
            pltpu.VMEM((channels, inner), jnp.bfloat16),
            pltpu.VMEM((images * tokens, width), jnp.float32),
            pltpu.VMEM((2, 8, channels), jnp.float32),
            pltpu.SemaphoreType.DMA((5,)),
        ],
        compiler_params=pltpu.CompilerParams(vmem_limit_bytes=48 * MIB),
        cost_estimate=pl.CostEstimate(
            flops=2 * images * tokens * channels * (9 * width + inner),
            bytes_accessed=2 * (conv_weight.size + channels * inner + 5 * latent.size),
            transcendentals=latent.size,
        ),
        name="conv_queries",
    )(inside, stats, gain, shift, bias, top, bottom, latent, conv_weight, attn_in)


def project_kernel(normal, weight, out):
    images, tokens, channels = normal.shape
    found = jnp.dot(
        normal[...].reshape(images * tokens, channels),
        weight[...],
        preferred_element_type=jnp.float32,
    )
    out[0] = found.astype(jnp.bfloat16).reshape(out.shape[1:])


def project(normal, attn_in):
    images, tokens, channels = normal.shape
    inner = attn_in.shape[1] // 3
    return pl.pallas_call(
        project_kernel,
        grid=(2,),
        out_shape=jax.ShapeDtypeStruct((2, images, tokens, inner), jnp.bfloat16),
        in_specs=[
            pl.BlockSpec(normal.shape, lambda j: (0, 0, 0)),
            pl.BlockSpec((channels, inner), lambda j: (0, j + 1)),
        ],
        out_specs=pl.BlockSpec((1, images, tokens, inner), lambda j: (j, 0, 0, 0)),
        compiler_params=pltpu.CompilerParams(vmem_limit_bytes=24 * MIB),
        cost_estimate=pl.CostEstimate(
            flops=4 * images * tokens * channels * inner,
            bytes_accessed=4 * (channels * inner + normal.size),
            transcendentals=0,
        ),
        name="keys_values",
    )(normal, attn_in)


def attend_kernel(queries, first, second, third, far_keys, far_values, out, *logs):
    tokens, inner = queries.shape[1:]
    size = inner // HEADS
    pair = 2 * size
    lane = lax.broadcasted_iota(jnp.int32, (tokens, pair), 1)
    low = lane < size
    sources = (first, second, third)
    found = jnp.zeros((tokens, LANES), jnp.float32)
    spot = lax.broadcasted_iota(jnp.int32, (tokens, LANES), 1)
    for p in range(HEADS // 2):
        lanes = slice(p * pair, (p + 1) * pair)
        query = queries[0, :, lanes]
        blank = jnp.zeros_like(query)
        both = jnp.concatenate(
            [jnp.where(low, query, blank), jnp.where(low, blank, query)], axis=0
        )
        keys = jnp.concatenate(
            [s[0, 0, :, lanes] for s in sources] + [far_keys[0, :, lanes]], axis=0
        )
        values = jnp.concatenate(
            [s[1, 0, :, lanes] for s in sources] + [far_values[0, :, lanes]], axis=0
        )
        scores = lax.dot_general(
            both, keys, (((1,), (1,)), ((), ())), preferred_element_type=jnp.float32
        )
        peak = jnp.max(scores, axis=-1, keepdims=True)
        exponent = jnp.exp(scores - peak)
        total = jnp.sum(exponent, axis=-1, keepdims=True)
        context = jnp.dot(
            exponent.astype(jnp.bfloat16), values, preferred_element_type=jnp.float32
        )
        context = context * (1.0 / total)
        out[0, :tokens, lanes] = jnp.where(low, context[:tokens], context[tokens:]).astype(out.dtype)
        level = peak + jnp.log(total)
        found = jnp.where(spot == 2 * p, level[:tokens], found)
        found = jnp.where(spot == 2 * p + 1, level[tokens:], found)
    level = jnp.transpose(found)[:SLOTS, :]
    if logs:
        logs[0][0] = level
        return
    for part in range(3):
        term = level.astype(jnp.bfloat16)
        out[0, tokens:, part * LANES : (part + 1) * LANES] = term
        level = level - term.astype(jnp.float32)
    out[0, tokens:, 3 * LANES :] = jnp.zeros((SLOTS, inner - 3 * LANES), out.dtype)


def attend(queries, first, second, third, far_keys, far_values, start, images, packed):
    tokens, inner = queries.shape[1:]
    kv_spec = pl.BlockSpec((2, 1, tokens, inner), lambda i: (0, i + start, 0, 0))
    elements = images * HEADS * tokens * 4 * tokens
    if packed:
        out_shape = (jax.ShapeDtypeStruct((images, tokens + SLOTS, inner), jnp.bfloat16),)
    else:
        out_shape = (
            jax.ShapeDtypeStruct((images, tokens, inner), jnp.float32),
            jax.ShapeDtypeStruct((images, SLOTS, tokens), jnp.float32),
        )
    return pl.pallas_call(
        attend_kernel,
        grid=(images,),
        out_shape=out_shape,
        in_specs=[pl.BlockSpec((1, tokens, inner), lambda i: (i + start, 0, 0))]
        + [kv_spec] * 3
        + [pl.BlockSpec((1, tokens, inner), lambda i: (i, 0, 0))] * 2,
        out_specs=tuple(
            pl.BlockSpec((1,) + o.shape[1:], lambda i: (i, 0, 0)) for o in out_shape
        ),
        compiler_params=pltpu.CompilerParams(vmem_limit_bytes=24 * MIB),
        cost_estimate=pl.CostEstimate(
            flops=4 * elements * 256,
            bytes_accessed=images * tokens * inner * 24,
            transcendentals=elements,
        ),
        name="attend",
    )(queries, first, second, third, far_keys, far_values)


def join_kernel(
    own_first,
    logs_first,
    own_second,
    logs_second,
    far_first,
    far_second,
    hidden,
    weight,
    out,
    attended,
):
    images, tokens = hidden.shape[:2]
    half, tokens, inner = own_first.shape
    size = inner // HEADS
    pair = 2 * size
    low = lax.broadcasted_iota(jnp.int32, (tokens, pair), 1) < size
    for i in range(images):
        own, logs, far = (
            (own_first, logs_first, far_first)
            if i < half
            else (own_second, logs_second, far_second)
        )
        j = i % half
        here = logs[j]
        there = sum(
            far[j, tokens:, part * LANES : (part + 1) * LANES].astype(jnp.float32)
            for part in range(3)
        )
        top = jnp.maximum(here, there)
        here, there = jnp.exp(here - top), jnp.exp(there - top)
        share = there * (1.0 / (here + there))
        share = jnp.concatenate(
            [share, jnp.zeros((LANES - share.shape[0], tokens), jnp.float32)], axis=0
        )
        share = jnp.transpose(share)
        for p in range(HEADS // 2):
            lanes = slice(p * pair, (p + 1) * pair)
            part = jnp.where(
                low,
                jnp.broadcast_to(share[:, 2 * p : 2 * p + 1], (tokens, pair)),
                jnp.broadcast_to(share[:, 2 * p + 1 : 2 * p + 2], (tokens, pair)),
            )
            mine = own[j, :, lanes].astype(jnp.float32)
            theirs = far[j, :tokens, lanes].astype(jnp.float32)
            attended[i * tokens : (i + 1) * tokens, lanes] = (
                mine * (1.0 - part) + theirs * part
            ).astype(jnp.bfloat16)
    for i in range(images):
        rows = attended[i * tokens : (i + 1) * tokens, :]
        update = jnp.dot(rows, weight[...], preferred_element_type=jnp.float32)
        out[i] = (hidden[i].astype(jnp.float32) + update).astype(jnp.bfloat16)


def join(own, far, hidden, attn_out):
    images, tokens, channels = hidden.shape
    inner = attn_out.shape[0]
    return pl.pallas_call(
        join_kernel,
        out_shape=jax.ShapeDtypeStruct(hidden.shape, jnp.bfloat16),
        in_specs=[pl.BlockSpec(memory_space=pltpu.VMEM)] * 8,
        out_specs=pl.BlockSpec(memory_space=pltpu.VMEM),
        scratch_shapes=[pltpu.VMEM((images * tokens, inner), jnp.bfloat16)],
        compiler_params=pltpu.CompilerParams(vmem_limit_bytes=24 * MIB),
        cost_estimate=pl.CostEstimate(
            flops=2 * images * tokens * inner * channels,
            bytes_accessed=2 * attn_out.size + 4 * hidden.size + 6 * images * tokens * inner,
            transcendentals=0,
        ),
        name="join_project",
    )(*own[0], *own[1], far[0], far[1], hidden, attn_out)


def on_device(
    latent,
    stale_act,
    stale_kv,
    timestep,
    norm_gain,
    norm_shift,
    conv_weight,
    time_weight,
    attn_in,
    attn_out,
):
    images, height, columns, channels = latent.shape
    width = conv_weight.shape[3]
    inner = attn_out.shape[0]
    tokens = height * columns
    per_group = channels // GROUPS
    out_shape = latent.shape
    kv_shape = stale_kv.shape
    slot = lax.axis_index("band") % STACK
    latent = latent.reshape(images, tokens, channels)
    stale_kv = stale_kv.reshape(2, images, tokens, inner)

    stale_act = stale_act.reshape(images, tokens, channels)
    stats, last_rows, first_rows = local_stats(latent, stale_act, columns)
    top = rotated(last_rows, STACK)
    bottom = rotated(first_rows, -STACK)
    place = lax.axis_index("band") // STACK
    inside = jnp.stack([place > 0, place < IMG_ROWS // height - 1]).astype(jnp.float32)
    count = tokens * per_group
    for bit in (2, 4):
        stats = merged(stats, flipped(stats, bit), count)
        count *= 2
    stats, stale_kv = lax.optimization_barrier((stats, stale_kv))
    kv_up = rotated(stale_kv, 2 * STACK)
    kv_down = rotated(stale_kv, -2 * STACK)
    stats = merged(stats, flipped(stats, 1), count)
    count *= 2

    own_steps = lax.dynamic_index_in_dim(timestep, slot, 1, keepdims=False)
    bias = time_term(own_steps, time_weight)
    hidden, normal, queries = convolve(
        inside,
        stats,
        norm_gain.reshape(1, channels),
        norm_shift.reshape(1, channels),
        bias,
        latent,
        top,
        bottom,
        conv_weight.reshape(3, 3 * channels, width),
        attn_in,
        float(count),
    )
    half = images // 2
    far_queries = flipped(queries, 1)
    fresh_kv = project(normal, attn_in)
    kv_up, kv_down, fresh_kv = lax.optimization_barrier((kv_up, kv_down, fresh_kv))
    k_far = [rotated(kv_up[0, k * half : (k + 1) * half], 2 * STACK) for k in range(2)]
    v_far = [rotated(kv_down[1, k * half : (k + 1) * half], -2 * STACK) for k in range(2)]
    far = []
    for k in range(2):
        packed = attend(
            far_queries, stale_kv, kv_up, kv_down, k_far[k], v_far[k], k * half, half, True
        )[0]
        far.append(flipped(packed, 1))
    own = [
        attend(
            queries, fresh_kv, kv_up, kv_down, k_far[k], v_far[k], k * half, half, False
        )
        for k in range(2)
    ]
    block_out = join(own, far, hidden, attn_out)
    return (block_out.reshape(out_shape), fresh_kv.reshape(kv_shape))


def solution(mesh):
    return jax.shard_map(
        on_device,
        mesh=mesh,
        in_specs=(
            P("img", "band", None, None),
            P("img", "band", None, None),
            P(None, "img", "band", None, None),
            P("img", None),
            P(),
            P(),
            P(),
            P(),
            P(),
            P(),
        ),
        out_specs=(P("img", "band", None, None), P(None, "img", "band", None, None)),
        check_vma=False,
    )
```

time: 143 us -> 88.7 us (0.62)
  waiting for transfers between devices: 64.5 us -> 16.2 us
  Pallas kernels: 45.2 us -> 40.9 us
  starting transfers between devices: 28.6 us -> 26.8 us
    ppermute x9 -> x6, waiting for transfers between devices: 54.4 us -> 12.2 us  [flipped(): lax.ppermute(value, 'band', [(i, i ^ bit * STACK) for i in range(count)])]
    ppermute x2 -> x0, waiting for transfers between devices: 10 us -> none  [shifted(): return lax.ppermute(value, 'band', pairs)]
    ppermute x3 -> x8, starting transfers between devices: 6.05 us -> 14.3 us  [rotated(): lax.ppermute(value, 'band', [(i, (i + by) % count) for i in range(count)])]
    ppermute x9 -> x6, starting transfers between devices: 18.8 us -> 12.5 us  [flipped(): lax.ppermute(value, 'band', [(i, i ^ bit * STACK) for i in range(count)])]
    ppermute x3 -> x8, waiting for transfers between devices: 0.01 us -> 4.02 us  [rotated(): lax.ppermute(value, 'band', [(i, (i + by) % count) for i in range(count)])]
    ppermute x2 -> x0, starting transfers between devices: 3.71 us -> none  [shifted(): return lax.ppermute(value, 'band', pairs)]
    pallas_call x1, Pallas kernels: 18.8 us -> 16 us  [convolve(): pl.pallas_call(body, out_shape=(jax.ShapeDtypeStruct(latent.shape, jnp.bf...]
    pallas_call x5 -> x6, Pallas kernels: 22.7 us -> 21.3 us  [the longest x4 14.6 us: attend(): pl.pallas_call(attend_kernel, grid=(images,), out_shape=out_shape, in_spe...]
  transfers between devices with their start and end apart: 14 -> 14, of which waited for: 4 -> 7; matrix products, arithmetic and copies ran while one was open for 1% -> 2% of each run, Pallas kernels for 29% -> 39%
where the time goes in v2:
time: 88.7 us; the launch traced here: 88.3 us
  Pallas kernels  40.9 us (46%)
  starting transfers between devices  26.8 us (30%)
  waiting for transfers between devices  16.2 us (18%)
  local copies, waits for them, and re-layouts  1.64 us (2%)
  other arithmetic  1.15 us (1%)
    pallas_call x1, Pallas kernels, convolve(): pl.pallas_call(body, out_shape=(jax.ShapeDtypeStruct(latent.shape, jnp.bf...  16 us
    pallas_call x4, Pallas kernels, attend(): pl.pallas_call(attend_kernel, grid=(images,), out_shape=out_shape, in_spe...  14.6 us
    ppermute x8, starting transfers between devices, rotated(): lax.ppermute(value, 'band', [(i, (i + by) % count) for i in range(count)])  14.3 us
    ppermute x6, starting transfers between devices, flipped(): lax.ppermute(value, 'band', [(i, i ^ bit * STACK) for i in range(count)])  12.5 us
    ppermute x6, waiting for transfers between devices, flipped(): lax.ppermute(value, 'band', [(i, i ^ bit * STACK) for i in range(count)])  12.2 us
    ppermute x8, waiting for transfers between devices, rotated(): lax.ppermute(value, 'band', [(i, (i + by) % count) for i in range(count)])  4.02 us
    pallas_call x1, Pallas kernels, local_stats(): pl.pallas_call(stats_kernel, out_shape=(jax.ShapeDtypeStruct((2, 8, LANES...  3.7 us
    pallas_call x1, Pallas kernels, project(): pl.pallas_call(project_kernel, grid=(2,), out_shape=jax.ShapeDtypeStruct(...  3.55 us
  transfers between devices with their start and end apart: 14, of which 7 were waited for; matrix products, arithmetic and copies ran while one was open for 2% of the time, Pallas kernels for 39%

profile of v2, /device:TPU:0, one launch (start us, length us, event | category | flops | bytes accessed | tf_op | source)
XLA Modules:
  0.0 88.3 jit_solution(11408780064993750486)
XLA Ops:
  0.6 0.0 copy-start
  0.6 0.0 copy-start.7
  0.7 3.7 %group_stats.1 = (f32[2,8,128]{2,1,0:T(8,128)}, bf16[4,32,1280]{2,1,0:T(8,128)(2,1)}, bf16[4,32,1280]{2,1,0:T(8,128)(2,1)}) custom-call(bf16[4,128,1280]{2,1,0:T(8,128)(2,1)} %bitcast.24, bf16[4,128,1280]{2,1,0:T(8,128)(2,1)} %bitcast.26), custom_call_target="tpu_custom_call" | custom-call | flops 5242880 | bytes 1966080 | tf_op jit(solution)/shard_map/group_stats/pallas_call | solution.py:98
  4.4 0.0 copy-start.2
  4.4 0.0 copy-start.5
  4.4 0.0 copy-start.6
  4.4 2.1 %collective-permute-start = (f32[2,8,128]{2,1,0:T(8,128)}, f32[2,8,128]{2,1,0:T(8,128)S(1)}, u32[]{:S(2)}, u32[]{:S(2)}) collective-permute-start(f32[2,8,128]{2,1,0:T(8,128)} %get-tuple-element.17), channel_id=1, source_target_pairs={{0,16},{1,17},{2,18},{3,19},{4,20},{5,21},{6,22},{7,23},{8,24},{9,... | collective-permute-start | bytes 24584 | tf_op jit(solution)/shard_map/ppermute | solution.py:27
  6.5 3.2 %collective-permute-start.3 = (bf16[4,32,1280]{2,1,0:T(8,128)(2,1)}, bf16[4,32,1280]{2,1,0:T(8,128)(2,1)S(1)}, u32[]{:S(2)}, u32[]{:S(2)}) collective-permute-start(bf16[4,32,1280]{2,1,0:T(8,128)(2,1)} %get-tuple-element.19), channel_id=1, source_target_pairs={{0,8},{1,9},{2,10},{3,11},{4,12},{5,13},{6,14},{7,15},{8,16},{9,17... | collective-permute-start | bytes 983048 | tf_op jit(solution)/shard_map/ppermute | solution.py:22
  9.7 2.4 %collective-permute-start.4 = (bf16[4,32,1280]{2,1,0:T(8,128)(2,1)}, bf16[4,32,1280]{2,1,0:T(8,128)(2,1)}, u32[]{:S(2)}, u32[]{:S(2)}) collective-permute-start(bf16[4,32,1280]{2,1,0:T(8,128)(2,1)} %get-tuple-element.20), channel_id=1, source_target_pairs={{0,56},{1,57},{2,58},{3,59},{4,60},{5,61},{6,62},{7,63},{8,0},{9,1... | collective-permute-start | bytes 983048 | tf_op jit(solution)/shard_map/ppermute | solution.py:22
  12.1 0.0 copy-done.7
  12.1 0.2 convert_reduce_fusion
  12.3 0.2 multiply_cosine_fusion
  12.5 0.0 collective-permute-done
  12.5 0.7 add_multiply_fusion.2
  13.2 2.4 %collective-permute-start.1 = (f32[2,8,128]{2,1,0:T(8,128)S(1)}, f32[2,8,128]{2,1,0:T(8,128)S(1)}, u32[]{:S(2)}, u32[]{:S(2)}) collective-permute-start(f32[2,8,128]{2,1,0:T(8,128)S(1)} %pad_maximum_fusion.2), channel_id=1, source_target_pairs={{0,32},{1,33},{2,34},{3,35},{4,36},{5,37},{6,38},{7,39},{8,40},{9,... | collective-permute-start | bytes 24584 | tf_op jit(solution)/shard_map/ppermute | solution.py:27
  15.6 0.0 copy-done
  15.6 0.7 fusion.refs_4_
  16.3 3.0 %collective-permute-done.1 = f32[2,8,128]{2,1,0:T(8,128)S(1)} collective-permute-done((f32[2,8,128]{2,1,0:T(8,128)S(1)}, f32[2,8,128]{2,1,0:T(8,128)S(1)}, u32[]{:S(2)}, u32[]{:S(2)}) %collective-permute-start.1) | collective-permute-done | bytes 8224 | tf_op jit(solution)/shard_map/ppermute | solution.py:27
  19.3 0.0 copy-done.2
  19.4 0.4 collective-permute-start.6
  19.8 1.7 %collective-permute-start.5 = (bf16[2,4,128,640]{3,2,1,0:T(8,128)(2,1)S(1)}, bf16[2,4,128,640]{3,2,1,0:T(8,128)(2,1)S(1)}, u32[]{:S(2)}, u32[]{:S(2)}) collective-permute-start(bf16[2,4,128,640]{3,2,1,0:T(8,128)(2,1)S(1)} %bitcast.19), channel_id=1, source_target_pairs={{0,16},{1,17},{2,18},{3,19},{4,20},{5,21},{6,22},{7,23},{8,24},{9,... | collective-permute-start | bytes 3932168 | tf_op jit(solution)/shard_map/ppermute | solution.py:22
  21.4 0.7 collective-permute-start.2
  22.1 0.1 add_convert_fusion.refs_0_
  22.2 0.0 copy-done.5
  22.2 0.0 copy-done.6
  22.2 4.4 %collective-permute-done.2 = f32[2,8,128]{2,1,0:T(8,128)S(1)} collective-permute-done((f32[2,8,128]{2,1,0:T(8,128)S(1)}, f32[2,8,128]{2,1,0:T(8,128)S(1)}, u32[]{:S(2)}, u32[]{:S(2)}) %collective-permute-start.2) | collective-permute-done | bytes 8224 | tf_op jit(solution)/shard_map/ppermute | solution.py:27
  26.6 0.0 collective-permute-done.3.refs_5_
  26.6 0.0 collective-permute-done.4.refs_6_
  26.6 0.0 slice-start
  26.6 0.0 copy-start.4
  26.7 1.5 %copy-done.4 = bf16[4,4,32,1280]{3,2,1,0:T(8,128)(2,1)S(1)} copy-done((bf16[4,4,32,1280]{3,2,1,0:T(8,128)(2,1)S(1)}, bf16[4,4,32,1280]{3,2,1,0:T(8,128)(2,1)}, u32[]{:S(2)}) %copy-start.4) | copy-done | bytes 1310744
  28.1 0.0 slice-start.1
  28.1 16.0 %conv_queries.1 = (bf16[4,128,1280]{2,1,0:T(8,128)(2,1)S(1)}, bf16[4,128,1280]{2,1,0:T(8,128)(2,1)S(1)}, bf16[4,128,640]{2,1,0:T(8,128)(2,1)S(1)}) custom-call(f32[2]{0:T(128)S(1)} %add_convert_fusion.refs_0_, f32[2,8,128]{2,1,0:T(8,128)S(1)} %pad_maximum_fusion.4.refs_1_, f32[1,1280]{1,0:T(1,128)S(1)} %reshape.36.refs_2_, f32[1,1280]{1,0:T(1,128)S(1)} %reshape.37.refs_3_, ...), custom_call_target="tpu_custom_call" | custom-call | flops 8388608000 | bytes 22937600 | tf_op jit(solution)/shard_map/conv_queries/pallas_call | solution.py:242
  44.1 1.5 %collective-permute-start.11 = (bf16[4,128,640]{2,1,0:T(8,128)(2,1)S(1)}, bf16[4,128,640]{2,1,0:T(8,128)(2,1)S(1)}, u32[]{:S(2)}, u32[]{:S(2)}) collective-permute-start(bf16[4,128,640]{2,1,0:T(8,128)(2,1)S(1)} %get-tuple-element.21.queries), channel_id=1, source_target_pairs={{0,8},{1,9},{2,10},{3,11},{4,12},{5,13},{6,14},{7,15},{8,0},{9,1},... | collective-permute-start | bytes 1966088 | tf_op jit(solution)/shard_map/ppermute | solution.py:27
  45.6 0.0 slice-done
  45.6 0.0 slice-done.1
  45.6 3.5 %keys_values.1.first = bf16[2,4,128,640]{3,2,1,0:T(8,128)(2,1)} custom-call(bf16[4,128,1280]{2,1,0:T(8,128)(2,1)S(1)} %get-tuple-element.23.normal, bf16[1280,1920]{1,0:T(8,128)(2,1)S(1)} %bitcast.23), custom_call_target="tpu_custom_call" | custom-call | flops 1677721600 | bytes 5898240 | tf_op jit(solution)/shard_map/keys_values/pallas_call | solution.py:283
  49.2 0.0 collective-permute-done.6.third
  49.2 0.4 collective-permute-done.5.second
  49.6 0.1 slice_bitcast_fusion.1
  49.7 2.7 %collective-permute-start.7 = (bf16[2,128,640]{2,1,0:T(8,128)(2,1)S(1)}, bf16[2,128,640]{2,1,0:T(8,128)(2,1)S(1)}, u32[]{:S(2)}, u32[]{:S(2)}) collective-permute-start(bf16[2,128,640]{2,1,0:T(8,128)(2,1)S(1)} %get-tuple-element.35), channel_id=1, source_target_pairs={{0,16},{1,17},{2,18},{3,19},{4,20},{5,21},{6,22},{7,23},{8,24},{9,... | collective-permute-start | bytes 983048 | tf_op jit(solution)/shard_map/ppermute | solution.py:22
  52.4 0.1 slice_bitcast_fusion
  52.4 0.7 collective-permute-start.8
  53.1 1.4 %collective-permute-start.9 = (bf16[2,128,640]{2,1,0:T(8,128)(2,1)S(1)}, bf16[2,128,640]{2,1,0:T(8,128)(2,1)S(1)}, u32[]{:S(2)}, u32[]{:S(2)}) collective-permute-start(bf16[2,128,640]{2,1,0:T(8,128)(2,1)S(1)} %get-tuple-element.34), channel_id=1, source_target_pairs={{0,16},{1,17},{2,18},{3,19},{4,20},{5,21},{6,22},{7,23},{8,24},{9,... | collective-permute-start | bytes 983048 | tf_op jit(solution)/shard_map/ppermute | solution.py:22
  54.5 1.8 %collective-permute-start.10 = (bf16[2,128,640]{2,1,0:T(8,128)(2,1)S(1)}, bf16[2,128,640]{2,1,0:T(8,128)(2,1)S(1)}, u32[]{:S(2)}, u32[]{:S(2)}) collective-permute-start(bf16[2,128,640]{2,1,0:T(8,128)(2,1)S(1)} %get-tuple-element.32), channel_id=1, source_target_pairs={{0,48},{1,49},{2,50},{3,51},{4,52},{5,53},{6,54},{7,55},{8,56},{9,... | collective-permute-start | bytes 983048 | tf_op jit(solution)/shard_map/ppermute | solution.py:22
  56.4 3.2 %collective-permute-done.11.queries = bf16[4,128,640]{2,1,0:T(8,128)(2,1)S(1)} collective-permute-done((bf16[4,128,640]{2,1,0:T(8,128)(2,1)S(1)}, bf16[4,128,640]{2,1,0:T(8,128)(2,1)S(1)}, u32[]{:S(2)}, u32[]{:S(2)}) %collective-permute-start.11) | collective-permute-done | bytes 655392 | tf_op jit(solution)/shard_map/ppermute | solution.py:27
  59.6 2.0 %collective-permute-done.7.far_keys = bf16[2,128,640]{2,1,0:T(8,128)(2,1)S(1)} collective-permute-done((bf16[2,128,640]{2,1,0:T(8,128)(2,1)S(1)}, bf16[2,128,640]{2,1,0:T(8,128)(2,1)S(1)}, u32[]{:S(2)}, u32[]{:S(2)}) %collective-permute-start.7) | collective-permute-done | bytes 327712 | tf_op jit(solution)/shard_map/ppermute | solution.py:22
  61.6 1.5 %collective-permute-done.8.far_values = bf16[2,128,640]{2,1,0:T(8,128)(2,1)S(1)} collective-permute-done((bf16[2,128,640]{2,1,0:T(8,128)(2,1)S(1)}, bf16[2,128,640]{2,1,0:T(8,128)(2,1)S(1)}, u32[]{:S(2)}, u32[]{:S(2)}) %collective-permute-start.8) | collective-permute-done | bytes 327712 | tf_op jit(solution)/shard_map/ppermute | solution.py:22
  63.2 3.6 %attend.6 = bf16[2,144,640]{2,1,0:T(8,128)(2,1)S(1)} custom-call(bf16[4,128,640]{2,1,0:T(8,128)(2,1)S(1)} %collective-permute-done.11.queries, bf16[2,4,128,640]{3,2,1,0:T(8,128)(2,1)S(1)} %bitcast.20, bf16[2,4,128,640]{3,2,1,0:T(8,128)(2,1)S(1)} %collective-permute-done.5.second, bf16[2,4,128,640]{3,2,1,0:T(8,128)(2,1)S(1)} %collective-permute-done.6.third, ...), custom_call_target="tpu_custom_call" | custom-call | flops 1342177280 | bytes 3932160 | tf_op jit(solution)/shard_map/attend/pallas_call | solution.py:360
  66.8 0.0 copy-start.1
  66.8 5.0 %collective-permute-start.12 = (bf16[2,144,640]{2,1,0:T(8,128)(2,1)S(1)}, bf16[2,144,640]{2,1,0:T(8,128)(2,1)S(1)}, u32[]{:S(2)}, u32[]{:S(2)}) collective-permute-start(bf16[2,144,640]{2,1,0:T(8,128)(2,1)S(1)} %attend.6), channel_id=1, source_target_pairs={{0,8},{1,9},{2,10},{3,11},{4,12},{5,13},{6,14},{7,15},{8,0},{9,1},... | collective-permute-start | bytes 1105928 | tf_op jit(solution)/shard_map/ppermute | solution.py:27
  71.8 0.0 collective-permute-done.9.far_keys
  71.8 0.0 collective-permute-done.10.far_values
  71.8 3.6 %attend.7 = bf16[2,144,640]{2,1,0:T(8,128)(2,1)S(1)} custom-call(bf16[4,128,640]{2,1,0:T(8,128)(2,1)S(1)} %collective-permute-done.11.queries, bf16[2,4,128,640]{3,2,1,0:T(8,128)(2,1)S(1)} %bitcast.21, bf16[2,4,128,640]{3,2,1,0:T(8,128)(2,1)S(1)} %collective-permute-done.5.second, bf16[2,4,128,640]{3,2,1,0:T(8,128)(2,1)S(1)} %collective-permute-done.6.third, ...), custom_call_target="tpu_custom_call" | custom-call | flops 1342177280 | bytes 3932160 | tf_op jit(solution)/shard_map/attend/pallas_call | solution.py:360
  75.4 0.8 collective-permute-start.13
  76.3 0.0 copy-done.1
  76.3 3.7 %attend.4 = (f32[2,128,640]{2,1,0:T(8,128)S(1)}, f32[2,16,128]{2,1,0:T(8,128)S(1)}) custom-call(bf16[4,128,640]{2,1,0:T(8,128)(2,1)S(1)} %get-tuple-element.21.queries, bf16[2,4,128,640]{3,2,1,0:T(8,128)(2,1)S(1)} %copy-done.1, bf16[2,4,128,640]{3,2,1,0:T(8,128)(2,1)S(1)} %collective-permute-done.5.second, ...), custom_call_target="tpu_custom_call" | custom-call | flops 1342177280 | bytes 3932160 | tf_op jit(solution)/shard_map/attend/pallas_call | solution.py:360
  79.9 0.0 copy-start.3
  79.9 3.7 %attend.5 = (f32[2,128,640]{2,1,0:T(8,128)S(1)}, f32[2,16,128]{2,1,0:T(8,128)S(1)}) custom-call(bf16[4,128,640]{2,1,0:T(8,128)(2,1)S(1)} %get-tuple-element.21.queries, bf16[2,4,128,640]{3,2,1,0:T(8,128)(2,1)S(1)} %copy-done.1, bf16[2,4,128,640]{3,2,1,0:T(8,128)(2,1)S(1)} %collective-permute-done.5.second, ...), custom_call_target="tpu_custom_call" | custom-call | flops 1342177280 | bytes 3932160 | tf_op jit(solution)/shard_map/attend/pallas_call | solution.py:360
  83.6 0.0 collective-permute-done.12.far_first
  83.6 1.6 %collective-permute-done.13.far_second = bf16[2,144,640]{2,1,0:T(8,128)(2,1)S(1)} collective-permute-done((bf16[2,144,640]{2,1,0:T(8,128)(2,1)S(1)}, bf16[2,144,640]{2,1,0:T(8,128)(2,1)S(1)}, u32[]{:S(2)}, u32[]{:S(2)}) %collective-permute-start.13) | collective-permute-done | bytes 368672 | tf_op jit(solution)/shard_map/ppermute | solution.py:27
  85.2 0.0 copy-done.3
  85.2 3.1 %join_project.1 = bf16[4,128,1280]{2,1,0:T(8,128)(2,1)} custom-call(f32[2,128,640]{2,1,0:T(8,128)S(1)} %get-tuple-element.27.own_first, f32[2,16,128]{2,1,0:T(8,128)S(1)} %get-tuple-element.28.logs_first, f32[2,128,640]{2,1,0:T(8,128)S(1)} %get-tuple-element.29.own_second, f32[2,16,128]{2,1,0:T(8,128)S(1)} %get-tuple-element.30.logs_second, ...), custom_call_target="tpu_custom_call" | custom-call | flops 838860800 | bytes 6225920 | tf_op jit(solution)/shard_map/join_project/pallas_call | solution.py:437
  (9 shorter events, 0.0 us)
Async XLA Ops:
  0.6 14.9 %copy-start = (bf16[1280,640]{1,0:T(8,128)(2,1)S(1)}, bf16[1280,640]{1,0:T(8,128)(2,1)}, u32[]{:S(2)}) copy-start(bf16[1280,640]{1,0:T(8,128)(2,1)} %param.17) | copy-start | bytes 4915204
  0.6 11.5 %copy-start.7 = (s32[4,8]{1,0:T(4,128)S(1)}, s32[4,8]{1,0:T(4,128)}, u32[]{:S(2)}) copy-start(s32[4,8]{1,0:T(4,128)} %param.13) | copy-start | bytes 388
  4.4 15.0 %copy-start.2 = (bf16[2,4,4,32,640]{4,3,2,1,0:T(8,128)(2,1)S(1)}, bf16[2,4,4,32,640]{4,3,2,1,0:T(8,128)(2,1)}, u32[]{:S(2)}) copy-start(bf16[2,4,4,32,640]{4,3,2,1,0:T(8,128)(2,1)} %param.12) | copy-start | bytes 3932164
  4.4 17.8 %copy-start.5 = (f32[1280]{0:T(1024)S(1)}, f32[1280]{0:T(1024)}, u32[]{:S(2)}) copy-start(f32[1280]{0:T(1024)} %param.14) | copy-start | bytes 15364
  4.4 17.8 %copy-start.6 = (f32[1280]{0:T(1024)S(1)}, f32[1280]{0:T(1024)}, u32[]{:S(2)}) copy-start(f32[1280]{0:T(1024)} %param.15) | copy-start | bytes 15364
  4.4 8.1 %collective-permute-start = (f32[2,8,128]{2,1,0:T(8,128)}, f32[2,8,128]{2,1,0:T(8,128)S(1)}, u32[]{:S(2)}, u32[]{:S(2)}) collective-permute-start(f32[2,8,128]{2,1,0:T(8,128)} %get-tuple-element.17), channel_id=1, source_target_pairs={{0,16},{1,17},{2,18},{3,19},{4,20},{5,21},{6,22},{7,23},{8,24},{9,... | collective-permute-start | bytes 24584 | tf_op jit(solution)/shard_map/ppermute | solution.py:27
  6.5 20.1 %collective-permute-start.3 = (bf16[4,32,1280]{2,1,0:T(8,128)(2,1)}, bf16[4,32,1280]{2,1,0:T(8,128)(2,1)S(1)}, u32[]{:S(2)}, u32[]{:S(2)}) collective-permute-start(bf16[4,32,1280]{2,1,0:T(8,128)(2,1)} %get-tuple-element.19), channel_id=1, source_target_pairs={{0,8},{1,9},{2,10},{3,11},{4,12},{5,13},{6,14},{7,15},{8,16},{9,17... | collective-permute-start | bytes 983048 | tf_op jit(solution)/shard_map/ppermute | solution.py:22
  9.7 16.9 %collective-permute-start.4 = (bf16[4,32,1280]{2,1,0:T(8,128)(2,1)}, bf16[4,32,1280]{2,1,0:T(8,128)(2,1)}, u32[]{:S(2)}, u32[]{:S(2)}) collective-permute-start(bf16[4,32,1280]{2,1,0:T(8,128)(2,1)} %get-tuple-element.20), channel_id=1, source_target_pairs={{0,56},{1,57},{2,58},{3,59},{4,60},{5,61},{6,62},{7,63},{8,0},{9,1... | collective-permute-start | bytes 983048 | tf_op jit(solution)/shard_map/ppermute | solution.py:22
  13.2 6.1 %collective-permute-start.1 = (f32[2,8,128]{2,1,0:T(8,128)S(1)}, f32[2,8,128]{2,1,0:T(8,128)S(1)}, u32[]{:S(2)}, u32[]{:S(2)}) collective-permute-start(f32[2,8,128]{2,1,0:T(8,128)S(1)} %pad_maximum_fusion.2), channel_id=1, source_target_pairs={{0,32},{1,33},{2,34},{3,35},{4,36},{5,37},{6,38},{7,39},{8,40},{9,... | collective-permute-start | bytes 24584 | tf_op jit(solution)/shard_map/ppermute | solution.py:27
  19.4 29.8 %collective-permute-start.6 = (bf16[2,4,128,640]{3,2,1,0:T(8,128)(2,1)S(1)}, bf16[2,4,128,640]{3,2,1,0:T(8,128)(2,1)S(1)}, u32[]{:S(2)}, u32[]{:S(2)}) collective-permute-start(bf16[2,4,128,640]{3,2,1,0:T(8,128)(2,1)S(1)} %bitcast.18), channel_id=1, source_target_pairs={{0,48},{1,49},{2,50},{3,51},{4,52},{5,53},{6,54},{7,55},{8,56},{9,... | collective-permute-start | bytes 3932168 | tf_op jit(solution)/shard_map/ppermute | solution.py:22
  19.8 29.9 %collective-permute-start.5 = (bf16[2,4,128,640]{3,2,1,0:T(8,128)(2,1)S(1)}, bf16[2,4,128,640]{3,2,1,0:T(8,128)(2,1)S(1)}, u32[]{:S(2)}, u32[]{:S(2)}) collective-permute-start(bf16[2,4,128,640]{3,2,1,0:T(8,128)(2,1)S(1)} %bitcast.19), channel_id=1, source_target_pairs={{0,16},{1,17},{2,18},{3,19},{4,20},{5,21},{6,22},{7,23},{8,24},{9,... | collective-permute-start | bytes 3932168 | tf_op jit(solution)/shard_map/ppermute | solution.py:22
  21.4 5.2 %collective-permute-start.2 = (f32[2,8,128]{2,1,0:T(8,128)S(1)}, f32[2,8,128]{2,1,0:T(8,128)S(1)}, u32[]{:S(2)}, u32[]{:S(2)}) collective-permute-start(f32[2,8,128]{2,1,0:T(8,128)S(1)} %pad_maximum_fusion.3), channel_id=1, source_target_pairs={{0,8},{1,9},{2,10},{3,11},{4,12},{5,13},{6,14},{7,15},{8,0},{9,1},... | collective-permute-start | bytes 24584 | tf_op jit(solution)/shard_map/ppermute | solution.py:27
  26.6 19.0 %slice-start = ((s8[4915200]{0:T(1024)(128)(4,1)}), s8[4194304]{0:T(1024)(128)(4,1)S(1)}, s32[]{:S(2)}) async-start(s8[4915200]{0:T(1024)(128)(4,1)} %bitcast.22), calls=%async_computation | async-start | bytes 8388608
  26.6 1.5 %copy-start.4 = (bf16[4,4,32,1280]{3,2,1,0:T(8,128)(2,1)S(1)}, bf16[4,4,32,1280]{3,2,1,0:T(8,128)(2,1)}, u32[]{:S(2)}) copy-start(bf16[4,4,32,1280]{3,2,1,0:T(8,128)(2,1)} %param.10) | copy-start | bytes 3932164
  28.1 17.5 %slice-start.1 = ((s8[4915200]{0:T(1024)(128)(4,1)}), s8[720896]{0:T(1024)(128)(4,1)S(1)}, s32[]{:S(2)}) async-start(s8[4915200]{0:T(1024)(128)(4,1)} %bitcast.22), calls=%async_computation.1 | async-start | bytes 1441792
  44.1 15.4 %collective-permute-start.11 = (bf16[4,128,640]{2,1,0:T(8,128)(2,1)S(1)}, bf16[4,128,640]{2,1,0:T(8,128)(2,1)S(1)}, u32[]{:S(2)}, u32[]{:S(2)}) collective-permute-start(bf16[4,128,640]{2,1,0:T(8,128)(2,1)S(1)} %get-tuple-element.21.queries), channel_id=1, source_target_pairs={{0,8},{1,9},{2,10},{3,11},{4,12},{5,13},{6,14},{7,15},{8,0},{9,1},... | collective-permute-start | bytes 1966088 | tf_op jit(solution)/shard_map/ppermute | solution.py:27
  49.7 11.9 %collective-permute-start.7 = (bf16[2,128,640]{2,1,0:T(8,128)(2,1)S(1)}, bf16[2,128,640]{2,1,0:T(8,128)(2,1)S(1)}, u32[]{:S(2)}, u32[]{:S(2)}) collective-permute-start(bf16[2,128,640]{2,1,0:T(8,128)(2,1)S(1)} %get-tuple-element.35), channel_id=1, source_target_pairs={{0,16},{1,17},{2,18},{3,19},{4,20},{5,21},{6,22},{7,23},{8,24},{9,... | collective-permute-start | bytes 983048 | tf_op jit(solution)/shard_map/ppermute | solution.py:22
  52.4 10.7 %collective-permute-start.8 = (bf16[2,128,640]{2,1,0:T(8,128)(2,1)S(1)}, bf16[2,128,640]{2,1,0:T(8,128)(2,1)S(1)}, u32[]{:S(2)}, u32[]{:S(2)}) collective-permute-start(bf16[2,128,640]{2,1,0:T(8,128)(2,1)S(1)} %get-tuple-element.33), channel_id=1, source_target_pairs={{0,48},{1,49},{2,50},{3,51},{4,52},{5,53},{6,54},{7,55},{8,56},{9,... | collective-permute-start | bytes 983048 | tf_op jit(solution)/shard_map/ppermute | solution.py:22
  53.1 18.7 %collective-permute-start.9 = (bf16[2,128,640]{2,1,0:T(8,128)(2,1)S(1)}, bf16[2,128,640]{2,1,0:T(8,128)(2,1)S(1)}, u32[]{:S(2)}, u32[]{:S(2)}) collective-permute-start(bf16[2,128,640]{2,1,0:T(8,128)(2,1)S(1)} %get-tuple-element.34), channel_id=1, source_target_pairs={{0,16},{1,17},{2,18},{3,19},{4,20},{5,21},{6,22},{7,23},{8,24},{9,... | collective-permute-start | bytes 983048 | tf_op jit(solution)/shard_map/ppermute | solution.py:22
  54.5 17.3 %collective-permute-start.10 = (bf16[2,128,640]{2,1,0:T(8,128)(2,1)S(1)}, bf16[2,128,640]{2,1,0:T(8,128)(2,1)S(1)}, u32[]{:S(2)}, u32[]{:S(2)}) collective-permute-start(bf16[2,128,640]{2,1,0:T(8,128)(2,1)S(1)} %get-tuple-element.32), channel_id=1, source_target_pairs={{0,48},{1,49},{2,50},{3,51},{4,52},{5,53},{6,54},{7,55},{8,56},{9,... | collective-permute-start | bytes 983048 | tf_op jit(solution)/shard_map/ppermute | solution.py:22
  66.8 9.5 %copy-start.1 = (bf16[2,4,128,640]{3,2,1,0:T(8,128)(2,1)S(1)}, bf16[2,4,128,640]{3,2,1,0:T(8,128)(2,1)}, u32[]{:S(2)}) copy-start(bf16[2,4,128,640]{3,2,1,0:T(8,128)(2,1)} %keys_values.1.first) | copy-start | bytes 3932164
  66.8 16.8 %collective-permute-start.12 = (bf16[2,144,640]{2,1,0:T(8,128)(2,1)S(1)}, bf16[2,144,640]{2,1,0:T(8,128)(2,1)S(1)}, u32[]{:S(2)}, u32[]{:S(2)}) collective-permute-start(bf16[2,144,640]{2,1,0:T(8,128)(2,1)S(1)} %attend.6), channel_id=1, source_target_pairs={{0,8},{1,9},{2,10},{3,11},{4,12},{5,13},{6,14},{7,15},{8,0},{9,1},... | collective-permute-start | bytes 1105928 | tf_op jit(solution)/shard_map/ppermute | solution.py:27
  75.4 9.8 %collective-permute-start.13 = (bf16[2,144,640]{2,1,0:T(8,128)(2,1)S(1)}, bf16[2,144,640]{2,1,0:T(8,128)(2,1)S(1)}, u32[]{:S(2)}, u32[]{:S(2)}) collective-permute-start(bf16[2,144,640]{2,1,0:T(8,128)(2,1)S(1)} %attend.7), channel_id=1, source_target_pairs={{0,8},{1,9},{2,10},{3,11},{4,12},{5,13},{6,14},{7,15},{8,0},{9,1},... | collective-permute-start | bytes 1105928 | tf_op jit(solution)/shard_map/ppermute | solution.py:27
  79.9 5.3 %copy-start.3 = (bf16[640,1280]{1,0:T(8,128)(2,1)S(1)}, bf16[640,1280]{1,0:T(8,128)(2,1)}, u32[]{:S(2)}) copy-start(bf16[640,1280]{1,0:T(8,128)(2,1)} %weight.3) | copy-start | bytes 4915204

commit v3 on v2

--- a/solution.py
+++ b/solution.py
@@ -27,6 +27,13 @@
     return lax.ppermute(value, "band", [(i, i ^ (bit * STACK)) for i in range(count)])
 
 
+def outward(value):
+    count = lax.axis_size("band")
+    step = [-2 * STACK, 2 * STACK]
+    pairs = [(i, (i + step[i // STACK % 2]) % count) for i in range(count)]
+    return lax.ppermute(value, "band", pairs)
+
+
 def time_term(timestep, time_weight):
     half_dim = TDIM // 2
     frequency = jnp.exp(-math.log(10000.0) * jnp.arange(half_dim, dtype=jnp.float32) / half_dim)
@@ -41,25 +48,34 @@
     shape = (LANES, channels) if transposed else (channels, LANES)
     channel = lax.broadcasted_iota(jnp.int32, shape, 1 if transposed else 0)
     first = lax.broadcasted_iota(jnp.int32, shape, 0 if transposed else 1) * per_group
-    return jnp.where((channel >= first) & (channel < first + per_group), 1.0, 0.0)
+    inside = (channel >= first) & (channel < first + per_group)
+    return jnp.where(inside, 1.0, 0.0).astype(jnp.bfloat16)
 
 
 def exact_dot(left, right):
-    return jnp.dot(
-        left, right, precision=lax.Precision.HIGHEST, preferred_element_type=jnp.float32
-    )
-
-
-def stats_kernel(latent_hbm, act_hbm, out, last_rows, first_rows, latent, rims, sums, sems):
+    terms = []
+    for _ in range(3):
+        terms.append(left.astype(jnp.bfloat16).astype(jnp.float32))
+        left = left - terms[-1]
+    stacked = jnp.concatenate(terms, axis=0).astype(jnp.bfloat16)
+    found = jnp.dot(stacked, right, preferred_element_type=jnp.float32)
+    return found[0:8] + found[8:16] + found[16:24]
+
+
+def stats_kernel(spot, latent_hbm, act_hbm, out, near, away, latent, rims, sums, sems):
     images, tokens, channels = latent.shape
-    columns = last_rows.shape[1]
+    columns = near.shape[1]
     per_group = channels // GROUPS
     copies = [
         pltpu.make_async_copy(latent_hbm.at[i], latent.at[i], sems.at[i]) for i in range(images)
     ]
     for copy in copies:
         copy.start()
-    sides = (slice(tokens - columns, tokens), slice(0, columns))
+    start = spot[0] * (tokens - columns)
+    sides = [
+        pl.ds(pl.multiple_of(first, columns), columns)
+        for first in (tokens - columns - start, start)
+    ]
     cuts = [
         pltpu.make_async_copy(act_hbm.at[:, side, :], rims.at[k], sems.at[images + k])
         for k, side in enumerate(sides)
@@ -68,7 +84,7 @@
         cut.start()
     passed = [
         pltpu.make_async_copy(rims.at[k], rows, sems.at[images + 2 + k])
-        for k, rows in enumerate((last_rows, first_rows))
+        for k, rows in enumerate((near, away))
     ]
     gather = group_matrix(channels, per_group, False)
     spread = group_matrix(channels, per_group, True)
@@ -90,7 +106,7 @@
         onward.wait()
 
 
-def local_stats(latent, stale_act, columns):
+def local_stats(spot, latent, stale_act, columns):
     images, tokens, channels = latent.shape
     anywhere = pl.BlockSpec(memory_space=pltpu.HBM)
     vmem = pl.BlockSpec(memory_space=pltpu.VMEM)
@@ -98,7 +114,7 @@
     return pl.pallas_call(
         stats_kernel,
         out_shape=(jax.ShapeDtypeStruct((2, 8, LANES), jnp.float32), rim, rim),
-        in_specs=[anywhere] * 2,
+        in_specs=[pl.BlockSpec(memory_space=pltpu.SMEM)] + [anywhere] * 2,
         out_specs=(vmem, anywhere, anywhere),
         scratch_shapes=[
             pltpu.VMEM(latent.shape, jnp.bfloat16),
@@ -111,7 +127,7 @@
             flops=8 * latent.size, bytes_accessed=3 * latent.size, transcendentals=0
         ),
         name="group_stats",
-    )(latent, stale_act)
+    )(spot, latent, stale_act)
 
 
 def merged(own, other, count):
@@ -121,13 +137,13 @@
 
 def conv_kernel(
     counted,
-    inside,
+    spot,
     stats,
     gain,
     shift,
     bias,
-    top,
-    bottom,
+    near,
+    away,
     latent_hbm,
     conv_hbm,
     attn_hbm,
@@ -143,7 +159,7 @@
     sems,
 ):
     images, tokens, channels = latent.shape
-    columns = top.shape[1]
+    columns = near.shape[1]
     height = tokens // columns
     width = acc.shape[1]
     slab = images * columns
@@ -172,8 +188,10 @@
     def fill(i, carry):
         center = scales[0, pl.ds(i, 1), :]
         factor = scales[1, pl.ds(i, 1), :]
-        put(top[i].astype(jnp.float32) * inside[0], 0, i)
-        put(bottom[i].astype(jnp.float32) * inside[1], height + 1, i)
+        near_row = (1 - spot[0]) * (height + 1)
+        put(near[i].astype(jnp.float32), near_row, i)
+        inside = spot[1].astype(jnp.float32)
+        put(away[i].astype(jnp.float32) * inside, height + 1 - near_row, i)
         for y in range(height):
             value = latent[i, y * columns : (y + 1) * columns, :].astype(jnp.float32)
             value = (value - center) * factor + shift[...]
@@ -227,9 +245,9 @@
     queries[...] = found.reshape(images, tokens, inner)
 
 
-def convolve(inside, stats, gain, shift, bias, latent, top, bottom, conv_weight, attn_in, counted):
+def convolve(spot, stats, gain, shift, bias, latent, near, away, conv_weight, attn_in, counted):
     images, tokens, channels = latent.shape
-    columns = top.shape[1]
+    columns = near.shape[1]
     width = conv_weight.shape[-1]
     inner = attn_in.shape[1] // 3
     slab = images * columns
@@ -264,7 +282,7 @@
             transcendentals=latent.size,
         ),
         name="conv_queries",
-    )(inside, stats, gain, shift, bias, top, bottom, latent, conv_weight, attn_in)
+    )(spot, stats, gain, shift, bias, near, away, latent, conv_weight, attn_in)
 
 
 def project_kernel(normal, weight, out):
@@ -325,12 +343,14 @@
             both, keys, (((1,), (1,)), ((), ())), preferred_element_type=jnp.float32
         )
         peak = jnp.max(scores, axis=-1, keepdims=True)
-        exponent = jnp.exp(scores - peak)
-        total = jnp.sum(exponent, axis=-1, keepdims=True)
+        exponent = jnp.exp(scores - peak).astype(jnp.bfloat16)
         context = jnp.dot(
-            exponent.astype(jnp.bfloat16), values, preferred_element_type=jnp.float32
-        )
-        context = context * (1.0 / total)
+            exponent,
+            jnp.concatenate([values, jnp.ones_like(values)], axis=1),
+            preferred_element_type=jnp.float32,
+        )
+        total = context[:, pair:]
+        context = context[:, :pair] * (1.0 / total)
         out[0, :tokens, lanes] = jnp.where(low, context[:tokens], context[tokens:]).astype(out.dtype)
         level = peak + jnp.log(total)
         found = jnp.where(spot == 2 * p, level[:tokens], found)
@@ -377,33 +397,16 @@
     )(queries, first, second, third, far_keys, far_values)
 
 
-def join_kernel(
-    own_first,
-    logs_first,
-    own_second,
-    logs_second,
-    far_first,
-    far_second,
-    hidden,
-    weight,
-    out,
-    attended,
-):
-    images, tokens = hidden.shape[:2]
-    half, tokens, inner = own_first.shape
+def join_kernel(own, logs, far, hidden, weight, *rest):
+    out, attended = rest[-2:]
+    images, tokens, inner = own.shape
     size = inner // HEADS
     pair = 2 * size
     low = lax.broadcasted_iota(jnp.int32, (tokens, pair), 1) < size
     for i in range(images):
-        own, logs, far = (
-            (own_first, logs_first, far_first)
-            if i < half
-            else (own_second, logs_second, far_second)
-        )
-        j = i % half
-        here = logs[j]
+        here = logs[i]
         there = sum(
-            far[j, tokens:, part * LANES : (part + 1) * LANES].astype(jnp.float32)
+            far[i, tokens:, part * LANES : (part + 1) * LANES].astype(jnp.float32)
             for part in range(3)
         )
         top = jnp.maximum(here, there)
@@ -420,34 +423,41 @@
                 jnp.broadcast_to(share[:, 2 * p : 2 * p + 1], (tokens, pair)),
                 jnp.broadcast_to(share[:, 2 * p + 1 : 2 * p + 2], (tokens, pair)),
             )
-            mine = own[j, :, lanes].astype(jnp.float32)
-            theirs = far[j, :tokens, lanes].astype(jnp.float32)
+            mine = own[i, :, lanes].astype(jnp.float32)
+            theirs = far[i, :tokens, lanes].astype(jnp.float32)
             attended[i * tokens : (i + 1) * tokens, lanes] = (
                 mine * (1.0 - part) + theirs * part
             ).astype(jnp.bfloat16)
-    for i in range(images):
-        rows = attended[i * tokens : (i + 1) * tokens, :]
-        update = jnp.dot(rows, weight[...], preferred_element_type=jnp.float32)
-        out[i] = (hidden[i].astype(jnp.float32) + update).astype(jnp.bfloat16)
-
-
-def join(own, far, hidden, attn_out):
-    images, tokens, channels = hidden.shape
-    inner = attn_out.shape[0]
+    update = jnp.dot(attended[...], weight[...], preferred_element_type=jnp.float32)
+    out[...] = (hidden[...].astype(jnp.float32) + update.reshape(out.shape)).astype(jnp.bfloat16)
+
+
+def join(own, logs, far, hidden, attn_out, block, earlier):
+    images, tokens, inner = own.shape
+    channels = hidden.shape[-1]
+    part = pl.BlockSpec((images, tokens, channels), lambda i: (block, 0, 0))
+
+    def whole(array):
+        return pl.BlockSpec(array.shape, lambda i: (0,) * array.ndim)
+
+    extra = [] if earlier is None else [earlier]
     return pl.pallas_call(
         join_kernel,
+        grid=(1,),
         out_shape=jax.ShapeDtypeStruct(hidden.shape, jnp.bfloat16),
-        in_specs=[pl.BlockSpec(memory_space=pltpu.VMEM)] * 8,
-        out_specs=pl.BlockSpec(memory_space=pltpu.VMEM),
+        in_specs=[whole(own), whole(logs), whole(far), part, whole(attn_out)]
+        + [pl.BlockSpec(memory_space=pl.ANY) for _ in extra],
+        out_specs=part,
+        input_output_aliases={5: 0} if extra else {},
         scratch_shapes=[pltpu.VMEM((images * tokens, inner), jnp.bfloat16)],
         compiler_params=pltpu.CompilerParams(vmem_limit_bytes=24 * MIB),
         cost_estimate=pl.CostEstimate(
             flops=2 * images * tokens * inner * channels,
-            bytes_accessed=2 * attn_out.size + 4 * hidden.size + 6 * images * tokens * inner,
+            bytes_accessed=2 * attn_out.size + 10 * images * tokens * inner,
             transcendentals=0,
         ),
         name="join_project",
-    )(*own[0], *own[1], far[0], far[1], hidden, attn_out)
+    )(own, logs, far, hidden, attn_out, *extra)
 
 
 def on_device(
@@ -474,11 +484,13 @@
     stale_kv = stale_kv.reshape(2, images, tokens, inner)
 
     stale_act = stale_act.reshape(images, tokens, channels)
-    stats, last_rows, first_rows = local_stats(latent, stale_act, columns)
-    top = rotated(last_rows, STACK)
-    bottom = rotated(first_rows, -STACK)
     place = lax.axis_index("band") // STACK
-    inside = jnp.stack([place > 0, place < IMG_ROWS // height - 1]).astype(jnp.float32)
+    upper = place % 2
+    inside = (place > 0) & (place < IMG_ROWS // height - 1)
+    spot = jnp.stack([upper, inside.astype(jnp.int32)]).astype(jnp.int32)
+    stats, near, away = local_stats(spot, latent, stale_act, columns)
+    near = flipped(near, 1)
+    away = flipped(outward(away), 1)
     count = tokens * per_group
     for bit in (2, 4):
         stats = merged(stats, flipped(stats, bit), count)
@@ -486,20 +498,21 @@
     stats, stale_kv = lax.optimization_barrier((stats, stale_kv))
     kv_up = rotated(stale_kv, 2 * STACK)
     kv_down = rotated(stale_kv, -2 * STACK)
+    stats, near, away = lax.optimization_barrier((stats, near, away))
     stats = merged(stats, flipped(stats, 1), count)
     count *= 2
 
     own_steps = lax.dynamic_index_in_dim(timestep, slot, 1, keepdims=False)
     bias = time_term(own_steps, time_weight)
     hidden, normal, queries = convolve(
-        inside,
+        spot,
         stats,
         norm_gain.reshape(1, channels),
         norm_shift.reshape(1, channels),
         bias,
         latent,
-        top,
-        bottom,
+        near,
+        away,
         conv_weight.reshape(3, 3 * channels, width),
         attn_in,
         float(count),
@@ -522,7 +535,9 @@
         )
         for k in range(2)
     ]
-    block_out = join(own, far, hidden, attn_out)
+    block_out = None
+    for k in range(2):
+        block_out = join(*own[k], far[k], hidden, attn_out, k, block_out)
     return (block_out.reshape(out_shape), fresh_kv.reshape(kv_shape))
 
 

time: 88.7 us -> 85.4 us (0.963)
  Pallas kernels: 40.9 us -> 37 us
  waiting for transfers between devices: 16.2 us -> 18.3 us
  local copies, waits for them, and re-layouts: 1.64 us -> 0.19 us
    ppermute x8 -> x6, starting transfers between devices: 14.3 us -> 8.96 us  [rotated(): lax.ppermute(value, 'band', [(i, (i + by) % count) for i in range(count)])]
    ppermute x0 -> x1, waiting for transfers between devices: none -> 4.68 us  [outward(): return lax.ppermute(value, 'band', pairs)]
    pallas_call x4, Pallas kernels: 14.6 us -> 10.2 us  [attend(): pl.pallas_call(attend_kernel, grid=(images,), out_shape=out_shape, in_spe...]
    ppermute x0 -> x1, starting transfers between devices: none -> 2.52 us  [outward(): return lax.ppermute(value, 'band', pairs)]
    ppermute x6 -> x8, starting transfers between devices: 12.5 us -> 14.9 us  [flipped(): lax.ppermute(value, 'band', [(i, i ^ bit * STACK) for i in range(count)])]
    ppermute x8 -> x6, waiting for transfers between devices: 4.02 us -> 1.63 us  [rotated(): lax.ppermute(value, 'band', [(i, (i + by) % count) for i in range(count)])]
    unnamed x20 -> x22, local copies, waits for them, and re-layouts: 1.51 us -> 0.05 us
    pallas_call x1 -> x2, Pallas kernels: 3.07 us -> 4.36 us  [join(): pl.pallas_call(join_kernel, grid=(1,), out_shape=jax.ShapeDtypeStruct(hid...]
  transfers between devices with their start and end apart: 14 -> 15, of which waited for: 7 -> 6; matrix products, arithmetic and copies ran while one was open for 2% -> 2% of each run, Pallas kernels for 39% -> 36%
where the time goes in v3:
time: 85.4 us; the launch traced here: 85.2 us
  Pallas kernels  37 us (43%)
  starting transfers between devices  26.4 us (31%)
  waiting for transfers between devices  18.3 us (21%)
  other arithmetic  1.82 us (2%)
    pallas_call x1, Pallas kernels, convolve(): pl.pallas_call(body, out_shape=(jax.ShapeDtypeStruct(latent.shape, jnp.bf...  15 us
    ppermute x8, starting transfers between devices, flipped(): lax.ppermute(value, 'band', [(i, i ^ bit * STACK) for i in range(count)])  14.9 us
    ppermute x8, waiting for transfers between devices, flipped(): lax.ppermute(value, 'band', [(i, i ^ bit * STACK) for i in range(count)])  12 us
    pallas_call x4, Pallas kernels, attend(): pl.pallas_call(attend_kernel, grid=(images,), out_shape=out_shape, in_spe...  10.2 us
    ppermute x6, starting transfers between devices, rotated(): lax.ppermute(value, 'band', [(i, (i + by) % count) for i in range(count)])  8.96 us
    ppermute x1, waiting for transfers between devices, outward(): return lax.ppermute(value, 'band', pairs)  4.68 us
    pallas_call x2, Pallas kernels, join(): pl.pallas_call(join_kernel, grid=(1,), out_shape=jax.ShapeDtypeStruct(hid...  4.36 us
    pallas_call x1, Pallas kernels, local_stats(): pl.pallas_call(stats_kernel, out_shape=(jax.ShapeDtypeStruct((2, 8, LANES...  3.9 us
  transfers between devices with their start and end apart: 15, of which 6 were waited for; matrix products, arithmetic and copies ran while one was open for 2% of the time, Pallas kernels for 36%

profile of v3, /device:TPU:0, one launch (start us, length us, event | category | flops | bytes accessed | tf_op | source)
XLA Modules:
  0.0 85.2 jit_solution(13276740596399415078)
XLA Ops:
  0.6 0.0 copy-start
  0.7 0.6 pad_add_fusion.spot.refs_0_
  1.3 0.0 copy-start.8
  1.3 3.9 %group_stats.1 = (f32[2,8,128]{2,1,0:T(8,128)}, bf16[4,32,1280]{2,1,0:T(8,128)(2,1)}, bf16[4,32,1280]{2,1,0:T(8,128)(2,1)}) custom-call(s32[2]{0:T(128)} %pad_add_fusion.spot.refs_0_, bf16[4,128,1280]{2,1,0:T(8,128)(2,1)} %bitcast.24, bf16[4,128,1280]{2,1,0:T(8,128)(2,1)} %bitcast.27), custom_call_target="tpu_custom_call" | custom-call | flops 5242880 | bytes 1966080 | tf_op jit(solution)/shard_map/group_stats/pallas_call | solution.py:114
  5.2 0.0 copy-start.6
  5.3 0.0 copy-start.7
  5.3 0.0 copy-start.5
  5.3 2.1 %collective-permute-start = (f32[2,8,128]{2,1,0:T(8,128)}, f32[2,8,128]{2,1,0:T(8,128)S(1)}, u32[]{:S(2)}, u32[]{:S(2)}) collective-permute-start(f32[2,8,128]{2,1,0:T(8,128)} %get-tuple-element.20), channel_id=1, source_target_pairs={{0,16},{1,17},{2,18},{3,19},{4,20},{5,21},{6,22},{7,23},{8,24},{9,... | collective-permute-start | bytes 24584 | tf_op jit(solution)/shard_map/ppermute | solution.py:27
  7.4 3.2 %collective-permute-start.2 = (bf16[4,32,1280]{2,1,0:T(8,128)(2,1)}, bf16[4,32,1280]{2,1,0:T(8,128)(2,1)S(1)}, u32[]{:S(2)}, u32[]{:S(2)}) collective-permute-start(bf16[4,32,1280]{2,1,0:T(8,128)(2,1)} %get-tuple-element.22), channel_id=1, source_target_pairs={{0,8},{1,9},{2,10},{3,11},{4,12},{5,13},{6,14},{7,15},{8,0},{9,1},... | collective-permute-start | bytes 983048 | tf_op jit(solution)/shard_map/ppermute | solution.py:27
  10.6 2.5 %collective-permute-start.3 = (bf16[4,32,1280]{2,1,0:T(8,128)(2,1)}, bf16[4,32,1280]{2,1,0:T(8,128)(2,1)}, u32[]{:S(2)}, u32[]{:S(2)}) collective-permute-start(bf16[4,32,1280]{2,1,0:T(8,128)(2,1)} %get-tuple-element.23), channel_id=1, source_target_pairs={{0,48},{1,49},{2,50},{3,51},{4,52},{5,53},{6,54},{7,55},{8,24},{9,... | collective-permute-start | bytes 983048 | tf_op jit(solution)/shard_map/ppermute | solution.py:34
  13.1 0.0 copy-done.8
  13.1 0.0 copy-start.4
  13.1 0.2 convert_reduce_fusion
  13.3 0.0 collective-permute-done
  13.3 0.8 add_multiply_fusion.2
  14.1 1.1 %collective-permute-start.1 = (f32[2,8,128]{2,1,0:T(8,128)S(1)}, f32[2,8,128]{2,1,0:T(8,128)S(1)}, u32[]{:S(2)}, u32[]{:S(2)}) collective-permute-start(f32[2,8,128]{2,1,0:T(8,128)S(1)} %pad_maximum_fusion.2), channel_id=1, source_target_pairs={{0,32},{1,33},{2,34},{3,35},{4,36},{5,37},{6,38},{7,39},{8,40},{9,... | collective-permute-start | bytes 24584 | tf_op jit(solution)/shard_map/ppermute | solution.py:27
  15.2 0.2 multiply_cosine_fusion
  15.3 4.7 %collective-permute-done.3 = bf16[4,32,1280]{2,1,0:T(8,128)(2,1)} collective-permute-done((bf16[4,32,1280]{2,1,0:T(8,128)(2,1)}, bf16[4,32,1280]{2,1,0:T(8,128)(2,1)}, u32[]{:S(2)}, u32[]{:S(2)}) %collective-permute-start.3) | collective-permute-done | bytes 327712 | tf_op jit(solution)/shard_map/ppermute | solution.py:34
  20.0 1.4 %collective-permute-start.4 = (bf16[4,32,1280]{2,1,0:T(8,128)(2,1)}, bf16[4,32,1280]{2,1,0:T(8,128)(2,1)S(1)}, u32[]{:S(2)}, u32[]{:S(2)}) collective-permute-start(bf16[4,32,1280]{2,1,0:T(8,128)(2,1)} %collective-permute-done.3), channel_id=1, source_target_pairs={{0,8},{1,9},{2,10},{3,11},{4,12},{5,13},{6,14},{7,15},{8,0},{9,1},... | collective-permute-start | bytes 983048 | tf_op jit(solution)/shard_map/ppermute | solution.py:27
  21.4 0.0 collective-permute-done.1
  21.4 0.0 copy-done.3
  21.4 2.3 %collective-permute-start.7 = (bf16[2,4,128,640]{3,2,1,0:T(8,128)(2,1)S(1)}, bf16[2,4,128,640]{3,2,1,0:T(8,128)(2,1)S(1)}, u32[]{:S(2)}, u32[]{:S(2)}) collective-permute-start(bf16[2,4,128,640]{3,2,1,0:T(8,128)(2,1)S(1)} %bitcast.18), channel_id=1, source_target_pairs={{0,48},{1,49},{2,50},{3,51},{4,52},{5,53},{6,54},{7,55},{8,56},{9,... | collective-permute-start | bytes 3932168 | tf_op jit(solution)/shard_map/ppermute | solution.py:22
  23.8 0.0 collective-permute-start.6
  23.8 0.0 collective-permute-done.2.refs_5_
  23.8 5.7 %collective-permute-done.4.refs_6_ = bf16[4,32,1280]{2,1,0:T(8,128)(2,1)S(1)} collective-permute-done((bf16[4,32,1280]{2,1,0:T(8,128)(2,1)}, bf16[4,32,1280]{2,1,0:T(8,128)(2,1)S(1)}, u32[]{:S(2)}, u32[]{:S(2)}) %collective-permute-start.4) | collective-permute-done | bytes 327712 | tf_op jit(solution)/shard_map/ppermute | solution.py:27
  29.4 1.5 %collective-permute-start.5 = (f32[2,8,128]{2,1,0:T(8,128)S(1)}, f32[2,8,128]{2,1,0:T(8,128)S(1)}, u32[]{:S(2)}, u32[]{:S(2)}) collective-permute-start(f32[2,8,128]{2,1,0:T(8,128)S(1)} %pad_maximum_fusion.3), channel_id=1, source_target_pairs={{0,8},{1,9},{2,10},{3,11},{4,12},{5,13},{6,14},{7,15},{8,0},{9,1},... | collective-permute-start | bytes 24584 | tf_op jit(solution)/shard_map/ppermute | solution.py:27
  31.0 0.0 copy-done
  31.0 0.7 fusion.refs_4_
  31.7 0.0 copy-done.6
  31.8 0.0 copy-done.7
  31.8 2.8 %collective-permute-done.5 = f32[2,8,128]{2,1,0:T(8,128)S(1)} collective-permute-done((f32[2,8,128]{2,1,0:T(8,128)S(1)}, f32[2,8,128]{2,1,0:T(8,128)S(1)}, u32[]{:S(2)}, u32[]{:S(2)}) %collective-permute-start.5) | collective-permute-done | bytes 8224 | tf_op jit(solution)/shard_map/ppermute | solution.py:27
  34.6 0.0 copy-done.5
  34.6 0.0 copy-done.4
  34.6 0.0 slice-start.1
  34.6 15.0 %conv_queries.1 = (bf16[4,128,1280]{2,1,0:T(8,128)(2,1)S(1)}, bf16[4,128,1280]{2,1,0:T(8,128)(2,1)S(1)}, bf16[4,128,640]{2,1,0:T(8,128)(2,1)S(1)}) custom-call(s32[2]{0:T(128)S(1)} %copy-done.5, f32[2,8,128]{2,1,0:T(8,128)S(1)} %pad_maximum_fusion.4.refs_1_, f32[1,1280]{1,0:T(1,128)S(1)} %reshape.36.refs_2_, f32[1,1280]{1,0:T(1,128)S(1)} %reshape.37.refs_3_, ...), custom_call_target="tpu_custom_call" | custom-call | flops 8388608000 | bytes 22937600 | tf_op jit(solution)/shard_map/conv_queries/pallas_call | solution.py:260
  49.6 1.9 %collective-permute-start.10 = (bf16[4,128,640]{2,1,0:T(8,128)(2,1)S(1)}, bf16[4,128,640]{2,1,0:T(8,128)(2,1)S(1)}, u32[]{:S(2)}, u32[]{:S(2)}) collective-permute-start(bf16[4,128,640]{2,1,0:T(8,128)(2,1)S(1)} %get-tuple-element.27.queries), channel_id=1, source_target_pairs={{0,8},{1,9},{2,10},{3,11},{4,12},{5,13},{6,14},{7,15},{8,0},{9,1},... | collective-permute-start | bytes 1966088 | tf_op jit(solution)/shard_map/ppermute | solution.py:27
  51.5 0.0 slice-done
  51.5 0.0 slice-done.1
  51.5 3.6 %keys_values.1.first = bf16[2,4,128,640]{3,2,1,0:T(8,128)(2,1)} custom-call(bf16[4,128,1280]{2,1,0:T(8,128)(2,1)S(1)} %get-tuple-element.29.normal, bf16[1280,1920]{1,0:T(8,128)(2,1)S(1)} %bitcast.23), custom_call_target="tpu_custom_call" | custom-call | flops 1677721600 | bytes 5898240 | tf_op jit(solution)/shard_map/keys_values/pallas_call | solution.py:301
  55.0 0.0 collective-permute-done.7.third
  55.0 0.0 collective-permute-done.6.second
  55.0 0.1 slice_bitcast_fusion.1
  55.1 0.9 %collective-permute-start.12 = (bf16[2,128,640]{2,1,0:T(8,128)(2,1)S(1)}, bf16[2,128,640]{2,1,0:T(8,128)(2,1)S(1)}, u32[]{:S(2)}, u32[]{:S(2)}) collective-permute-start(bf16[2,128,640]{2,1,0:T(8,128)(2,1)S(1)} %get-tuple-element.40), channel_id=1, source_target_pairs={{0,16},{1,17},{2,18},{3,19},{4,20},{5,21},{6,22},{7,23},{8,24},{9,... | collective-permute-start | bytes 983048 | tf_op jit(solution)/shard_map/ppermute | solution.py:22
  56.0 0.1 slice_bitcast_fusion
  56.1 2.5 %collective-permute-start.13 = (bf16[2,128,640]{2,1,0:T(8,128)(2,1)S(1)}, bf16[2,128,640]{2,1,0:T(8,128)(2,1)S(1)}, u32[]{:S(2)}, u32[]{:S(2)}) collective-permute-start(bf16[2,128,640]{2,1,0:T(8,128)(2,1)S(1)} %get-tuple-element.38), channel_id=1, source_target_pairs={{0,48},{1,49},{2,50},{3,51},{4,52},{5,53},{6,54},{7,55},{8,56},{9,... | collective-permute-start | bytes 983048 | tf_op jit(solution)/shard_map/ppermute | solution.py:22
  58.5 0.0 collective-permute-start.8
  58.5 3.2 %collective-permute-start.9 = (bf16[2,128,640]{2,1,0:T(8,128)(2,1)S(1)}, bf16[2,128,640]{2,1,0:T(8,128)(2,1)S(1)}, u32[]{:S(2)}, u32[]{:S(2)}) collective-permute-start(bf16[2,128,640]{2,1,0:T(8,128)(2,1)S(1)} %get-tuple-element.39), channel_id=1, source_target_pairs={{0,48},{1,49},{2,50},{3,51},{4,52},{5,53},{6,54},{7,55},{8,56},{9,... | collective-permute-start | bytes 983048 | tf_op jit(solution)/shard_map/ppermute | solution.py:22
  61.8 2.3 %collective-permute-done.10.queries = bf16[4,128,640]{2,1,0:T(8,128)(2,1)S(1)} collective-permute-done((bf16[4,128,640]{2,1,0:T(8,128)(2,1)S(1)}, bf16[4,128,640]{2,1,0:T(8,128)(2,1)S(1)}, u32[]{:S(2)}, u32[]{:S(2)}) %collective-permute-start.10) | collective-permute-done | bytes 655392 | tf_op jit(solution)/shard_map/ppermute | solution.py:27
  64.1 1.6 %collective-permute-done.12.far_keys = bf16[2,128,640]{2,1,0:T(8,128)(2,1)S(1)} collective-permute-done((bf16[2,128,640]{2,1,0:T(8,128)(2,1)S(1)}, bf16[2,128,640]{2,1,0:T(8,128)(2,1)S(1)}, u32[]{:S(2)}, u32[]{:S(2)}) %collective-permute-start.12) | collective-permute-done | bytes 327712 | tf_op jit(solution)/shard_map/ppermute | solution.py:22
  65.7 0.0 collective-permute-done.13.far_values
  65.7 2.5 %attend.7 = bf16[2,144,640]{2,1,0:T(8,128)(2,1)S(1)} custom-call(bf16[4,128,640]{2,1,0:T(8,128)(2,1)S(1)} %collective-permute-done.10.queries, bf16[2,4,128,640]{3,2,1,0:T(8,128)(2,1)S(1)} %bitcast.20, bf16[2,4,128,640]{3,2,1,0:T(8,128)(2,1)S(1)} %collective-permute-done.6.second, bf16[2,4,128,640]{3,2,1,0:T(8,128)(2,1)S(1)} %collective-permute-done.7.third, ...), custom_call_target="tpu_custom_call" | custom-call | flops 1342177280 | bytes 3932160 | tf_op jit(solution)/shard_map/attend/pallas_call | solution.py:380
  68.3 2.8 %collective-permute-start.14 = (bf16[2,144,640]{2,1,0:T(8,128)(2,1)S(1)}, bf16[2,144,640]{2,1,0:T(8,128)(2,1)S(1)}, u32[]{:S(2)}, u32[]{:S(2)}) collective-permute-start(bf16[2,144,640]{2,1,0:T(8,128)(2,1)S(1)} %attend.7), channel_id=1, source_target_pairs={{0,8},{1,9},{2,10},{3,11},{4,12},{5,13},{6,14},{7,15},{8,0},{9,1},... | collective-permute-start | bytes 1105928 | tf_op jit(solution)/shard_map/ppermute | solution.py:27
  71.0 0.0 collective-permute-done.8.far_keys
  71.0 0.0 collective-permute-done.9.far_values
  71.1 2.5 %attend.5 = bf16[2,144,640]{2,1,0:T(8,128)(2,1)S(1)} custom-call(bf16[4,128,640]{2,1,0:T(8,128)(2,1)S(1)} %collective-permute-done.10.queries, bf16[2,4,128,640]{3,2,1,0:T(8,128)(2,1)S(1)} %bitcast.21, bf16[2,4,128,640]{3,2,1,0:T(8,128)(2,1)S(1)} %collective-permute-done.6.second, bf16[2,4,128,640]{3,2,1,0:T(8,128)(2,1)S(1)} %collective-permute-done.7.third, ...), custom_call_target="tpu_custom_call" | custom-call | flops 1342177280 | bytes 3932160 | tf_op jit(solution)/shard_map/attend/pallas_call | solution.py:380
  73.6 0.9 %collective-permute-start.11 = (bf16[2,144,640]{2,1,0:T(8,128)(2,1)S(1)}, bf16[2,144,640]{2,1,0:T(8,128)(2,1)S(1)}, u32[]{:S(2)}, u32[]{:S(2)}) collective-permute-start(bf16[2,144,640]{2,1,0:T(8,128)(2,1)S(1)} %attend.5), channel_id=1, source_target_pairs={{0,8},{1,9},{2,10},{3,11},{4,12},{5,13},{6,14},{7,15},{8,0},{9,1},... | collective-permute-start | bytes 1105928 | tf_op jit(solution)/shard_map/ppermute | solution.py:27
  74.5 0.0 copy-done.1
  74.6 2.6 %attend.4 = (f32[2,128,640]{2,1,0:T(8,128)S(1)}, f32[2,16,128]{2,1,0:T(8,128)S(1)}) custom-call(bf16[4,128,640]{2,1,0:T(8,128)(2,1)S(1)} %get-tuple-element.27.queries, bf16[2,4,128,640]{3,2,1,0:T(8,128)(2,1)S(1)} %copy-done.1, bf16[2,4,128,640]{3,2,1,0:T(8,128)(2,1)S(1)} %collective-permute-done.6.second, ...), custom_call_target="tpu_custom_call" | custom-call | flops 1342177280 | bytes 3932160 | tf_op jit(solution)/shard_map/attend/pallas_call | solution.py:380
  77.1 2.6 %attend.6 = (f32[2,128,640]{2,1,0:T(8,128)S(1)}, f32[2,16,128]{2,1,0:T(8,128)S(1)}) custom-call(bf16[4,128,640]{2,1,0:T(8,128)(2,1)S(1)} %get-tuple-element.27.queries, bf16[2,4,128,640]{3,2,1,0:T(8,128)(2,1)S(1)} %copy-done.1, bf16[2,4,128,640]{3,2,1,0:T(8,128)(2,1)S(1)} %collective-permute-done.6.second, ...), custom_call_target="tpu_custom_call" | custom-call | flops 1342177280 | bytes 3932160 | tf_op jit(solution)/shard_map/attend/pallas_call | solution.py:380
  79.7 0.0 collective-permute-done.14.far
  79.7 0.0 copy-done.2
  79.7 2.2 %join_project.2.rest_0_ = bf16[4,128,1280]{2,1,0:T(8,128)(2,1)} custom-call(f32[2,128,640]{2,1,0:T(8,128)S(1)} %get-tuple-element.36.own, f32[2,16,128]{2,1,0:T(8,128)S(1)} %get-tuple-element.37.logs, bf16[2,144,640]{2,1,0:T(8,128)(2,1)S(1)} %collective-permute-done.14.far, bf16[4,128,1280]{2,1,0:T(8,128)(2,1)S(1)} %get-tuple-element.35.hidden, ...), custom_call_target="tpu_custom_call" | custom-call | flops 419430400 | bytes 3276800 | tf_op jit(solution)/shard_map/join_project/pallas_call | solution.py:444
  81.9 1.2 %collective-permute-done.11.far = bf16[2,144,640]{2,1,0:T(8,128)(2,1)S(1)} collective-permute-done((bf16[2,144,640]{2,1,0:T(8,128)(2,1)S(1)}, bf16[2,144,640]{2,1,0:T(8,128)(2,1)S(1)}, u32[]{:S(2)}, u32[]{:S(2)}) %collective-permute-start.11) | collective-permute-done | bytes 368672 | tf_op jit(solution)/shard_map/ppermute | solution.py:27
  83.1 2.2 %join_project.3 = bf16[4,128,1280]{2,1,0:T(8,128)(2,1)} custom-call(f32[2,128,640]{2,1,0:T(8,128)S(1)} %get-tuple-element.33.own, f32[2,16,128]{2,1,0:T(8,128)S(1)} %get-tuple-element.34.logs, bf16[2,144,640]{2,1,0:T(8,128)(2,1)S(1)} %collective-permute-done.11.far, ...), custom_call_target="tpu_custom_call", output_to_operand_aliasing={{}: (5, {})} | custom-call | flops 419430400 | bytes 3276800 | tf_op jit(solution)/shard_map/join_project/pallas_call | solution.py:444
  (13 shorter events, 0.1 us)
Async XLA Ops:
  0.6 30.4 %copy-start = (bf16[1280,640]{1,0:T(8,128)(2,1)S(1)}, bf16[1280,640]{1,0:T(8,128)(2,1)}, u32[]{:S(2)}) copy-start(bf16[1280,640]{1,0:T(8,128)(2,1)} %param.17) | copy-start | bytes 4915204
  1.3 11.8 %copy-start.8 = (s32[4,8]{1,0:T(4,128)S(1)}, s32[4,8]{1,0:T(4,128)}, u32[]{:S(2)}) copy-start(s32[4,8]{1,0:T(4,128)} %param.13) | copy-start | bytes 388
  1.3 20.1 %copy-start.3 = (bf16[2,4,4,32,640]{4,3,2,1,0:T(8,128)(2,1)S(1)}, bf16[2,4,4,32,640]{4,3,2,1,0:T(8,128)(2,1)}, u32[]{:S(2)}) copy-start(bf16[2,4,4,32,640]{4,3,2,1,0:T(8,128)(2,1)} %param.12) | copy-start | bytes 3932164
  5.2 26.5 %copy-start.6 = (f32[1280]{0:T(1024)S(1)}, f32[1280]{0:T(1024)}, u32[]{:S(2)}) copy-start(f32[1280]{0:T(1024)} %param.14) | copy-start | bytes 15364
  5.3 26.5 %copy-start.7 = (f32[1280]{0:T(1024)S(1)}, f32[1280]{0:T(1024)}, u32[]{:S(2)}) copy-start(f32[1280]{0:T(1024)} %param.15) | copy-start | bytes 15364
  5.3 29.3 %copy-start.5 = (s32[2]{0:T(128)S(1)}, s32[2]{0:T(128)}, u32[]{:S(2)}) copy-start(s32[2]{0:T(128)} %pad_add_fusion.spot.refs_0_) | copy-start | bytes 28
  5.3 8.0 %collective-permute-start = (f32[2,8,128]{2,1,0:T(8,128)}, f32[2,8,128]{2,1,0:T(8,128)S(1)}, u32[]{:S(2)}, u32[]{:S(2)}) collective-permute-start(f32[2,8,128]{2,1,0:T(8,128)} %get-tuple-element.20), channel_id=1, source_target_pairs={{0,16},{1,17},{2,18},{3,19},{4,20},{5,21},{6,22},{7,23},{8,24},{9,... | collective-permute-start | bytes 24584 | tf_op jit(solution)/shard_map/ppermute | solution.py:27
  7.4 16.4 %collective-permute-start.2 = (bf16[4,32,1280]{2,1,0:T(8,128)(2,1)}, bf16[4,32,1280]{2,1,0:T(8,128)(2,1)S(1)}, u32[]{:S(2)}, u32[]{:S(2)}) collective-permute-start(bf16[4,32,1280]{2,1,0:T(8,128)(2,1)} %get-tuple-element.22), channel_id=1, source_target_pairs={{0,8},{1,9},{2,10},{3,11},{4,12},{5,13},{6,14},{7,15},{8,0},{9,1},... | collective-permute-start | bytes 983048 | tf_op jit(solution)/shard_map/ppermute | solution.py:27
  10.6 9.5 %collective-permute-start.3 = (bf16[4,32,1280]{2,1,0:T(8,128)(2,1)}, bf16[4,32,1280]{2,1,0:T(8,128)(2,1)}, u32[]{:S(2)}, u32[]{:S(2)}) collective-permute-start(bf16[4,32,1280]{2,1,0:T(8,128)(2,1)} %get-tuple-element.23), channel_id=1, source_target_pairs={{0,48},{1,49},{2,50},{3,51},{4,52},{5,53},{6,54},{7,55},{8,24},{9,... | collective-permute-start | bytes 983048 | tf_op jit(solution)/shard_map/ppermute | solution.py:34
  13.1 21.5 %copy-start.4 = (bf16[4,4,32,1280]{3,2,1,0:T(8,128)(2,1)S(1)}, bf16[4,4,32,1280]{3,2,1,0:T(8,128)(2,1)}, u32[]{:S(2)}) copy-start(bf16[4,4,32,1280]{3,2,1,0:T(8,128)(2,1)} %param.10) | copy-start | bytes 3932164
  14.1 7.3 %collective-permute-start.1 = (f32[2,8,128]{2,1,0:T(8,128)S(1)}, f32[2,8,128]{2,1,0:T(8,128)S(1)}, u32[]{:S(2)}, u32[]{:S(2)}) collective-permute-start(f32[2,8,128]{2,1,0:T(8,128)S(1)} %pad_maximum_fusion.2), channel_id=1, source_target_pairs={{0,32},{1,33},{2,34},{3,35},{4,36},{5,37},{6,38},{7,39},{8,40},{9,... | collective-permute-start | bytes 24584 | tf_op jit(solution)/shard_map/ppermute | solution.py:27
  20.0 9.4 %collective-permute-start.4 = (bf16[4,32,1280]{2,1,0:T(8,128)(2,1)}, bf16[4,32,1280]{2,1,0:T(8,128)(2,1)S(1)}, u32[]{:S(2)}, u32[]{:S(2)}) collective-permute-start(bf16[4,32,1280]{2,1,0:T(8,128)(2,1)} %collective-permute-done.3), channel_id=1, source_target_pairs={{0,8},{1,9},{2,10},{3,11},{4,12},{5,13},{6,14},{7,15},{8,0},{9,1},... | collective-permute-start | bytes 983048 | tf_op jit(solution)/shard_map/ppermute | solution.py:27
  21.4 33.6 %collective-permute-start.7 = (bf16[2,4,128,640]{3,2,1,0:T(8,128)(2,1)S(1)}, bf16[2,4,128,640]{3,2,1,0:T(8,128)(2,1)S(1)}, u32[]{:S(2)}, u32[]{:S(2)}) collective-permute-start(bf16[2,4,128,640]{3,2,1,0:T(8,128)(2,1)S(1)} %bitcast.18), channel_id=1, source_target_pairs={{0,48},{1,49},{2,50},{3,51},{4,52},{5,53},{6,54},{7,55},{8,56},{9,... | collective-permute-start | bytes 3932168 | tf_op jit(solution)/shard_map/ppermute | solution.py:22
  23.8 31.3 %collective-permute-start.6 = (bf16[2,4,128,640]{3,2,1,0:T(8,128)(2,1)S(1)}, bf16[2,4,128,640]{3,2,1,0:T(8,128)(2,1)S(1)}, u32[]{:S(2)}, u32[]{:S(2)}) collective-permute-start(bf16[2,4,128,640]{3,2,1,0:T(8,128)(2,1)S(1)} %bitcast.19), channel_id=1, source_target_pairs={{0,16},{1,17},{2,18},{3,19},{4,20},{5,21},{6,22},{7,23},{8,24},{9,... | collective-permute-start | bytes 3932168 | tf_op jit(solution)/shard_map/ppermute | solution.py:22
  29.4 5.2 %collective-permute-start.5 = (f32[2,8,128]{2,1,0:T(8,128)S(1)}, f32[2,8,128]{2,1,0:T(8,128)S(1)}, u32[]{:S(2)}, u32[]{:S(2)}) collective-permute-start(f32[2,8,128]{2,1,0:T(8,128)S(1)} %pad_maximum_fusion.3), channel_id=1, source_target_pairs={{0,8},{1,9},{2,10},{3,11},{4,12},{5,13},{6,14},{7,15},{8,0},{9,1},... | collective-permute-start | bytes 24584 | tf_op jit(solution)/shard_map/ppermute | solution.py:27
  34.6 16.9 %slice-start = ((s8[4915200]{0:T(1024)(128)(4,1)}), s8[4194304]{0:T(1024)(128)(4,1)S(1)}, s32[]{:S(2)}) async-start(s8[4915200]{0:T(1024)(128)(4,1)} %bitcast.22), calls=%async_computation | async-start | bytes 8388608
  34.6 16.8 %slice-start.1 = ((s8[4915200]{0:T(1024)(128)(4,1)}), s8[720896]{0:T(1024)(128)(4,1)S(1)}, s32[]{:S(2)}) async-start(s8[4915200]{0:T(1024)(128)(4,1)} %bitcast.22), calls=%async_computation.1 | async-start | bytes 1441792
  49.6 14.5 %collective-permute-start.10 = (bf16[4,128,640]{2,1,0:T(8,128)(2,1)S(1)}, bf16[4,128,640]{2,1,0:T(8,128)(2,1)S(1)}, u32[]{:S(2)}, u32[]{:S(2)}) collective-permute-start(bf16[4,128,640]{2,1,0:T(8,128)(2,1)S(1)} %get-tuple-element.27.queries), channel_id=1, source_target_pairs={{0,8},{1,9},{2,10},{3,11},{4,12},{5,13},{6,14},{7,15},{8,0},{9,1},... | collective-permute-start | bytes 1966088 | tf_op jit(solution)/shard_map/ppermute | solution.py:27
  55.1 10.6 %collective-permute-start.12 = (bf16[2,128,640]{2,1,0:T(8,128)(2,1)S(1)}, bf16[2,128,640]{2,1,0:T(8,128)(2,1)S(1)}, u32[]{:S(2)}, u32[]{:S(2)}) collective-permute-start(bf16[2,128,640]{2,1,0:T(8,128)(2,1)S(1)} %get-tuple-element.40), channel_id=1, source_target_pairs={{0,16},{1,17},{2,18},{3,19},{4,20},{5,21},{6,22},{7,23},{8,24},{9,... | collective-permute-start | bytes 983048 | tf_op jit(solution)/shard_map/ppermute | solution.py:22
  56.1 9.6 %collective-permute-start.13 = (bf16[2,128,640]{2,1,0:T(8,128)(2,1)S(1)}, bf16[2,128,640]{2,1,0:T(8,128)(2,1)S(1)}, u32[]{:S(2)}, u32[]{:S(2)}) collective-permute-start(bf16[2,128,640]{2,1,0:T(8,128)(2,1)S(1)} %get-tuple-element.38), channel_id=1, source_target_pairs={{0,48},{1,49},{2,50},{3,51},{4,52},{5,53},{6,54},{7,55},{8,56},{9,... | collective-permute-start | bytes 983048 | tf_op jit(solution)/shard_map/ppermute | solution.py:22
  58.5 12.5 %collective-permute-start.8 = (bf16[2,128,640]{2,1,0:T(8,128)(2,1)S(1)}, bf16[2,128,640]{2,1,0:T(8,128)(2,1)S(1)}, u32[]{:S(2)}, u32[]{:S(2)}) collective-permute-start(bf16[2,128,640]{2,1,0:T(8,128)(2,1)S(1)} %get-tuple-element.41), channel_id=1, source_target_pairs={{0,16},{1,17},{2,18},{3,19},{4,20},{5,21},{6,22},{7,23},{8,24},{9,... | collective-permute-start | bytes 983048 | tf_op jit(solution)/shard_map/ppermute | solution.py:22
  58.5 12.5 %collective-permute-start.9 = (bf16[2,128,640]{2,1,0:T(8,128)(2,1)S(1)}, bf16[2,128,640]{2,1,0:T(8,128)(2,1)S(1)}, u32[]{:S(2)}, u32[]{:S(2)}) collective-permute-start(bf16[2,128,640]{2,1,0:T(8,128)(2,1)S(1)} %get-tuple-element.39), channel_id=1, source_target_pairs={{0,48},{1,49},{2,50},{3,51},{4,52},{5,53},{6,54},{7,55},{8,56},{9,... | collective-permute-start | bytes 983048 | tf_op jit(solution)/shard_map/ppermute | solution.py:22
  68.2 6.3 %copy-start.1 = (bf16[2,4,128,640]{3,2,1,0:T(8,128)(2,1)S(1)}, bf16[2,4,128,640]{3,2,1,0:T(8,128)(2,1)}, u32[]{:S(2)}) copy-start(bf16[2,4,128,640]{3,2,1,0:T(8,128)(2,1)} %keys_values.1.first) | copy-start | bytes 3932164
  68.3 11.4 %collective-permute-start.14 = (bf16[2,144,640]{2,1,0:T(8,128)(2,1)S(1)}, bf16[2,144,640]{2,1,0:T(8,128)(2,1)S(1)}, u32[]{:S(2)}, u32[]{:S(2)}) collective-permute-start(bf16[2,144,640]{2,1,0:T(8,128)(2,1)S(1)} %attend.7), channel_id=1, source_target_pairs={{0,8},{1,9},{2,10},{3,11},{4,12},{5,13},{6,14},{7,15},{8,0},{9,1},... | collective-permute-start | bytes 1105928 | tf_op jit(solution)/shard_map/ppermute | solution.py:27
  73.6 9.5 %collective-permute-start.11 = (bf16[2,144,640]{2,1,0:T(8,128)(2,1)S(1)}, bf16[2,144,640]{2,1,0:T(8,128)(2,1)S(1)}, u32[]{:S(2)}, u32[]{:S(2)}) collective-permute-start(bf16[2,144,640]{2,1,0:T(8,128)(2,1)S(1)} %attend.5), channel_id=1, source_target_pairs={{0,8},{1,9},{2,10},{3,11},{4,12},{5,13},{6,14},{7,15},{8,0},{9,1},... | collective-permute-start | bytes 1105928 | tf_op jit(solution)/shard_map/ppermute | solution.py:27
  77.1 2.6 %copy-start.2 = (bf16[640,1280]{1,0:T(8,128)(2,1)S(1)}, bf16[640,1280]{1,0:T(8,128)(2,1)}, u32[]{:S(2)}) copy-start(bf16[640,1280]{1,0:T(8,128)(2,1)} %weight.5) | copy-start | bytes 4915204

commit v4 on v3

--- a/solution.py
+++ b/solution.py
@@ -62,7 +62,7 @@
     return found[0:8] + found[8:16] + found[16:24]
 
 
-def stats_kernel(spot, latent_hbm, act_hbm, out, near, away, latent, rims, sums, sems):
+def stats_kernel(latent_hbm, act_hbm, out, near, away, latent, rims, sums, sems):
     images, tokens, channels = latent.shape
     columns = near.shape[1]
     per_group = channels // GROUPS
@@ -71,7 +71,7 @@
     ]
     for copy in copies:
         copy.start()
-    start = spot[0] * (tokens - columns)
+    start = lax.rem(lax.div(lax.axis_index("band"), STACK), 2) * (tokens - columns)
     sides = [
         pl.ds(pl.multiple_of(first, columns), columns)
         for first in (tokens - columns - start, start)
@@ -106,7 +106,7 @@
         onward.wait()
 
 
-def local_stats(spot, latent, stale_act, columns):
+def local_stats(latent, stale_act, columns):
     images, tokens, channels = latent.shape
     anywhere = pl.BlockSpec(memory_space=pltpu.HBM)
     vmem = pl.BlockSpec(memory_space=pltpu.VMEM)
@@ -114,7 +114,7 @@
     return pl.pallas_call(
         stats_kernel,
         out_shape=(jax.ShapeDtypeStruct((2, 8, LANES), jnp.float32), rim, rim),
-        in_specs=[pl.BlockSpec(memory_space=pltpu.SMEM)] + [anywhere] * 2,
+        in_specs=[anywhere] * 2,
         out_specs=(vmem, anywhere, anywhere),
         scratch_shapes=[
             pltpu.VMEM(latent.shape, jnp.bfloat16),
@@ -127,7 +127,7 @@
             flops=8 * latent.size, bytes_accessed=3 * latent.size, transcendentals=0
         ),
         name="group_stats",
-    )(spot, latent, stale_act)
+    )(latent, stale_act)
 
 
 def merged(own, other, count):
@@ -488,7 +488,7 @@
     upper = place % 2
     inside = (place > 0) & (place < IMG_ROWS // height - 1)
     spot = jnp.stack([upper, inside.astype(jnp.int32)]).astype(jnp.int32)
-    stats, near, away = local_stats(spot, latent, stale_act, columns)
+    stats, near, away = local_stats(latent, stale_act, columns)
     near = flipped(near, 1)
     away = flipped(outward(away), 1)
     count = tokens * per_group

time: 85.4 us -> 85.5 us (level)
  local copies, waits for them, and re-layouts: 0.19 us -> 1.63 us
    unnamed x22 -> x20, local copies, waits for them, and re-layouts: 0.05 us -> 1.51 us
where the time goes in v4:
time: 85.5 us; the launch traced here: 85.3 us
  Pallas kernels  36.3 us (42%)
  starting transfers between devices  26.3 us (31%)
  waiting for transfers between devices  18.4 us (22%)
  local copies, waits for them, and re-layouts  1.63 us (2%)
  other arithmetic  1.15 us (1%)
    pallas_call x1, Pallas kernels, convolve(): pl.pallas_call(body, out_shape=(jax.ShapeDtypeStruct(latent.shape, jnp.bf...  15 us
    ppermute x8, starting transfers between devices, flipped(): lax.ppermute(value, 'band', [(i, i ^ bit * STACK) for i in range(count)])  14.6 us
    ppermute x8, waiting for transfers between devices, flipped(): lax.ppermute(value, 'band', [(i, i ^ bit * STACK) for i in range(count)])  12.5 us
    pallas_call x4, Pallas kernels, attend(): pl.pallas_call(attend_kernel, grid=(images,), out_shape=out_shape, in_spe...  10.2 us
    ppermute x6, starting transfers between devices, rotated(): lax.ppermute(value, 'band', [(i, (i + by) % count) for i in range(count)])  9.18 us
    pallas_call x2, Pallas kernels, join(): pl.pallas_call(join_kernel, grid=(1,), out_shape=jax.ShapeDtypeStruct(hid...  4.36 us
    ppermute x1, waiting for transfers between devices, outward(): return lax.ppermute(value, 'band', pairs)  4.03 us
    pallas_call x1, Pallas kernels, project(): pl.pallas_call(project_kernel, grid=(2,), out_shape=jax.ShapeDtypeStruct(...  3.55 us
  transfers between devices with their start and end apart: 15, of which 6 were waited for; matrix products, arithmetic and copies ran while one was open for 2% of the time, Pallas kernels for 36%

profile of v4, /device:TPU:0, one launch (start us, length us, event | category | flops | bytes accessed | tf_op | source)
XLA Modules:
  0.0 85.3 jit_solution(2927394399071984322)
XLA Ops:
  0.6 0.0 copy-start
  0.6 0.0 copy-start.7
  0.7 3.2 %group_stats.1 = (f32[2,8,128]{2,1,0:T(8,128)}, bf16[4,32,1280]{2,1,0:T(8,128)(2,1)}, bf16[4,32,1280]{2,1,0:T(8,128)(2,1)}) custom-call(bf16[4,128,1280]{2,1,0:T(8,128)(2,1)} %bitcast.24, bf16[4,128,1280]{2,1,0:T(8,128)(2,1)} %bitcast.27), custom_call_target="tpu_custom_call" | custom-call | flops 5242880 | bytes 1966080 | tf_op jit(solution)/shard_map/group_stats/pallas_call | solution.py:114
  3.9 0.0 copy-start.3
  3.9 0.0 copy-start.5
  3.9 0.0 copy-start.6
  3.9 2.1 %collective-permute-start = (f32[2,8,128]{2,1,0:T(8,128)}, f32[2,8,128]{2,1,0:T(8,128)S(1)}, u32[]{:S(2)}, u32[]{:S(2)}) collective-permute-start(f32[2,8,128]{2,1,0:T(8,128)} %get-tuple-element.20), channel_id=1, source_target_pairs={{0,16},{1,17},{2,18},{3,19},{4,20},{5,21},{6,22},{7,23},{8,24},{9,... | collective-permute-start | bytes 24584 | tf_op jit(solution)/shard_map/ppermute | solution.py:27
  6.0 3.2 %collective-permute-start.2 = (bf16[4,32,1280]{2,1,0:T(8,128)(2,1)}, bf16[4,32,1280]{2,1,0:T(8,128)(2,1)S(1)}, u32[]{:S(2)}, u32[]{:S(2)}) collective-permute-start(bf16[4,32,1280]{2,1,0:T(8,128)(2,1)} %get-tuple-element.22), channel_id=1, source_target_pairs={{0,8},{1,9},{2,10},{3,11},{4,12},{5,13},{6,14},{7,15},{8,0},{9,1},... | collective-permute-start | bytes 983048 | tf_op jit(solution)/shard_map/ppermute | solution.py:27
  9.2 2.5 %collective-permute-start.3 = (bf16[4,32,1280]{2,1,0:T(8,128)(2,1)}, bf16[4,32,1280]{2,1,0:T(8,128)(2,1)}, u32[]{:S(2)}, u32[]{:S(2)}) collective-permute-start(bf16[4,32,1280]{2,1,0:T(8,128)(2,1)} %get-tuple-element.23), channel_id=1, source_target_pairs={{0,48},{1,49},{2,50},{3,51},{4,52},{5,53},{6,54},{7,55},{8,24},{9,... | collective-permute-start | bytes 983048 | tf_op jit(solution)/shard_map/ppermute | solution.py:34
  11.7 0.0 copy-done.7
  11.7 0.2 convert_reduce_fusion
  11.9 0.2 multiply_cosine_fusion
  12.1 0.0 collective-permute-done
  12.1 0.7 add_multiply_fusion.2
  12.8 1.1 %collective-permute-start.1 = (f32[2,8,128]{2,1,0:T(8,128)S(1)}, f32[2,8,128]{2,1,0:T(8,128)S(1)}, u32[]{:S(2)}, u32[]{:S(2)}) collective-permute-start(f32[2,8,128]{2,1,0:T(8,128)S(1)} %pad_maximum_fusion.2), channel_id=1, source_target_pairs={{0,32},{1,33},{2,34},{3,35},{4,36},{5,37},{6,38},{7,39},{8,40},{9,... | collective-permute-start | bytes 24584 | tf_op jit(solution)/shard_map/ppermute | solution.py:27
  13.9 0.0 copy-done
  13.9 0.7 fusion.refs_4_
  14.6 4.0 %collective-permute-done.3 = bf16[4,32,1280]{2,1,0:T(8,128)(2,1)} collective-permute-done((bf16[4,32,1280]{2,1,0:T(8,128)(2,1)}, bf16[4,32,1280]{2,1,0:T(8,128)(2,1)}, u32[]{:S(2)}, u32[]{:S(2)}) %collective-permute-start.3) | collective-permute-done | bytes 327712 | tf_op jit(solution)/shard_map/ppermute | solution.py:34
  18.7 1.4 %collective-permute-start.4 = (bf16[4,32,1280]{2,1,0:T(8,128)(2,1)}, bf16[4,32,1280]{2,1,0:T(8,128)(2,1)S(1)}, u32[]{:S(2)}, u32[]{:S(2)}) collective-permute-start(bf16[4,32,1280]{2,1,0:T(8,128)(2,1)} %collective-permute-done.3), channel_id=1, source_target_pairs={{0,8},{1,9},{2,10},{3,11},{4,12},{5,13},{6,14},{7,15},{8,0},{9,1},... | collective-permute-start | bytes 983048 | tf_op jit(solution)/shard_map/ppermute | solution.py:27
  20.1 0.0 collective-permute-done.1
  20.1 0.0 copy-done.3
  20.1 2.3 %collective-permute-start.7 = (bf16[2,4,128,640]{3,2,1,0:T(8,128)(2,1)S(1)}, bf16[2,4,128,640]{3,2,1,0:T(8,128)(2,1)S(1)}, u32[]{:S(2)}, u32[]{:S(2)}) collective-permute-start(bf16[2,4,128,640]{3,2,1,0:T(8,128)(2,1)S(1)} %bitcast.18), channel_id=1, source_target_pairs={{0,48},{1,49},{2,50},{3,51},{4,52},{5,53},{6,54},{7,55},{8,56},{9,... | collective-permute-start | bytes 3932168 | tf_op jit(solution)/shard_map/ppermute | solution.py:22
  22.4 0.0 collective-permute-start.6
  22.4 0.0 collective-permute-done.2.refs_5_
  22.4 5.7 %collective-permute-done.4.refs_6_ = bf16[4,32,1280]{2,1,0:T(8,128)(2,1)S(1)} collective-permute-done((bf16[4,32,1280]{2,1,0:T(8,128)(2,1)}, bf16[4,32,1280]{2,1,0:T(8,128)(2,1)S(1)}, u32[]{:S(2)}, u32[]{:S(2)}) %collective-permute-start.4) | collective-permute-done | bytes 327712 | tf_op jit(solution)/shard_map/ppermute | solution.py:27
  28.1 1.5 %collective-permute-start.5 = (f32[2,8,128]{2,1,0:T(8,128)S(1)}, f32[2,8,128]{2,1,0:T(8,128)S(1)}, u32[]{:S(2)}, u32[]{:S(2)}) collective-permute-start(f32[2,8,128]{2,1,0:T(8,128)S(1)} %pad_maximum_fusion.3), channel_id=1, source_target_pairs={{0,8},{1,9},{2,10},{3,11},{4,12},{5,13},{6,14},{7,15},{8,0},{9,1},... | collective-permute-start | bytes 24584 | tf_op jit(solution)/shard_map/ppermute | solution.py:27
  29.6 0.1 pad_add_fusion.refs_0_
  29.7 0.0 copy-done.5
  29.7 0.0 copy-done.6
  29.7 3.5 %collective-permute-done.5 = f32[2,8,128]{2,1,0:T(8,128)S(1)} collective-permute-done((f32[2,8,128]{2,1,0:T(8,128)S(1)}, f32[2,8,128]{2,1,0:T(8,128)S(1)}, u32[]{:S(2)}, u32[]{:S(2)}) %collective-permute-start.5) | collective-permute-done | bytes 8224 | tf_op jit(solution)/shard_map/ppermute | solution.py:27
  33.3 0.0 slice-start
  33.3 0.0 copy-start.4
  33.3 1.5 %copy-done.4 = bf16[4,4,32,1280]{3,2,1,0:T(8,128)(2,1)S(1)} copy-done((bf16[4,4,32,1280]{3,2,1,0:T(8,128)(2,1)S(1)}, bf16[4,4,32,1280]{3,2,1,0:T(8,128)(2,1)}, u32[]{:S(2)}) %copy-start.4) | copy-done | bytes 1310744
  34.7 0.0 slice-start.1
  34.7 15.0 %conv_queries.1 = (bf16[4,128,1280]{2,1,0:T(8,128)(2,1)S(1)}, bf16[4,128,1280]{2,1,0:T(8,128)(2,1)S(1)}, bf16[4,128,640]{2,1,0:T(8,128)(2,1)S(1)}) custom-call(s32[2]{0:T(128)S(1)} %pad_add_fusion.refs_0_, f32[2,8,128]{2,1,0:T(8,128)S(1)} %pad_maximum_fusion.4.refs_1_, f32[1,1280]{1,0:T(1,128)S(1)} %reshape.36.refs_2_, f32[1,1280]{1,0:T(1,128)S(1)} %reshape.37.refs_3_, ...), custom_call_target="tpu_custom_call" | custom-call | flops 8388608000 | bytes 22937600 | tf_op jit(solution)/shard_map/conv_queries/pallas_call | solution.py:260
  49.7 1.6 %collective-permute-start.10 = (bf16[4,128,640]{2,1,0:T(8,128)(2,1)S(1)}, bf16[4,128,640]{2,1,0:T(8,128)(2,1)S(1)}, u32[]{:S(2)}, u32[]{:S(2)}) collective-permute-start(bf16[4,128,640]{2,1,0:T(8,128)(2,1)S(1)} %get-tuple-element.27.queries), channel_id=1, source_target_pairs={{0,8},{1,9},{2,10},{3,11},{4,12},{5,13},{6,14},{7,15},{8,0},{9,1},... | collective-permute-start | bytes 1966088 | tf_op jit(solution)/shard_map/ppermute | solution.py:27
  51.3 0.0 slice-done
  51.3 0.0 slice-done.1
  51.3 3.6 %keys_values.1.first = bf16[2,4,128,640]{3,2,1,0:T(8,128)(2,1)} custom-call(bf16[4,128,1280]{2,1,0:T(8,128)(2,1)S(1)} %get-tuple-element.29.normal, bf16[1280,1920]{1,0:T(8,128)(2,1)S(1)} %bitcast.23), custom_call_target="tpu_custom_call" | custom-call | flops 1677721600 | bytes 5898240 | tf_op jit(solution)/shard_map/keys_values/pallas_call | solution.py:301
  54.9 0.0 collective-permute-done.7.third
  54.9 0.0 collective-permute-done.6.second
  54.9 0.1 slice_bitcast_fusion.1
  55.0 1.1 %collective-permute-start.12 = (bf16[2,128,640]{2,1,0:T(8,128)(2,1)S(1)}, bf16[2,128,640]{2,1,0:T(8,128)(2,1)S(1)}, u32[]{:S(2)}, u32[]{:S(2)}) collective-permute-start(bf16[2,128,640]{2,1,0:T(8,128)(2,1)S(1)} %get-tuple-element.40), channel_id=1, source_target_pairs={{0,16},{1,17},{2,18},{3,19},{4,20},{5,21},{6,22},{7,23},{8,24},{9,... | collective-permute-start | bytes 983048 | tf_op jit(solution)/shard_map/ppermute | solution.py:22
  56.1 0.1 slice_bitcast_fusion
  56.1 2.5 %collective-permute-start.13 = (bf16[2,128,640]{2,1,0:T(8,128)(2,1)S(1)}, bf16[2,128,640]{2,1,0:T(8,128)(2,1)S(1)}, u32[]{:S(2)}, u32[]{:S(2)}) collective-permute-start(bf16[2,128,640]{2,1,0:T(8,128)(2,1)S(1)} %get-tuple-element.38), channel_id=1, source_target_pairs={{0,48},{1,49},{2,50},{3,51},{4,52},{5,53},{6,54},{7,55},{8,56},{9,... | collective-permute-start | bytes 983048 | tf_op jit(solution)/shard_map/ppermute | solution.py:22
  58.6 0.0 collective-permute-start.8
  58.6 3.2 %collective-permute-start.9 = (bf16[2,128,640]{2,1,0:T(8,128)(2,1)S(1)}, bf16[2,128,640]{2,1,0:T(8,128)(2,1)S(1)}, u32[]{:S(2)}, u32[]{:S(2)}) collective-permute-start(bf16[2,128,640]{2,1,0:T(8,128)(2,1)S(1)} %get-tuple-element.39), channel_id=1, source_target_pairs={{0,48},{1,49},{2,50},{3,51},{4,52},{5,53},{6,54},{7,55},{8,56},{9,... | collective-permute-start | bytes 983048 | tf_op jit(solution)/shard_map/ppermute | solution.py:22
  61.9 2.1 %collective-permute-done.10.queries = bf16[4,128,640]{2,1,0:T(8,128)(2,1)S(1)} collective-permute-done((bf16[4,128,640]{2,1,0:T(8,128)(2,1)S(1)}, bf16[4,128,640]{2,1,0:T(8,128)(2,1)S(1)}, u32[]{:S(2)}, u32[]{:S(2)}) %collective-permute-start.10) | collective-permute-done | bytes 655392 | tf_op jit(solution)/shard_map/ppermute | solution.py:27
  64.0 1.8 %collective-permute-done.12.far_keys = bf16[2,128,640]{2,1,0:T(8,128)(2,1)S(1)} collective-permute-done((bf16[2,128,640]{2,1,0:T(8,128)(2,1)S(1)}, bf16[2,128,640]{2,1,0:T(8,128)(2,1)S(1)}, u32[]{:S(2)}, u32[]{:S(2)}) %collective-permute-start.12) | collective-permute-done | bytes 327712 | tf_op jit(solution)/shard_map/ppermute | solution.py:22
  65.8 0.0 collective-permute-done.13.far_values
  65.8 2.5 %attend.7 = bf16[2,144,640]{2,1,0:T(8,128)(2,1)S(1)} custom-call(bf16[4,128,640]{2,1,0:T(8,128)(2,1)S(1)} %collective-permute-done.10.queries, bf16[2,4,128,640]{3,2,1,0:T(8,128)(2,1)S(1)} %bitcast.20, bf16[2,4,128,640]{3,2,1,0:T(8,128)(2,1)S(1)} %collective-permute-done.6.second, bf16[2,4,128,640]{3,2,1,0:T(8,128)(2,1)S(1)} %collective-permute-done.7.third, ...), custom_call_target="tpu_custom_call" | custom-call | flops 1342177280 | bytes 3932160 | tf_op jit(solution)/shard_map/attend/pallas_call | solution.py:380
  68.3 2.8 %collective-permute-start.14 = (bf16[2,144,640]{2,1,0:T(8,128)(2,1)S(1)}, bf16[2,144,640]{2,1,0:T(8,128)(2,1)S(1)}, u32[]{:S(2)}, u32[]{:S(2)}) collective-permute-start(bf16[2,144,640]{2,1,0:T(8,128)(2,1)S(1)} %attend.7), channel_id=1, source_target_pairs={{0,8},{1,9},{2,10},{3,11},{4,12},{5,13},{6,14},{7,15},{8,0},{9,1},... | collective-permute-start | bytes 1105928 | tf_op jit(solution)/shard_map/ppermute | solution.py:27
  71.1 0.0 collective-permute-done.8.far_keys
  71.1 0.0 collective-permute-done.9.far_values
  71.1 2.5 %attend.5 = bf16[2,144,640]{2,1,0:T(8,128)(2,1)S(1)} custom-call(bf16[4,128,640]{2,1,0:T(8,128)(2,1)S(1)} %collective-permute-done.10.queries, bf16[2,4,128,640]{3,2,1,0:T(8,128)(2,1)S(1)} %bitcast.21, bf16[2,4,128,640]{3,2,1,0:T(8,128)(2,1)S(1)} %collective-permute-done.6.second, bf16[2,4,128,640]{3,2,1,0:T(8,128)(2,1)S(1)} %collective-permute-done.7.third, ...), custom_call_target="tpu_custom_call" | custom-call | flops 1342177280 | bytes 3932160 | tf_op jit(solution)/shard_map/attend/pallas_call | solution.py:380
  73.7 0.9 %collective-permute-start.11 = (bf16[2,144,640]{2,1,0:T(8,128)(2,1)S(1)}, bf16[2,144,640]{2,1,0:T(8,128)(2,1)S(1)}, u32[]{:S(2)}, u32[]{:S(2)}) collective-permute-start(bf16[2,144,640]{2,1,0:T(8,128)(2,1)S(1)} %attend.5), channel_id=1, source_target_pairs={{0,8},{1,9},{2,10},{3,11},{4,12},{5,13},{6,14},{7,15},{8,0},{9,1},... | collective-permute-start | bytes 1105928 | tf_op jit(solution)/shard_map/ppermute | solution.py:27
  74.6 0.0 copy-done.1
  74.6 2.6 %attend.4 = (f32[2,128,640]{2,1,0:T(8,128)S(1)}, f32[2,16,128]{2,1,0:T(8,128)S(1)}) custom-call(bf16[4,128,640]{2,1,0:T(8,128)(2,1)S(1)} %get-tuple-element.27.queries, bf16[2,4,128,640]{3,2,1,0:T(8,128)(2,1)S(1)} %copy-done.1, bf16[2,4,128,640]{3,2,1,0:T(8,128)(2,1)S(1)} %collective-permute-done.6.second, ...), custom_call_target="tpu_custom_call" | custom-call | flops 1342177280 | bytes 3932160 | tf_op jit(solution)/shard_map/attend/pallas_call | solution.py:380
  77.2 2.6 %attend.6 = (f32[2,128,640]{2,1,0:T(8,128)S(1)}, f32[2,16,128]{2,1,0:T(8,128)S(1)}) custom-call(bf16[4,128,640]{2,1,0:T(8,128)(2,1)S(1)} %get-tuple-element.27.queries, bf16[2,4,128,640]{3,2,1,0:T(8,128)(2,1)S(1)} %copy-done.1, bf16[2,4,128,640]{3,2,1,0:T(8,128)(2,1)S(1)} %collective-permute-done.6.second, ...), custom_call_target="tpu_custom_call" | custom-call | flops 1342177280 | bytes 3932160 | tf_op jit(solution)/shard_map/attend/pallas_call | solution.py:380
  79.8 0.0 collective-permute-done.14.far
  79.8 0.0 copy-done.2
  79.8 2.2 %join_project.2.rest_0_ = bf16[4,128,1280]{2,1,0:T(8,128)(2,1)} custom-call(f32[2,128,640]{2,1,0:T(8,128)S(1)} %get-tuple-element.36.own, f32[2,16,128]{2,1,0:T(8,128)S(1)} %get-tuple-element.37.logs, bf16[2,144,640]{2,1,0:T(8,128)(2,1)S(1)} %collective-permute-done.14.far, bf16[4,128,1280]{2,1,0:T(8,128)(2,1)S(1)} %get-tuple-element.35.hidden, ...), custom_call_target="tpu_custom_call" | custom-call | flops 419430400 | bytes 3276800 | tf_op jit(solution)/shard_map/join_project/pallas_call | solution.py:444
  82.0 1.2 %collective-permute-done.11.far = bf16[2,144,640]{2,1,0:T(8,128)(2,1)S(1)} collective-permute-done((bf16[2,144,640]{2,1,0:T(8,128)(2,1)S(1)}, bf16[2,144,640]{2,1,0:T(8,128)(2,1)S(1)}, u32[]{:S(2)}, u32[]{:S(2)}) %collective-permute-start.11) | collective-permute-done | bytes 368672 | tf_op jit(solution)/shard_map/ppermute | solution.py:27
  83.2 2.2 %join_project.3 = bf16[4,128,1280]{2,1,0:T(8,128)(2,1)} custom-call(f32[2,128,640]{2,1,0:T(8,128)S(1)} %get-tuple-element.33.own, f32[2,16,128]{2,1,0:T(8,128)S(1)} %get-tuple-element.34.logs, bf16[2,144,640]{2,1,0:T(8,128)(2,1)S(1)} %collective-permute-done.11.far, ...), custom_call_target="tpu_custom_call", output_to_operand_aliasing={{}: (5, {})} | custom-call | flops 419430400 | bytes 3276800 | tf_op jit(solution)/shard_map/join_project/pallas_call | solution.py:444
  (11 shorter events, 0.0 us)
Async XLA Ops:
  0.6 13.3 %copy-start = (bf16[1280,640]{1,0:T(8,128)(2,1)S(1)}, bf16[1280,640]{1,0:T(8,128)(2,1)}, u32[]{:S(2)}) copy-start(bf16[1280,640]{1,0:T(8,128)(2,1)} %param.17) | copy-start | bytes 4915204
  0.6 11.1 %copy-start.7 = (s32[4,8]{1,0:T(4,128)S(1)}, s32[4,8]{1,0:T(4,128)}, u32[]{:S(2)}) copy-start(s32[4,8]{1,0:T(4,128)} %param.13) | copy-start | bytes 388
  3.9 16.2 %copy-start.3 = (bf16[2,4,4,32,640]{4,3,2,1,0:T(8,128)(2,1)S(1)}, bf16[2,4,4,32,640]{4,3,2,1,0:T(8,128)(2,1)}, u32[]{:S(2)}) copy-start(bf16[2,4,4,32,640]{4,3,2,1,0:T(8,128)(2,1)} %param.12) | copy-start | bytes 3932164
  3.9 25.8 %copy-start.5 = (f32[1280]{0:T(1024)S(1)}, f32[1280]{0:T(1024)}, u32[]{:S(2)}) copy-start(f32[1280]{0:T(1024)} %param.14) | copy-start | bytes 15364
  3.9 25.8 %copy-start.6 = (f32[1280]{0:T(1024)S(1)}, f32[1280]{0:T(1024)}, u32[]{:S(2)}) copy-start(f32[1280]{0:T(1024)} %param.15) | copy-start | bytes 15364
  3.9 8.2 %collective-permute-start = (f32[2,8,128]{2,1,0:T(8,128)}, f32[2,8,128]{2,1,0:T(8,128)S(1)}, u32[]{:S(2)}, u32[]{:S(2)}) collective-permute-start(f32[2,8,128]{2,1,0:T(8,128)} %get-tuple-element.20), channel_id=1, source_target_pairs={{0,16},{1,17},{2,18},{3,19},{4,20},{5,21},{6,22},{7,23},{8,24},{9,... | collective-permute-start | bytes 24584 | tf_op jit(solution)/shard_map/ppermute | solution.py:27
  6.0 16.4 %collective-permute-start.2 = (bf16[4,32,1280]{2,1,0:T(8,128)(2,1)}, bf16[4,32,1280]{2,1,0:T(8,128)(2,1)S(1)}, u32[]{:S(2)}, u32[]{:S(2)}) collective-permute-start(bf16[4,32,1280]{2,1,0:T(8,128)(2,1)} %get-tuple-element.22), channel_id=1, source_target_pairs={{0,8},{1,9},{2,10},{3,11},{4,12},{5,13},{6,14},{7,15},{8,0},{9,1},... | collective-permute-start | bytes 983048 | tf_op jit(solution)/shard_map/ppermute | solution.py:27
  9.2 9.5 %collective-permute-start.3 = (bf16[4,32,1280]{2,1,0:T(8,128)(2,1)}, bf16[4,32,1280]{2,1,0:T(8,128)(2,1)}, u32[]{:S(2)}, u32[]{:S(2)}) collective-permute-start(bf16[4,32,1280]{2,1,0:T(8,128)(2,1)} %get-tuple-element.23), channel_id=1, source_target_pairs={{0,48},{1,49},{2,50},{3,51},{4,52},{5,53},{6,54},{7,55},{8,24},{9,... | collective-permute-start | bytes 983048 | tf_op jit(solution)/shard_map/ppermute | solution.py:34
  12.8 7.2 %collective-permute-start.1 = (f32[2,8,128]{2,1,0:T(8,128)S(1)}, f32[2,8,128]{2,1,0:T(8,128)S(1)}, u32[]{:S(2)}, u32[]{:S(2)}) collective-permute-start(f32[2,8,128]{2,1,0:T(8,128)S(1)} %pad_maximum_fusion.2), channel_id=1, source_target_pairs={{0,32},{1,33},{2,34},{3,35},{4,36},{5,37},{6,38},{7,39},{8,40},{9,... | collective-permute-start | bytes 24584 | tf_op jit(solution)/shard_map/ppermute | solution.py:27
  18.7 9.4 %collective-permute-start.4 = (bf16[4,32,1280]{2,1,0:T(8,128)(2,1)}, bf16[4,32,1280]{2,1,0:T(8,128)(2,1)S(1)}, u32[]{:S(2)}, u32[]{:S(2)}) collective-permute-start(bf16[4,32,1280]{2,1,0:T(8,128)(2,1)} %collective-permute-done.3), channel_id=1, source_target_pairs={{0,8},{1,9},{2,10},{3,11},{4,12},{5,13},{6,14},{7,15},{8,0},{9,1},... | collective-permute-start | bytes 983048 | tf_op jit(solution)/shard_map/ppermute | solution.py:27
  20.1 34.8 %collective-permute-start.7 = (bf16[2,4,128,640]{3,2,1,0:T(8,128)(2,1)S(1)}, bf16[2,4,128,640]{3,2,1,0:T(8,128)(2,1)S(1)}, u32[]{:S(2)}, u32[]{:S(2)}) collective-permute-start(bf16[2,4,128,640]{3,2,1,0:T(8,128)(2,1)S(1)} %bitcast.18), channel_id=1, source_target_pairs={{0,48},{1,49},{2,50},{3,51},{4,52},{5,53},{6,54},{7,55},{8,56},{9,... | collective-permute-start | bytes 3932168 | tf_op jit(solution)/shard_map/ppermute | solution.py:22
  22.4 32.5 %collective-permute-start.6 = (bf16[2,4,128,640]{3,2,1,0:T(8,128)(2,1)S(1)}, bf16[2,4,128,640]{3,2,1,0:T(8,128)(2,1)S(1)}, u32[]{:S(2)}, u32[]{:S(2)}) collective-permute-start(bf16[2,4,128,640]{3,2,1,0:T(8,128)(2,1)S(1)} %bitcast.19), channel_id=1, source_target_pairs={{0,16},{1,17},{2,18},{3,19},{4,20},{5,21},{6,22},{7,23},{8,24},{9,... | collective-permute-start | bytes 3932168 | tf_op jit(solution)/shard_map/ppermute | solution.py:22
  28.1 5.2 %collective-permute-start.5 = (f32[2,8,128]{2,1,0:T(8,128)S(1)}, f32[2,8,128]{2,1,0:T(8,128)S(1)}, u32[]{:S(2)}, u32[]{:S(2)}) collective-permute-start(f32[2,8,128]{2,1,0:T(8,128)S(1)} %pad_maximum_fusion.3), channel_id=1, source_target_pairs={{0,8},{1,9},{2,10},{3,11},{4,12},{5,13},{6,14},{7,15},{8,0},{9,1},... | collective-permute-start | bytes 24584 | tf_op jit(solution)/shard_map/ppermute | solution.py:27
  33.3 18.1 %slice-start = ((s8[4915200]{0:T(1024)(128)(4,1)}), s8[4194304]{0:T(1024)(128)(4,1)S(1)}, s32[]{:S(2)}) async-start(s8[4915200]{0:T(1024)(128)(4,1)} %bitcast.22), calls=%async_computation | async-start | bytes 8388608
  33.3 1.5 %copy-start.4 = (bf16[4,4,32,1280]{3,2,1,0:T(8,128)(2,1)S(1)}, bf16[4,4,32,1280]{3,2,1,0:T(8,128)(2,1)}, u32[]{:S(2)}) copy-start(bf16[4,4,32,1280]{3,2,1,0:T(8,128)(2,1)} %param.10) | copy-start | bytes 3932164
  34.7 16.6 %slice-start.1 = ((s8[4915200]{0:T(1024)(128)(4,1)}), s8[720896]{0:T(1024)(128)(4,1)S(1)}, s32[]{:S(2)}) async-start(s8[4915200]{0:T(1024)(128)(4,1)} %bitcast.22), calls=%async_computation.1 | async-start | bytes 1441792
  49.7 14.3 %collective-permute-start.10 = (bf16[4,128,640]{2,1,0:T(8,128)(2,1)S(1)}, bf16[4,128,640]{2,1,0:T(8,128)(2,1)S(1)}, u32[]{:S(2)}, u32[]{:S(2)}) collective-permute-start(bf16[4,128,640]{2,1,0:T(8,128)(2,1)S(1)} %get-tuple-element.27.queries), channel_id=1, source_target_pairs={{0,8},{1,9},{2,10},{3,11},{4,12},{5,13},{6,14},{7,15},{8,0},{9,1},... | collective-permute-start | bytes 1966088 | tf_op jit(solution)/shard_map/ppermute | solution.py:27
  55.0 10.8 %collective-permute-start.12 = (bf16[2,128,640]{2,1,0:T(8,128)(2,1)S(1)}, bf16[2,128,640]{2,1,0:T(8,128)(2,1)S(1)}, u32[]{:S(2)}, u32[]{:S(2)}) collective-permute-start(bf16[2,128,640]{2,1,0:T(8,128)(2,1)S(1)} %get-tuple-element.40), channel_id=1, source_target_pairs={{0,16},{1,17},{2,18},{3,19},{4,20},{5,21},{6,22},{7,23},{8,24},{9,... | collective-permute-start | bytes 983048 | tf_op jit(solution)/shard_map/ppermute | solution.py:22
  56.1 9.6 %collective-permute-start.13 = (bf16[2,128,640]{2,1,0:T(8,128)(2,1)S(1)}, bf16[2,128,640]{2,1,0:T(8,128)(2,1)S(1)}, u32[]{:S(2)}, u32[]{:S(2)}) collective-permute-start(bf16[2,128,640]{2,1,0:T(8,128)(2,1)S(1)} %get-tuple-element.38), channel_id=1, source_target_pairs={{0,48},{1,49},{2,50},{3,51},{4,52},{5,53},{6,54},{7,55},{8,56},{9,... | collective-permute-start | bytes 983048 | tf_op jit(solution)/shard_map/ppermute | solution.py:22
  58.6 12.5 %collective-permute-start.8 = (bf16[2,128,640]{2,1,0:T(8,128)(2,1)S(1)}, bf16[2,128,640]{2,1,0:T(8,128)(2,1)S(1)}, u32[]{:S(2)}, u32[]{:S(2)}) collective-permute-start(bf16[2,128,640]{2,1,0:T(8,128)(2,1)S(1)} %get-tuple-element.41), channel_id=1, source_target_pairs={{0,16},{1,17},{2,18},{3,19},{4,20},{5,21},{6,22},{7,23},{8,24},{9,... | collective-permute-start | bytes 983048 | tf_op jit(solution)/shard_map/ppermute | solution.py:22
  58.6 12.5 %collective-permute-start.9 = (bf16[2,128,640]{2,1,0:T(8,128)(2,1)S(1)}, bf16[2,128,640]{2,1,0:T(8,128)(2,1)S(1)}, u32[]{:S(2)}, u32[]{:S(2)}) collective-permute-start(bf16[2,128,640]{2,1,0:T(8,128)(2,1)S(1)} %get-tuple-element.39), channel_id=1, source_target_pairs={{0,48},{1,49},{2,50},{3,51},{4,52},{5,53},{6,54},{7,55},{8,56},{9,... | collective-permute-start | bytes 983048 | tf_op jit(solution)/shard_map/ppermute | solution.py:22
  68.3 6.3 %copy-start.1 = (bf16[2,4,128,640]{3,2,1,0:T(8,128)(2,1)S(1)}, bf16[2,4,128,640]{3,2,1,0:T(8,128)(2,1)}, u32[]{:S(2)}) copy-start(bf16[2,4,128,640]{3,2,1,0:T(8,128)(2,1)} %keys_values.1.first) | copy-start | bytes 3932164
  68.3 11.4 %collective-permute-start.14 = (bf16[2,144,640]{2,1,0:T(8,128)(2,1)S(1)}, bf16[2,144,640]{2,1,0:T(8,128)(2,1)S(1)}, u32[]{:S(2)}, u32[]{:S(2)}) collective-permute-start(bf16[2,144,640]{2,1,0:T(8,128)(2,1)S(1)} %attend.7), channel_id=1, source_target_pairs={{0,8},{1,9},{2,10},{3,11},{4,12},{5,13},{6,14},{7,15},{8,0},{9,1},... | collective-permute-start | bytes 1105928 | tf_op jit(solution)/shard_map/ppermute | solution.py:27
  73.7 9.5 %collective-permute-start.11 = (bf16[2,144,640]{2,1,0:T(8,128)(2,1)S(1)}, bf16[2,144,640]{2,1,0:T(8,128)(2,1)S(1)}, u32[]{:S(2)}, u32[]{:S(2)}) collective-permute-start(bf16[2,144,640]{2,1,0:T(8,128)(2,1)S(1)} %attend.5), channel_id=1, source_target_pairs={{0,8},{1,9},{2,10},{3,11},{4,12},{5,13},{6,14},{7,15},{8,0},{9,1},... | collective-permute-start | bytes 1105928 | tf_op jit(solution)/shard_map/ppermute | solution.py:27
  77.2 2.6 %copy-start.2 = (bf16[640,1280]{1,0:T(8,128)(2,1)S(1)}, bf16[640,1280]{1,0:T(8,128)(2,1)}, u32[]{:S(2)}) copy-start(bf16[640,1280]{1,0:T(8,128)(2,1)} %weight.5) | copy-start | bytes 4915204
